TPU v7x, 32 devices: a whole 2x2x4 slice. The times are simulated.
32 devices in a mesh: dp: 8 (over y, x, core), mp: 4 (over z).
Axes of the slice: x: 2, y: 2, z: 4, core: 2. Of those that a mesh axis runs over, the one named last changes fastest.
Arguments:
- tokens: bfloat16 [16, 1024, 768], P('dp', 'mp'), may hold values from -6 to 6
- cotangent: bfloat16 [16, 1024, 768], P('dp', 'mp'), may hold values from -6 to 6
- w_query: bfloat16 [768, 768], P('dp', 'mp'), may hold values from -0.21875 to 0.21875
- w_key: bfloat16 [768, 768], P('dp', 'mp'), may hold values from -0.21875 to 0.21875
- w_value: bfloat16 [768, 768], P('dp', 'mp'), may hold values from -0.21875 to 0.21875
- w_out: bfloat16 [768, 768], P('mp', 'dp'), may hold values from -1.75 to 1.75
- w_inner: bfloat16 [768, 3072], P('dp', 'mp'), may hold values from -0.21875 to 0.21875
- w_outer: bfloat16 [3072, 768], P('mp', 'dp'), may hold values from -0.109375 to 0.109375
- gain_attn: bfloat16 [768], P('dp'), may hold values from 0.099609375 to 1.8984375
- shift_attn: bfloat16 [768], P('dp'), may hold values from -3 to 3
- gain_ffn: bfloat16 [768], P('dp'), may hold values from 0.099609375 to 1.8984375
- shift_ffn: bfloat16 [768], P('dp'), may hold values from -3 to 3
- seq_lengths: int32 [16], P('dp'), may hold values from 256 to 1024, as said below
- rand_blocks: int32 [12, 16, 3], P('mp'), may hold values from 1 to 14, as said below
Outputs:
- output: bfloat16 [16, 1024, 768], P('dp', 'mp')
- grad_tokens: bfloat16 [16, 1024, 768], P('dp', 'mp')
- grad_w_query: float32 [768, 768], P('dp', 'mp')
- grad_w_key: float32 [768, 768], P('dp', 'mp')
- grad_w_value: float32 [768, 768], P('dp', 'mp')
- grad_w_out: float32 [768, 768], P('mp', 'dp')
- grad_w_inner: float32 [768, 3072], P('dp', 'mp')
- grad_w_outer: float32 [3072, 768], P('mp', 'dp')
- grad_gain_attn: float32 [768], P('dp')
- grad_shift_attn: float32 [768], P('dp')
- grad_gain_ffn: float32 [768], P('dp')
- grad_shift_ffn: float32 [768], P('dp')
Inputs may be any that keep to these rules, and one draw needn't show every extreme that they name: `seq_lengths`: valid positions of each sequence; the first sequence has 1024 and the second 1024 // 4. `rand_blocks`: for each head and block row r: three different block numbers, none equal to 0 or 15 and none within one of r.
All inputs are finite; a program needn't handle non-finite values.
Results may differ from a plain program's by a relative error of at most 0.017.
Values may be sent and summed in bfloat16 or wider, within the bound.
A program may use at most 128 MiB of HBM per device.

v0:
```python
import math

import jax
import jax.numpy as jnp
from jax import lax
from jax.sharding import PartitionSpec as P

EPS = 1e-06
NEG = -1000000000.0


def norm_rows(values, gain, shift):
    centre = values - jnp.mean(values, -1, keepdims=True)
    spread = jnp.mean(centre * centre, -1, keepdims=True)
    return centre * lax.rsqrt(spread + EPS) * gain + shift


def gelu_slope(values):
    cumul = 0.5 * (1.0 + lax.erf(values * (1.0 / math.sqrt(2.0))))
    return cumul + values * jnp.exp(-0.5 * values * values) * (1.0 / math.sqrt(2.0 * math.pi))


def pattern(rand_blocks, seq_len):
    nblocks = rand_blocks.shape[1]
    blk_size = seq_len // nblocks
    blocks = jnp.arange(nblocks)
    rand_hits = jnp.any(rand_blocks[:, :, :, None] == blocks[None, None, None, :], axis=2)
    row_block = blocks[:, None]
    column_block = blocks[None, :]
    edge_row = (row_block == 0) | (row_block == nblocks - 1)
    edge_col = (column_block == 0) | (column_block == nblocks - 1)
    near_blocks = edge_row | edge_col | (jnp.abs(row_block - column_block) <= 1)
    allowed = rand_hits | near_blocks[None]
    return jnp.repeat(jnp.repeat(allowed, blk_size, axis=1), blk_size, axis=2)


def unpack(full_set):
    joined = jnp.concatenate(full_set[0:3], axis=1)
    norm_params = tuple((entry.astype(jnp.float32) for entry in full_set[6:10]))
    return (joined, full_set[3], full_set[4], full_set[5], norm_params)


def per_device(
    tokens,
    cotangent,
    w_query,
    w_key,
    w_value,
    w_out,
    w_inner,
    w_outer,
    gain_attn,
    shift_attn,
    gain_ffn,
    shift_ffn,
    seq_lengths,
    rand_blocks,
):
    single_float = jnp.float32
    bf16 = jnp.bfloat16
    seq_count = tokens.shape[0]
    local_rows = tokens.shape[1]
    seq_len = local_rows * lax.axis_size("mp")
    heads_here = rand_blocks.shape[0]
    columns = w_query.shape[1]
    head_size = columns // heads_here
    score_scale = 1.0 / math.sqrt(head_size)
    query_rows = min(512, seq_len)
    allowed = pattern(rand_blocks, seq_len)
    gathered = (
        lax.all_gather(w_query, "dp", axis=0, tiled=True),
        lax.all_gather(w_key, "dp", axis=0, tiled=True),
        lax.all_gather(w_value, "dp", axis=0, tiled=True),
        lax.all_gather(w_out, "dp", axis=1, tiled=True),
        lax.all_gather(w_inner, "dp", axis=0, tiled=True),
        lax.all_gather(w_outer, "dp", axis=1, tiled=True),
        lax.all_gather(gain_attn, "dp", axis=0, tiled=True),
        lax.all_gather(shift_attn, "dp", axis=0, tiled=True),
        lax.all_gather(gain_ffn, "dp", axis=0, tiled=True),
        lax.all_gather(shift_ffn, "dp", axis=0, tiled=True),
    )
    w_joined, output_complete, inner_full, outer_complete, norm_params = unpack(gathered)
    joined_rows = jnp.einsum(
        "iyu,up->iyp",
        lax.all_gather(tokens, "mp", axis=1, tiled=True),
        w_joined,
        preferred_element_type=single_float,
    ).astype(bf16)
    queries = joined_rows[:, :, :columns].reshape(seq_count, seq_len, heads_here, head_size)
    key_rows = joined_rows[:, :, columns : 2 * columns].reshape(
        seq_count, seq_len, heads_here, head_size
    )
    value_rows = joined_rows[:, :, 2 * columns :].reshape(seq_count, seq_len, heads_here, head_size)

    def masked_scores(query_block, key_block, length, offset):
        raw_scores = (
            jnp.einsum("qhe,khe->hqk", query_block, key_block, preferred_element_type=single_float)
            * score_scale
        )
        key_ok = jnp.arange(seq_len) < length
        keep_mask = allowed[:, offset : offset + query_rows, :] & key_ok[None, None, :]
        return jnp.where(keep_mask, raw_scores, NEG)

    def attend(seq_pack):
        query_seq, key_seq, value_seq, length = seq_pack
        outputs = []
        log_parts = []
        for offset in range(0, seq_len, query_rows):
            scores = masked_scores(query_seq[offset : offset + query_rows], key_seq, length, offset)
            row_peak = jnp.max(scores, -1, keepdims=True)
            log_total = row_peak + jnp.log(jnp.sum(jnp.exp(scores - row_peak), -1, keepdims=True))
            soft_b = jnp.exp(scores - log_total).astype(bf16)
            outputs.append(
                jnp.einsum("hqk,khe->qhe", soft_b, value_seq, preferred_element_type=single_float)
            )
            log_parts.append(log_total)
        context_seq = jnp.concatenate(outputs, 0).reshape(seq_len, columns).astype(bf16)
        return (context_seq, jnp.concatenate(log_parts, 1))

    context_output, log_totals = lax.map(attend, (queries, key_rows, value_rows, seq_lengths))
    attn_sum = lax.psum_scatter(
        jnp.einsum(
            "ntb,bi->nti", context_output, output_complete, preferred_element_type=single_float
        ),
        "mp",
        scatter_dimension=1,
        tiled=True,
    )
    resid_one = tokens.astype(single_float) + attn_sum
    hidden = norm_rows(resid_one, norm_params[0], norm_params[1])
    hidden_b = hidden.astype(bf16)
    inner_pre = jnp.einsum(
        "cny,yt->cnt",
        lax.all_gather(hidden_b, "mp", axis=1, tiled=True),
        inner_full,
        preferred_element_type=single_float,
    )
    active_tokens = jax.nn.gelu(inner_pre, approximate=False).astype(bf16)
    ffn_sum = lax.psum_scatter(
        jnp.einsum(
            "ahr,rk->ahk", active_tokens, outer_complete, preferred_element_type=single_float
        ),
        "mp",
        scatter_dimension=1,
        tiled=True,
    )
    resid_two = hidden + ffn_sum
    result = norm_rows(resid_two, norm_params[2], norm_params[3])
    row_ids = lax.axis_index("mp") * local_rows + jnp.arange(local_rows)
    valid_rows = (row_ids[None, :] < seq_lengths[:, None]).astype(single_float)[:, :, None]
    output = (result * valid_rows).astype(bf16)
    back_set = unpack(
        (
            lax.all_gather(w_query, "dp", axis=0, tiled=True),
            lax.all_gather(w_key, "dp", axis=0, tiled=True),
            lax.all_gather(w_value, "dp", axis=0, tiled=True),
            lax.all_gather(w_out, "dp", axis=1, tiled=True),
            lax.all_gather(w_inner, "dp", axis=0, tiled=True),
            lax.all_gather(w_outer, "dp", axis=1, tiled=True),
            lax.all_gather(gain_attn, "dp", axis=0, tiled=True),
            lax.all_gather(shift_attn, "dp", axis=0, tiled=True),
            lax.all_gather(gain_ffn, "dp", axis=0, tiled=True),
            lax.all_gather(shift_ffn, "dp", axis=0, tiled=True),
        )
    )
    joined_backward, output_backward, inner_backward, outer_backward, norm_bw = back_set
    grad_result = cotangent.astype(single_float) * valid_rows
    _, pull_two = jax.vjp(norm_rows, resid_two, norm_bw[2], norm_bw[3])
    d_resid_two, d_gain_two, d_shift_two = pull_two(grad_result)
    rows_per_block = lax.all_gather(d_resid_two.astype(bf16), "mp", axis=1, tiled=True)
    weight_total = jnp.einsum(
        "tka,tkc->ac", active_tokens, rows_per_block, preferred_element_type=single_float
    )
    activation_total = jnp.einsum(
        "xbp,ip->xbi", rows_per_block, outer_backward, preferred_element_type=single_float
    )
    grad_outer = weight_total
    inner_gradient = (activation_total * gelu_slope(inner_pre)).astype(bf16)
    grad_part = inner_gradient
    grad_w_inner = jnp.einsum(
        "gpa,gpw->aw",
        lax.all_gather(hidden_b, "mp", axis=1, tiled=True),
        grad_part,
        preferred_element_type=single_float,
    )
    d_hidden = d_resid_two + lax.psum_scatter(
        jnp.einsum(
            "whj,cj->whc", inner_gradient, inner_backward, preferred_element_type=single_float
        ),
        "mp",
        scatter_dimension=1,
        tiled=True,
    )
    _, pull_one = jax.vjp(norm_rows, resid_one, norm_bw[0], norm_bw[1])
    d_resid_one, d_gain_one, d_shift_one = pull_one(d_hidden)
    rows_per_block = lax.all_gather(d_resid_one.astype(bf16), "mp", axis=1, tiled=True)
    weight_total = jnp.einsum(
        "jco,jck->ok", context_output, rows_per_block, preferred_element_type=single_float
    )
    context_total = jnp.einsum(
        "awm,km->awk", rows_per_block, output_backward, preferred_element_type=single_float
    )
    grad_context_b = context_total.astype(bf16).reshape(seq_count, seq_len, heads_here, head_size)

    def attend_back(seq_pack):
        query_seq, key_seq, value_seq, grad_seq, log_seq, length = seq_pack
        grad_key = jnp.zeros(key_seq.shape, single_float)
        grad_value = jnp.zeros(value_seq.shape, single_float)
        query_parts = []
        for offset in range(0, seq_len, query_rows):
            query_block = query_seq[offset : offset + query_rows]
            scores = masked_scores(query_block, key_seq, length, offset)
            soft = jnp.exp(scores - log_seq[:, offset : offset + query_rows])
            grad_block = grad_seq[offset : offset + query_rows]
            grad_value = grad_value + jnp.einsum(
                "hqk,qhe->khe", soft.astype(bf16), grad_block, preferred_element_type=single_float
            )
            grad_soft = jnp.einsum(
                "qhe,khe->hqk", grad_block, value_seq, preferred_element_type=single_float
            )
            inner_sum = jnp.sum(soft * grad_soft, -1, keepdims=True)
            grad_score = (soft * (grad_soft - inner_sum)).astype(bf16)
            query_parts.append(
                jnp.einsum("hqk,khe->qhe", grad_score, key_seq, preferred_element_type=single_float)
                * score_scale
            )
            grad_key = (
                grad_key
                + jnp.einsum(
                    "hqk,qhe->khe", grad_score, query_block, preferred_element_type=single_float
                )
                * score_scale
            )
        grad_query = jnp.concatenate(query_parts, 0)
        return jnp.concatenate(
            [
                grad_query.reshape(seq_len, columns),
                grad_key.reshape(seq_len, columns),
                grad_value.reshape(seq_len, columns),
            ],
            1,
        ).astype(bf16)

    joined_gradient = lax.map(
        attend_back, (queries, key_rows, value_rows, grad_context_b, log_totals, seq_lengths)
    )
    grad_part = joined_gradient
    grad_w_joined = jnp.einsum(
        "fuw,fum->wm",
        lax.all_gather(tokens, "mp", axis=1, tiled=True),
        grad_part,
        preferred_element_type=single_float,
    )
    grad_tokens = d_resid_one + lax.psum_scatter(
        jnp.einsum(
            "nyq,gq->nyg", joined_gradient, joined_backward, preferred_element_type=single_float
        ).astype(jnp.bfloat16),
        "mp",
        scatter_dimension=1,
        tiled=True,
    ).astype(jnp.float32)
    norm_grads = lax.psum(jnp.stack([d_gain_one, d_shift_one, d_gain_two, d_shift_two]), "mp")
    shards = (
        lax.psum_scatter(grad_w_joined[:, :columns], "dp", scatter_dimension=0, tiled=True),
        lax.psum_scatter(
            grad_w_joined[:, columns : 2 * columns], "dp", scatter_dimension=0, tiled=True
        ),
        lax.psum_scatter(grad_w_joined[:, 2 * columns :], "dp", scatter_dimension=0, tiled=True),
        lax.psum_scatter(weight_total, "dp", scatter_dimension=1, tiled=True),
        lax.psum_scatter(grad_w_inner, "dp", scatter_dimension=0, tiled=True),
        lax.psum_scatter(grad_outer, "dp", scatter_dimension=1, tiled=True),
        lax.psum_scatter(norm_grads, "dp", scatter_dimension=1, tiled=True),
    )
    return (
        output,
        grad_tokens.astype(bf16),
        shards[0],
        shards[1],
        shards[2],
        shards[3],
        shards[4],
        shards[5],
        shards[6][0],
        shards[6][1],
        shards[6][2],
        shards[6][3],
    )


def solution(mesh):
    placed = (
        P("dp", "mp", None),
        P("dp", "mp", None),
        P("dp", "mp"),
        P("dp", "mp"),
        P("dp", "mp"),
        P("mp", "dp"),
        P("dp", "mp"),
        P("mp", "dp"),
        P("dp"),
        P("dp"),
        P("dp"),
        P("dp"),
        P("dp"),
        P("mp", None, None),
    )
    return jax.shard_map(
        per_device,
        mesh=mesh,
        in_specs=placed,
        out_specs=(
            P("dp", "mp", None),
            P("dp", "mp", None),
            P("dp", "mp"),
            P("dp", "mp"),
            P("dp", "mp"),
            P("mp", "dp"),
            P("dp", "mp"),
            P("mp", "dp"),
            P("dp"),
            P("dp"),
            P("dp"),
            P("dp"),
        ),
        check_vma=False,
    )
```

profile of v0, /device:TPU:0, one launch (start us, length us, event | category | flops | bytes accessed | tf_op | source)
XLA Modules:
  0.0 1059.6 jit_solution(16481088245905995327)
XLA Ops:
  11.1 11.3 %all_gather.52 = bf16[768,192]{1,0:T(8,128)(2,1)S(1)} all-gather(bf16[96,192]{1,0:T(8,128)(2,1)} %param.20), channel_id=1, replica_groups=mesh['dp'=8,'mp'=4] {'dp'}, dimensions={0}, use_global_device_ids=true | all-gather | bytes 331776 | tf_op jit(solution)/shard_map/all_gather | solution.py:71
  22.5 9.3 all_gather.53
  32.0 8.9 all_gather.54
  47.4 9.5 all_gather.56
  56.9 19.7 %all-gather.7.cloned.1.call-done = bf16[2,1024,768]{2,1,0:T(8,128)(2,1)} async-done(((bf16[2,256,768]{2,1,0:T(8,128)(2,1)}), bf16[2,1024,768]{2,1,0:T(8,128)(2,1)}) %all-gather.7.cloned.1.call-update) | async-done | bytes 3145744 | tf_op jit(solution)/shard_map/all_gather | solution.py:85
  81.2 26.3 %while.22 = (s32[]{:T(128)}, bf16[2,1024,192]{1,2,0:T(8,128)(2,1)S(1)}, f32[2,3,1024,1]{2,1,3,0:T(4,128)}, bf16[2,1024,3,64]{1,3,2,0:T(8,128)(2,1)S(1)}, pred[3,...) while((s32[]{:T(128)}, ...), condition=%wide.region_6.7_spmd, body=%wide.region_1.6_spmd.sunk | while | flops 831456256 | bytes 57734900 | solution.py:120
  114.4 14.6 %all-reduce.4 = (bf16[768]{0:T(1024)(128)(2,1)S(1)}, bf16[768]{0:T(1024)(128)(2,1)S(1)}, bf16[768]{0:T(1024)(128)(2,1)}, bf16[768]{0:T(1024)(128)(2,1)}) all-reduce(bf16[768]{0:T(1024)(128)(2,1)S(1)} %dynamic-update-slice.1, bf16[768]{0:T(1024)(128)(2,1)S(1)} %dynamic-update-slice, ...), channel_id=1, replica_groups=mesh['dp'=8,'mp'=4] {'dp'}, use_global_device_ids=true, to_apply=%add.1 | all-reduce | flops 3072 | bytes 12288
  129.0 91.9 %reduce-scatter.22.cloned.1.call-done = f32[2,256,768]{2,1,0:T(8,128)} async-done(((f32[2,1024,768]{2,1,0:T(8,128)}), f32[2,256,768]{2,1,0:T(8,128)}) %reduce-scatter.22.cloned.1.call-update) | async-done | bytes 1572880 | tf_op jit(solution)/shard_map/reduce_scatter | solution.py:121
  225.6 63.3 %all-gather.9.cloned.1.call-done = bf16[2,1024,768]{2,1,0:T(8,128)(2,1)} async-done(((bf16[2,256,768]{2,1,0:T(8,128)(2,1)}), bf16[2,1024,768]{2,1,0:T(8,128)(2,1)}) %all-gather.9.cloned.1.call-update) | async-done | bytes 3145744 | tf_op jit(solution)/shard_map/all_gather | solution.py:134
  298.2 15.2 %fusion.64 = bf16[2,1024,768]{2,1,0:T(8,128)(2,1)} fusion(f32[2,1024,768]{2,1,0:T(8,128)S(1)} %get-tuple-element.282, u8[1024,768]{1,0:T(8,128)(4,1)S(1)} %get-tuple-element.205, u8[1024,768]{1,0:T(8,128)(4,1)S(1)} %get-tuple-element.204), kind=kLoop, calls=%fused_computation.95 | loop fusion | flops 110100480 | bytes 11010048 | tf_op jit(solution)/shard_map/convert_element_type | solution.py:138
  313.4 7.5 fusion.84
  323.4 108.1 %reduce-scatter.24.cloned.1.call-done = f32[2,256,768]{2,1,0:T(8,128)} async-done(((f32[2,1024,768]{2,1,0:T(8,128)}), f32[2,256,768]{2,1,0:T(8,128)}) %reduce-scatter.24.cloned.1.call-update) | async-done | bytes 1572880 | tf_op jit(solution)/shard_map/reduce_scatter | solution.py:139
  437.8 64.1 %all-gather.15.cloned.1.call-done = bf16[2,1024,768]{2,1,0:T(8,128)(2,1)} async-done(((bf16[2,256,768]{2,1,0:T(8,128)(2,1)}), bf16[2,1024,768]{2,1,0:T(8,128)(2,1)}) %all-gather.15.cloned.1.call-update) | async-done | bytes 3145744 | tf_op jit(solution)/shard_map/all_gather | solution.py:170
  516.1 108.1 %reduce-scatter.26.cloned.1.call-done = f32[2,256,768]{2,1,0:T(8,128)} async-done(((f32[2,1024,768]{2,1,0:T(8,128)}), f32[2,256,768]{2,1,0:T(8,128)}) %reduce-scatter.26.cloned.1.call-update) | async-done | bytes 1572880 | tf_op jit(solution)/shard_map/reduce_scatter | solution.py:186
  632.8 62.9 %all-gather.17.cloned.1.call-done = bf16[2,1024,768]{2,1,0:T(8,128)(2,1)} async-done(((bf16[2,256,768]{2,1,0:T(8,128)(2,1)}), bf16[2,1024,768]{2,1,0:T(8,128)(2,1)}) %all-gather.17.cloned.1.call-update) | async-done | bytes 3145744 | tf_op jit(solution)/shard_map/all_gather | solution.py:196
  703.0 74.9 %while.23 = (s32[]{:T(128)}, bf16[2,1024,576]{1,2,0:T(8,128)(2,1)}, bf16[2,1024,3,64]{1,3,2,0:T(8,128)(2,1)S(1)}, pred[3,1024,1024]{2,1,0:T(32,128)(4,1)}, s32[2...) while((s32[]{:T(128)}, bf16[2,1024,576]{1,2,0:T(8,128)(2,1)}, ...), condition=%wide.region_21.22_spmd, body=%wide.region_18.21_spmd.sunk | while | flops 2050422784 | bytes 193954256 | solution.py:244
  791.4 7.0 convolution_bitcast_fusion
  807.2 10.0 psum.8
  819.4 24.1 %reduce-scatter.28.cloned.1.call-done = bf16[2,256,768]{2,1,0:T(8,128)(2,1)} async-done(((bf16[2,1024,768]{2,1,0:T(8,128)(2,1)}), bf16[2,256,768]{2,1,0:T(8,128)(2,1)}) %reduce-scatter.28.cloned.1.call-update) | async-done | bytes 786448 | tf_op jit(solution)/shard_map/reduce_scatter | solution.py:254
  845.7 43.8 %reduce-scatter.30.cloned.1.call-done = f32[96,768]{1,0:T(8,128)} async-done(((f32[768,768]{1,0:T(8,128)}), f32[96,768]{1,0:T(8,128)}) %reduce-scatter.30.cloned.1.call-update) | async-done | bytes 294928 | tf_op jit(solution)/shard_map/reduce_scatter | solution.py:270
  889.5 46.7 %reduce-scatter.32.cloned.1.call-done = f32[768,96]{0,1:T(8,128)} async-done(((f32[768,768]{0,1:T(8,128)}), f32[768,96]{0,1:T(8,128)}) %reduce-scatter.32.cloned.1.call-update) | async-done | bytes 294928 | tf_op jit(solution)/shard_map/reduce_scatter | solution.py:271
  936.2 38.6 %reduce-scatter.38.cloned.1.call-done = f32[96,192]{1,0:T(8,128)} async-done(((f32[768,192]{1,0:T(8,128)}), f32[96,192]{1,0:T(8,128)}) %reduce-scatter.38.cloned.1.call-update) | async-done | bytes 73744
  974.7 38.7 %reduce-scatter.36.cloned.1.call-done = f32[96,192]{1,0:T(8,128)} async-done(((f32[768,192]{1,0:T(8,128)}), f32[96,192]{1,0:T(8,128)}) %reduce-scatter.36.cloned.1.call-update) | async-done | bytes 73744
  1013.5 38.6 %reduce-scatter.34.cloned.1.call-done = f32[96,192]{1,0:T(8,128)} async-done(((f32[768,192]{1,0:T(8,128)}), f32[96,192]{1,0:T(8,128)}) %reduce-scatter.34.cloned.1.call-update) | async-done | bytes 73744
  (297 shorter events, 200.0 us)
Async XLA Ops:
  8.0 68.6 %all-gather.7.cloned.1.call-start = ((), (), s32[]{:S(2)}) async-start(), calls=%async_computation.11 | async-start | bytes 3932160 | tf_op jit(solution)/shard_map/all_gather | solution.py:85
  8.8 212.2 %reduce-scatter.22.cloned.1.call-start = ((), (), s32[]{:S(2)}) async-start(), calls=%async_computation.12 | async-start | bytes 7864320 | tf_op jit(solution)/shard_map/reduce_scatter | solution.py:121
  22.5 54.1 %copy-start.17 = (bf16[768,192]{0,1:T(8,128)(2,1)}, bf16[768,192]{0,1:T(8,128)(2,1)S(1)}, u32[]{:S(2)}) copy-start(bf16[768,192]{0,1:T(8,128)(2,1)S(1)} %copy.60) | copy-start | bytes 884740
  32.0 44.6 %copy-start.18 = (bf16[768,192]{0,1:T(8,128)(2,1)}, bf16[768,192]{0,1:T(8,128)(2,1)S(1)}, u32[]{:S(2)}) copy-start(bf16[768,192]{0,1:T(8,128)(2,1)S(1)} %copy.61) | copy-start | bytes 884740
  41.0 35.6 %copy-start.19 = (bf16[768,192]{0,1:T(8,128)(2,1)}, bf16[768,192]{0,1:T(8,128)(2,1)S(1)}, u32[]{:S(2)}) copy-start(bf16[768,192]{0,1:T(8,128)(2,1)S(1)} %copy.62) | copy-start | bytes 884740
  111.3 114.2 %all-gather.11.cloned.1.call-start = ((), (), s32[]{:S(2)}) async-start(), calls=%async_computation.14 | async-start | bytes 1327104 | tf_op jit(solution)/shard_map/all_gather | solution.py:75
  111.9 176.9 %all-gather.9.cloned.1.call-start = ((), (), s32[]{:S(2)}) async-start(), calls=%async_computation.13 | async-start | bytes 3932160 | tf_op jit(solution)/shard_map/all_gather | solution.py:134
  129.0 95.9 %copy-start.25 = (f32[768]{0:T(1024)}, f32[768]{0:T(1024)S(1)}, u32[]{:S(2)}) copy-start(f32[768]{0:T(1024)S(1)} %convert_element_type.104) | copy-start | bytes 9220
  224.9 88.5 %all-gather.13.cloned.1.call-start = ((), (), s32[]{:S(2)}) async-start(), calls=%async_computation.15 | async-start | bytes 1327104 | tf_op jit(solution)/shard_map/all_gather | solution.py:76
  225.5 206.0 %reduce-scatter.24.cloned.1.call-start = ((), (), s32[]{:S(2)}) async-start(), calls=%async_computation.16 | async-start | bytes 7864320 | tf_op jit(solution)/shard_map/reduce_scatter | solution.py:139
  320.9 181.0 %all-gather.15.cloned.1.call-start = ((), (), s32[]{:S(2)}) async-start(), calls=%async_computation.17 | async-start | bytes 3932160 | tf_op jit(solution)/shard_map/all_gather | solution.py:170
  437.8 186.5 %reduce-scatter.26.cloned.1.call-start = ((), (), s32[]{:S(2)}) async-start(), calls=%async_computation.18 | async-start | bytes 7864320 | tf_op jit(solution)/shard_map/reduce_scatter | solution.py:186
  514.8 180.9 %all-gather.17.cloned.1.call-start = ((), (), s32[]{:S(2)}) async-start(), calls=%async_computation.19 | async-start | bytes 3932160 | tf_op jit(solution)/shard_map/all_gather | solution.py:196
  629.4 66.3 %copy-start.16 = (bf16[2,1024,192]{1,2,0:T(8,128)(2,1)S(1)}, bf16[2,1024,192]{1,2,0:T(8,128)(2,1)}, u32[]{:S(2)}) copy-start(bf16[2,1024,192]{1,2,0:T(8,128)(2,1)} %copy-done.15) | copy-start | bytes 2359300
  631.6 174.7 %reduce-scatter.42.cloned.1.call-start = ((), (), s32[]{:S(2)}) async-start(), calls=%async_computation.27 | async-start | bytes 442368
  632.8 185.0 %reduce-scatter.40.cloned.1.call-start = ((), (), s32[]{:S(2)}) async-start(), calls=%async_computation.26 | async-start | bytes 884736
  699.9 143.6 %reduce-scatter.28.cloned.1.call-start = ((), (), s32[]{:S(2)}) async-start(), calls=%async_computation.20 | async-start | bytes 3932160 | tf_op jit(solution)/shard_map/reduce_scatter | solution.py:254
  784.1 105.4 %reduce-scatter.30.cloned.1.call-start = ((), (), s32[]{:S(2)}) async-start(), calls=%async_computation.21 | async-start | bytes 2654208 | tf_op jit(solution)/shard_map/reduce_scatter | solution.py:270
  791.4 144.8 %reduce-scatter.32.cloned.1.call-start = ((), (), s32[]{:S(2)}) async-start(), calls=%async_computation.22 | async-start | bytes 2654208 | tf_op jit(solution)/shard_map/reduce_scatter | solution.py:271
  798.5 176.2 %reduce-scatter.38.cloned.1.call-start = ((), (), s32[]{:S(2)}) async-start(), calls=%async_computation.25 | async-start | bytes 884736
  802.6 40.9 %copy-start.7 = (f32[2,256,768]{2,1,0:T(8,128)S(1)}, f32[2,256,768]{2,1,0:T(8,128)}, u32[]{:S(2)}) copy-start(f32[2,256,768]{2,1,0:T(8,128)} %copy-done.6) | copy-start | bytes 4718596
  802.6 40.9 %copy-start.32 = (f32[2,256]{1,0:T(2,128)S(1)}, f32[2,256]{1,0:T(2,128)}, u32[]{:S(2)}) copy-start(f32[2,256]{1,0:T(2,128)} %copy-done.31) | copy-start | bytes 6148
  803.8 209.7 %reduce-scatter.36.cloned.1.call-start = ((), (), s32[]{:S(2)}) async-start(), calls=%async_computation.24 | async-start | bytes 884736
  805.1 246.9 %reduce-scatter.34.cloned.1.call-start = ((), (), s32[]{:S(2)}) async-start(), calls=%async_computation.23 | async-start | bytes 884736
  (55 other events, 153.4 us)
Sparse Core Ops, SparseCore 0:
  10.4 66.1 all-gather.6
  111.5 109.4 reduce-scatter.21
  437.9 63.9 all-gather.14
  631.7 63.9 all-gather.16
Sparse Core Ops, SparseCore 1:
  113.7 22.7 all-gather.10
  225.0 63.8 all-gather.8
  290.6 22.5 all-gather.12
  321.0 110.4 reduce-scatter.23
  514.9 109.3 reduce-scatter.25
  635.4 34.4 reduce-scatter.41
  700.0 33.6 reduce-scatter.39
  784.2 59.2 reduce-scatter.27
  847.3 42.2 reduce-scatter.29
  893.8 42.3 reduce-scatter.31
  939.8 34.9 reduce-scatter.37
  978.5 34.9 reduce-scatter.35
  1017.0 34.9 reduce-scatter.33
where the time goes:
time: 1070 us; the launch traced here: 1060 us
  waiting for transfers between devices  751 us (70%)
  matrix products  127 us (12%)
  blocking collectives  63.5 us (6%)
  other arithmetic  60.4 us (6%)
  local copies, waits for them, and re-layouts  39.1 us (4%)
  between operations  17.1 us (2%)
    unnamed x22, waiting for transfers between devices  118 us
    reduce_scatter x1, waiting for transfers between devices, per_device(): lax.psum_scatter(jnp.einsum('whj,cj->whc', inner_gradient, inner_backward...  108 us
    reduce_scatter x1, waiting for transfers between devices, per_device(): lax.psum_scatter(jnp.einsum('ahr,rk->ahk', active_tokens, outer_complete,...  108 us
    reduce_scatter x1, waiting for transfers between devices, per_device(): lax.psum_scatter(jnp.einsum('ntb,bi->nti', context_output, output_complet...  91.9 us
    all_gather x1, waiting for transfers between devices, per_device(): lax.all_gather(d_resid_two.astype(bf16), 'mp', axis=1, tiled=True)  64.1 us
    all_gather x1, waiting for transfers between devices, per_device(): lax.all_gather(hidden_b, 'mp', axis=1, tiled=True)  63.3 us
    all_gather x1, waiting for transfers between devices, per_device(): lax.all_gather(d_resid_one.astype(bf16), 'mp', axis=1, tiled=True)  62.9 us
    reduce_scatter x1, waiting for transfers between devices, per_device(): lax.psum_scatter(grad_outer, 'dp', scatter_dimension=1, tiled=True)  46.7 us
  transfers between devices with their start and end apart: 17, of which 13 were waited for; matrix products, arithmetic and copies ran while one was open for 14% of the time, Pallas kernels for 0%

commit v1 on v0

v1 whole, which is shorter than its diff:
```python
import math

import jax
import jax.numpy as jnp
from jax import lax
from jax.experimental import pallas as pl
from jax.experimental.pallas import tpu as pltpu
from jax.sharding import PartitionSpec as P

EPS = 1e-06
NEG = -1000000000.0
MESH = pl.DeviceIdType.MESH
F32 = jnp.float32
BF16 = jnp.bfloat16
ANY = pl.BlockSpec(memory_space=pl.ANY)
VMEM = pl.BlockSpec(memory_space=pltpu.VMEM)
DMA = pltpu.SemaphoreType.DMA


class Place:
    def __init__(self):
        self.d = lax.axis_index("dp")
        self.m = lax.axis_index("mp")
        self.c = lax.rem(self.d, 2)
        self.base = self.d - self.c
        self.sib = self.d + 1 - 2 * self.c
        bx = lax.rem(lax.div(self.d, 2), 2)
        by = lax.rem(lax.div(self.d, 4), 2)
        self.xp = self.d + 2 - 4 * bx
        self.yp = self.d + 4 - 8 * by
        self.bx = self.xp - self.c
        self.by = self.yp - self.c
        self.bd = self.bx + 4 - 8 * by
        self.h = lax.div(self.m, 2)
        self.a = lax.rem(self.m, 2)


def remote(src, dst, ssem, rsem, dev):
    return pltpu.make_async_remote_copy(
        src_ref=src, dst_ref=dst, send_sem=ssem, recv_sem=rsem, device_id=dev, device_id_type=MESH
    )


def push(src, dst, ssem, rsem, dev, same):
    @pl.when(same)
    def _():
        pltpu.make_async_copy(src, dst, rsem).start()

    @pl.when(jnp.logical_not(same))
    def _():
        remote(src, dst, ssem, rsem, dev).start()


def pushed(src, dst, ssem, rsem, dev, same):
    @pl.when(jnp.logical_not(same))
    def _():
        remote(src, dst, ssem, rsem, dev).wait_send()


def got(dst, ssem, rsem, dev):
    remote(dst, dst, ssem, rsem, dev).wait_recv()


def greet(peers):
    barrier = pltpu.get_barrier_semaphore()
    for dev in peers:
        pl.semaphore_signal(barrier, inc=1, device_id=dev, device_id_type=MESH)
    pl.semaphore_wait(barrier, len(peers))


def column_peers(p, mp):
    peers = []
    for k in range(1, mp):
        z = lax.rem(p.m + k, mp)
        peers += [(p.base, z), (p.base + 1, z)]
    return peers


class Gather:
    def __init__(self, p, src, dst, sems, mp):
        self.p, self.src, self.dst, self.mp = p, src, dst, mp
        self.zs, self.zr, self.xs, self.xr, self.ys, self.yr = sems
        self.n = src.shape[0]

    def rows(self, a, first, count):
        return self.dst.at[a, pl.ds(first * self.n, count * self.n), :]

    def z_args(self, k):
        p = self.p
        z = lax.rem(p.m + k, self.mp)
        same = (p.h == p.c) if k == 0 else None
        return (self.src, self.rows(p.a, p.d, 1), self.zs.at[k], self.zr.at[2 * p.c + p.a], (p.base + p.h, z)), same

    def z_send(self):
        for k in (2, 1, 3, 0):
            args, same = self.z_args(k)
            if same is None:
                remote(*args).start()
            else:
                push(*args, same)

    def z_recv(self):
        p = self.p
        for core in range(2):
            for a in range(2):
                got(self.rows(a, p.base + core, 1), self.zs.at[0], self.zr.at[2 * core + a], (p.d, p.m))

    def hop(self, axis, step, a):
        p = self.p
        peer = p.xp if axis == 0 else p.yp
        first = p.base if step == 0 else (p.by if axis == 0 else p.bx)
        part = self.rows(a, first, 2)
        s, r = (self.xs, self.xr) if axis == 0 else (self.ys, self.yr)
        i = 2 if step else a
        return remote(part, part, s.at[i], r.at[i], (peer, p.m))

    def xy_send(self):
        for a in range(2):
            self.hop(0, 0, a).start()
            self.hop(1, 0, 1 - a).start()

    def arrived(self, axis, step, a):
        p = self.p
        first = (p.bx if axis == 0 else p.by) if step == 0 else p.bd
        s, r = (self.xs, self.xr) if axis == 0 else (self.ys, self.yr)
        i = 2 if step else a
        got(self.rows(a, first, 2), s.at[i], r.at[i], (p.d, p.m))

    def forward(self):
        self.arrived(0, 0, 0)
        self.hop(1, 1, 0).start()
        self.arrived(1, 0, 1)
        self.hop(0, 1, 1).start()

    def finish(self):
        self.arrived(0, 0, 1)
        self.arrived(1, 0, 0)
        self.arrived(1, 1, 0)
        self.arrived(0, 1, 1)
        for k in range(self.mp):
            args, same = self.z_args(k)
            if same is None:
                remote(*args).wait_send()
            else:
                pushed(*args, same)
        for a in range(2):
            self.hop(0, 0, a).wait_send()
            self.hop(1, 0, a).wait_send()
        self.hop(1, 1, 0).wait_send()
        self.hop(0, 1, 1).wait_send()


def gather_sems(mp):
    return [DMA((mp,)), DMA((4,)), DMA((3,)), DMA((3,)), DMA((3,)), DMA((3,))]


class Tokens:
    def __init__(self, p, tok, x, sems):
        self.p, self.tok, self.x = p, tok, x
        self.s, self.r, self.fs, self.fr = sems
        self.piece = tok.shape[1] // 2

    def args(self, i, half):
        p, n = self.p, self.piece
        z = 2 * p.c + i
        dev = (p.base + half, z)
        dst = self.x.at[pl.ds((2 * p.m + half) * n, n), :]
        src = self.tok.at[i, pl.ds(half * n, n), :]
        return (src, dst, self.s.at[2 * i + half], self.r.at[p.m], dev), jnp.logical_and(p.c == half, p.m == z)

    def send(self):
        for i in range(2):
            for half in range(2):
                args, same = self.args(i, half)
                push(*args, same)

    def part(self, q, core):
        return self.x.at[pl.ds((2 * q + core) * self.piece, self.piece), :]

    def forward(self, mp):
        p = self.p
        for q in range(mp):
            got(self.part(q, p.c), self.s.at[0], self.r.at[q], (p.d, p.m))
            remote(self.part(q, p.c), self.part(q, p.c), self.fs.at[q], self.fr.at[q], (p.sib, p.m)).start()

    def finish(self, mp):
        p = self.p
        for q in range(mp):
            got(self.part(q, 1 - p.c), self.fs.at[q], self.fr.at[q], (p.d, p.m))
            remote(self.part(q, p.c), self.part(q, p.c), self.fs.at[q], self.fr.at[q], (p.sib, p.m)).wait_send()
        for i in range(2):
            for half in range(2):
                args, same = self.args(i, half)
                pushed(*args, same)


class Quarters:
    def __init__(self, p, src, dst, sems):
        self.p, self.src, self.dst = p, src, dst
        self.s, self.r = sems
        self.n = src.shape[1]

    def args(self, i):
        p = self.p
        z = 2 * p.c + i
        dst = self.dst.at[pl.ds(p.a * self.n, self.n), :]
        same = jnp.logical_and(p.h == p.c, p.m == z)
        return (self.src.at[i], dst, self.s.at[i], self.r.at[p.a], (p.base + p.h, z)), same

    def send(self):
        for i in range(2):
            args, same = self.args(i)
            push(*args, same)

    def finish(self):
        p = self.p
        for a in range(2):
            got(self.dst.at[pl.ds(a * self.n, self.n), :], self.s.at[a], self.r.at[a], (p.d, p.m))
        for i in range(2):
            args, same = self.args(i)
            pushed(*args, same)


class Homewards:
    def __init__(self, p, src, dst, sems):
        self.p, self.src, self.dst = p, src, dst
        self.s, self.r = sems
        self.n = dst.shape[1]

    def args(self, q):
        p = self.p
        src = self.src.at[pl.ds(q * self.n, self.n), :]
        owner = p.base + p.h
        same = jnp.logical_and(owner == p.d, p.m == 2 * p.c + q)
        return (src, self.dst.at[p.a], self.s.at[q], self.r.at[p.a], (owner, 2 * p.c + q)), same

    def send(self):
        for q in range(2):
            args, same = self.args(q)
            push(*args, same)

    def finish(self):
        p = self.p
        for i in range(2):
            got(self.dst.at[i], self.s.at[i], self.r.at[i], (p.d, p.m))
        for q in range(2):
            args, same = self.args(q)
            pushed(*args, same)


class Scatter:
    def __init__(self, p, src, out, bufs, sems, mp):
        self.p, self.src, self.out, self.mp = p, src, out, mp
        self.r1, self.r2, self.r3, self.total = bufs
        self.xs, self.xr, self.ys, self.yr, self.zs, self.zr = sems
        self.n = out.shape[1]

    def rows(self, a, first):
        return self.src.at[a, pl.ds(first * self.n, 2 * self.n), :]

    def hop(self, kind, axis):
        p = self.p
        peer = p.xp if axis == 0 else p.yp
        s, r = (self.xs, self.xr) if axis == 0 else (self.ys, self.yr)
        if kind == 0:
            a = 1 if axis == 0 else 0
            src, dst = self.rows(a, p.bd), self.r1.at[axis]
        elif kind == 1:
            a = 1 if axis == 0 else 0
            src, dst = self.rows(a, p.bx if axis == 0 else p.by), self.r2.at[axis]
        else:
            src, dst = self.r1.at[1 - axis], self.r3.at[axis]
        return remote(src, dst, s.at[kind], r.at[kind], (peer, p.m))

    def first(self):
        for axis in range(2):
            self.hop(0, axis).start()
        for axis in range(2):
            self.hop(1, axis).start()

    def second(self):
        p = self.p
        for axis in range(2):
            other = 1 - axis
            self.hop(0, axis).wait_recv()
            a = 1 if axis == 0 else 0
            rows = pl.ds((p.by if axis == 0 else p.bx) * self.n, 2 * self.n)
            self.r1[axis] = (self.src[a, rows, :].astype(F32) + self.r1[axis].astype(F32)).astype(BF16)
            self.hop(2, other).start()

    def third(self):
        p = self.p
        rows = pl.ds(p.base * self.n, 2 * self.n)
        for axis in range(2):
            self.hop(1, axis).wait_recv()
            self.hop(2, axis).wait_recv()
        for a in range(2):
            self.total[a] = (
                self.src[a, rows, :].astype(F32)
                + self.r2[1 - a].astype(F32)
                + self.r3[a].astype(F32)
            ).astype(BF16)
        for a in range(2):
            for core in range(2):
                args, same = self.z_args(a, core)
                push(*args, same)

    def z_args(self, a, core):
        p = self.p
        i = 2 * a + core
        owner = (p.base + core, 2 * p.c + a)
        same = jnp.logical_and(p.c == core, p.m == 2 * p.c + a)
        src = self.total.at[a, pl.ds(core * self.n, self.n), :]
        return (src, self.out.at[p.m], self.zs.at[i], self.zr.at[p.m], owner), same

    def finish(self):
        p = self.p
        for z in range(self.mp):
            got(self.out.at[z], self.zs.at[0], self.zr.at[z], (p.d, p.m))
        for axis in range(2):
            for kind in range(3):
                self.hop(kind, axis).wait_send()
        for a in range(2):
            for core in range(2):
                args, same = self.z_args(a, core)
                pushed(*args, same)


def scatter_bufs(n, width):
    return [pltpu.VMEM((2, 2 * n, width), BF16)] * 4


def scatter_sems(mp):
    return [DMA((3,)), DMA((3,)), DMA((3,)), DMA((3,)), DMA((4,)), DMA((mp,))]


def fetch_kernel(mp, tok, cot, pa, pb, pc, vec, x, ct, ga, gb, gc, gvd, gvz, *sems):
    p = Place()
    vs, vr, us, ur = sems[:4]
    tokens = Tokens(p, tok, x, sems[4:8])
    cots = Quarters(p, cot, ct, sems[8:10])
    weights = [Gather(p, s, g, sems[10 + 6 * i : 16 + 6 * i], mp) for i, (s, g) in enumerate(((pa, ga), (pb, gb), (pc, gc)))]
    plane = [lax.rem(p.d + k, 8) for k in range(1, 8)]
    greet(column_peers(p, mp) + [(d, p.m) for d in plane])
    weights[0].z_send()
    tokens.send()
    vcopies = [remote(vec, gvd.at[p.d], vs.at[k], vr.at[p.d], (d, p.m)) for k, d in enumerate(plane)]
    ucopies = [remote(vec, gvz.at[p.m], us.at[k - 1], ur.at[p.m], (p.d, lax.rem(p.m + k, mp))) for k in range(1, mp)]
    own = [pltpu.make_async_copy(vec, gvd.at[p.d], vr.at[p.d]), pltpu.make_async_copy(vec, gvz.at[p.m], ur.at[p.m])]
    for copy in vcopies + ucopies + own:
        copy.start()
    weights[0].z_recv()
    weights[0].xy_send()
    weights[1].z_send()
    tokens.forward(mp)
    weights[0].forward()
    weights[1].z_recv()
    weights[1].xy_send()
    weights[2].z_send()
    cots.send()
    weights[1].forward()
    weights[2].z_recv()
    weights[2].xy_send()
    weights[2].forward()
    tokens.finish(mp)
    cots.finish()
    for w in weights:
        w.finish()
    for d in range(8):
        got(gvd.at[d], vs.at[0], vr.at[d], (p.d, p.m))
    for z in range(mp):
        got(gvz.at[z], us.at[0], ur.at[z], (p.d, p.m))
    for copy in vcopies + ucopies:
        copy.wait_send()


def fetch(mp, tok, cot, pa, pb, pc, vec):
    rows, width = pa.shape
    seq = tok.shape[1] * mp
    shape = jax.ShapeDtypeStruct
    gathered = shape((2, 8 * rows, width), BF16)
    return pl.pallas_call(
        lambda *refs: fetch_kernel(mp, *refs),
        name="fetch",
        out_shape=[
            shape((seq, tok.shape[2]), BF16),
            shape((seq // 2, tok.shape[2]), BF16),
            gathered,
            gathered,
            gathered,
            shape((8,) + vec.shape, F32),
            shape((mp,) + vec.shape, F32),
        ],
        in_specs=[ANY] * 6,
        out_specs=[ANY] * 7,
        scratch_shapes=[
            DMA((7,)), DMA((8,)), DMA((mp - 1,)), DMA((mp,)),
            DMA((4,)), DMA((mp,)), DMA((mp,)), DMA((mp,)),
            DMA((2,)), DMA((2,)),
            *gather_sems(mp), *gather_sems(mp), *gather_sems(mp),
        ],
        compiler_params=pltpu.CompilerParams(collective_id=0, has_side_effects=True),
    )(tok, cot, pa, pb, pc, vec)


def deliver_kernel(mp, da, db, dc, out, gtok, ra, rb, rc, hout, hgtok, *scr):
    p = Place()
    weights = []
    for i, (s, o) in enumerate(((da, ra), (db, rb), (dc, rc))):
        weights.append(Scatter(p, s, o, scr[4 * i : 4 * i + 4], scr[12 + 6 * i : 18 + 6 * i], mp))
    home = Homewards(p, out, hout, scr[30:32])
    home_g = Homewards(p, gtok, hgtok, scr[32:34])
    greet(column_peers(p, mp) + [(p.sib, p.m), (p.xp, p.m), (p.yp, p.m)])
    home.send()
    home_g.send()
    for w in weights:
        w.first()
    for w in weights:
        w.second()
        w.third()
    for w in weights:
        w.finish()
    home.finish()
    home_g.finish()


def deliver(mp, da, db, dc, out, gtok, rows, quarter):
    width = da.shape[2]
    shape = jax.ShapeDtypeStruct
    part = shape((mp, rows, width), BF16)
    piece = shape((2, quarter, out.shape[1]), BF16)
    return pl.pallas_call(
        lambda *refs: deliver_kernel(mp, *refs),
        name="deliver",
        out_shape=[part, part, part, piece, piece],
        in_specs=[VMEM] * 3 + [ANY] * 2,
        out_specs=[ANY] * 5,
        scratch_shapes=[
            *scatter_bufs(rows, width), *scatter_bufs(rows, width), *scatter_bufs(rows, width),
            *scatter_sems(mp), *scatter_sems(mp), *scatter_sems(mp),
            DMA((2,)), DMA((2,)), DMA((2,)), DMA((2,)),
        ],
        compiler_params=pltpu.CompilerParams(collective_id=1, has_side_effects=True, vmem_limit_bytes=48 << 20),
    )(da, db, dc, out, gtok)


def attend_kernel(q_ref, k_ref, v_ref, bias_ref, hot_ref, ctx_ref, lse_ref, qa, ka):
    seq = q_ref.shape[2]
    head = q_ref.shape[1]
    scale = 1.0 / math.sqrt(head)
    blocks = bias_ref.shape[2]
    step = min(256, seq)
    qa[0:head, :] = (q_ref[0].astype(F32) * scale).astype(BF16)
    qa[head : head + blocks, :] = bias_ref[0, 0]
    low = lax.broadcasted_iota(jnp.int32, (qa.shape[0] - head - blocks, seq), 0)
    qa[head + blocks :, :] = jnp.where(low == 0, NEG, 0.0).astype(BF16)
    ka[0:head, :] = k_ref[0]
    ka[head:, :] = hot_ref[...]
    for i in range(seq // step):
        cols = slice(i * step, (i + 1) * step)
        scores = lax.dot_general(ka[...], qa[:, cols], (((0,), (0,)), ((), ())), preferred_element_type=F32)
        peak = jnp.max(scores, 0, keepdims=True)
        weights = jnp.exp(scores - peak)
        total = jnp.sum(weights, 0, keepdims=True)
        mixed = jnp.dot(v_ref[0], weights.astype(BF16), preferred_element_type=F32)
        ctx_ref[0, :, cols] = (mixed / total).astype(BF16)
        lse_ref[0, 0, :, cols] = peak + jnp.log(total)


def head_specs(head, seq, per, blocks, hot_rows):
    row = lambda part: pl.BlockSpec((1, head, seq), lambda m, h: (m, part * per + h, 0))
    return (
        [row(0), row(1), row(2)],
        pl.BlockSpec((1, 1, blocks, seq), lambda m, h: (m, h, 0, 0)),
        pl.BlockSpec((hot_rows, seq), lambda m, h: (0, 0)),
        pl.BlockSpec((1, 1, 1, seq), lambda m, h: (m, h, 0, 0)),
        row(0),
    )


def attend(qkv, bias, hot, head):
    groups, width, seq = qkv.shape
    per = width // (3 * head)
    rows, bias_spec, hot_spec, line, out = head_specs(head, seq, per, bias.shape[2], hot.shape[0])
    deep = head + hot.shape[0]
    return pl.pallas_call(
        attend_kernel,
        name="attend",
        grid=(groups, per),
        out_shape=[
            jax.ShapeDtypeStruct((groups, per * head, seq), BF16),
            jax.ShapeDtypeStruct((groups, per, 1, seq), F32),
        ],
        in_specs=rows + [bias_spec, hot_spec],
        out_specs=[out, line],
        scratch_shapes=[pltpu.VMEM((deep, seq), BF16), pltpu.VMEM((deep, seq), BF16)],
        compiler_params=pltpu.CompilerParams(vmem_limit_bytes=48 << 20),
    )(qkv, qkv, qkv, bias, hot)


def attend_back_kernel(q_ref, k_ref, v_ref, bias_ref, hot_ref, lse_ref, g_ref, dq_ref, dk_ref, dv_ref, qa, ka, ak, av):
    seq = q_ref.shape[2]
    head = q_ref.shape[1]
    scale = 1.0 / math.sqrt(head)
    blocks = bias_ref.shape[2]
    step = min(256, seq)
    qa[0:head, :] = (q_ref[0].astype(F32) * scale).astype(BF16)
    qa[head : head + blocks, :] = bias_ref[0, 0]
    low = lax.broadcasted_iota(jnp.int32, (qa.shape[0] - head - blocks, seq), 0)
    qa[head + blocks :, :] = jnp.where(low == 0, NEG, 0.0).astype(BF16)
    ka[0:head, :] = k_ref[0]
    ka[head:, :] = hot_ref[...]
    for i in range(seq // step):
        cols = slice(i * step, (i + 1) * step)
        scores = lax.dot_general(ka[...], qa[:, cols], (((0,), (0,)), ((), ())), preferred_element_type=F32)
        probs = jnp.exp(scores - lse_ref[0, 0, :, cols])
        grad = g_ref[0, :, cols]
        grad_probs = lax.dot_general(v_ref[0], grad, (((0,), (0,)), ((), ())), preferred_element_type=F32)
        inner = jnp.sum(probs * grad_probs, 0, keepdims=True)
        grad_scores = (probs * (grad_probs - inner)).astype(BF16)
        dq_ref[0, :, cols] = (jnp.dot(k_ref[0], grad_scores, preferred_element_type=F32) * scale).astype(BF16)
        gk = lax.dot_general(qa[0:head, cols], grad_scores, (((1,), (1,)), ((), ())), preferred_element_type=F32)
        gv = lax.dot_general(grad, probs.astype(BF16), (((1,), (1,)), ((), ())), preferred_element_type=F32)
        if i == 0:
            ak[...] = gk
            av[...] = gv
        else:
            ak[...] += gk
            av[...] += gv
    dk_ref[0] = ak[...].astype(BF16)
    dv_ref[0] = av[...].astype(BF16)


def attend_back(qkv, bias, hot, lse, grad, head):
    groups, width, seq = qkv.shape
    per = width // (3 * head)
    rows, bias_spec, hot_spec, line, out = head_specs(head, seq, per, bias.shape[2], hot.shape[0])
    deep = head + hot.shape[0]
    return pl.pallas_call(
        attend_back_kernel,
        name="attend_back",
        grid=(groups, per),
        out_shape=[jax.ShapeDtypeStruct((groups, per * head, seq), BF16)] * 3,
        in_specs=rows + [bias_spec, hot_spec, line, out],
        out_specs=[out] * 3,
        scratch_shapes=[
            pltpu.VMEM((deep, seq), BF16),
            pltpu.VMEM((deep, seq), BF16),
            pltpu.VMEM((head, seq), F32),
            pltpu.VMEM((head, seq), F32),
        ],
        compiler_params=pltpu.CompilerParams(vmem_limit_bytes=48 << 20),
    )(qkv, qkv, qkv, bias, hot, lse, grad)


def fetch_plain(dp, mp, tok, cot, pa, pb, pc, vec):
    d, m = lax.axis_index("dp"), lax.axis_index("mp")
    core = d % 2
    swap = [(i, i ^ 1) for i in range(dp)]

    def sequence(rows):
        whole = lax.all_gather(rows, "mp", axis=1, tiled=True)
        other = lax.ppermute(whole, "dp", swap)
        return jnp.where(m // 2 == core, whole, other)[m % 2]

    def weight(part):
        plane = lax.all_gather(part, "dp", axis=0, tiled=True)
        return lax.dynamic_slice_in_dim(lax.all_gather(plane, "mp"), 2 * core, 2, 0)

    half = tok.shape[1] * mp // 2
    ct = lax.dynamic_slice_in_dim(sequence(cot), core * half, half, 0)
    return (
        sequence(tok), ct, weight(pa), weight(pb), weight(pc), lax.all_gather(vec, "dp"), lax.all_gather(vec, "mp"),
    )


def deliver_plain(dp, mp, da, db, dc, out, gtok, rows, quarter):
    d, m = lax.axis_index("dp"), lax.axis_index("mp")
    core = d % 2
    swap = [(i, i ^ 1) for i in range(dp)]

    def grad(part):
        wide = jnp.zeros((mp,) + part.shape[1:], F32)
        wide = lax.dynamic_update_slice_in_dim(wide, part.astype(F32), 2 * core, 0)
        mine = lax.psum_scatter(wide, "mp", scatter_dimension=0, tiled=True)[0]
        return lax.psum_scatter(mine, "dp", scatter_dimension=0, tiled=True)[None]

    def home(half):
        both = jnp.zeros((2,) + half.shape, half.dtype)
        both = lax.dynamic_update_slice_in_dim(both, half[None], core, 0)
        both = lax.dynamic_update_slice_in_dim(both, lax.ppermute(half, "dp", swap)[None], 1 - core, 0)
        all_rows = lax.all_gather(both.reshape(mp, quarter, -1), "mp")
        mine = lax.dynamic_slice_in_dim(all_rows, 2 * core, 2, 0)
        return lax.dynamic_slice_in_dim(mine, m, 1, 1)[:, 0]

    return grad(da), grad(db), grad(dc), home(out), home(gtok)


def layer(
    dp, mp, tokens, cotangent, w_query, w_key, w_value, w_out, w_inner, w_outer,
    gain_attn, shift_attn, gain_ffn, shift_ffn, seq_lengths, rand_blocks,
):
    d, m = lax.axis_index("dp"), lax.axis_index("mp")
    core = d % 2
    swap = [(i, i ^ 1) for i in range(dp)]
    quarter, width = tokens.shape[1:]
    seq = quarter * mp
    half = seq // 2
    per, nblocks, picks = rand_blocks.shape
    cols = w_query.shape[1]
    head = cols // per
    block = seq // nblocks
    rows = w_query.shape[0]
    vec_rows = [v.astype(F32) for v in (gain_attn, shift_attn, gain_ffn, shift_ffn)]
    vec_rows += [seq_lengths.astype(F32)]
    flat = rand_blocks.astype(F32).reshape(-1)
    vec_rows += [flat[:128], flat[128:]]
    vec = jnp.stack([jnp.pad(v, (0, 128 - v.shape[0])) for v in vec_rows] + [jnp.zeros(128, F32)])
    pa = jnp.concatenate([w_query, w_key, w_value, w_out.T], 1)
    kernels = dp == 8 and mp == 4 and rows % 16 == 0 and pa.shape[1] % 128 == 0
    sizes = (mp,) if kernels else (dp, mp)
    x, ct, ga, gb, gc, gvd, gvz = (fetch if kernels else fetch_plain)(
        *sizes, tokens, cotangent, pa, w_inner, w_outer.T, vec
    )
    norms = jnp.swapaxes(gvd[:, :4, :rows], 0, 1).reshape(4, width)
    g1, b1, g2, b2 = (norms[i][None] for i in range(4))
    owner = d - core + m // 2
    lens = lax.dynamic_slice_in_dim(gvd[:, 4, :2], owner, 1, 0)[0]
    length = jnp.where(m % 2 == 0, lens[0], lens[1]).astype(jnp.int32)
    picked = lax.dynamic_slice_in_dim(gvz, 2 * core, 2, 0)
    picked = picked[:, 5:7].reshape(2, 256)[:, : per * nblocks * picks].astype(jnp.int32)
    picked = picked.reshape(2, per, nblocks, picks)

    r = jnp.arange(nblocks)
    near = (r[:, None] == 0) | (r[:, None] == nblocks - 1) | (r[None] == 0) | (r[None] == nblocks - 1)
    near = near | (jnp.abs(r[:, None] - r[None]) <= 1)
    hits = jnp.any(picked[:, :, :, :, None] == r, axis=3) | near
    bias = jnp.where(jnp.swapaxes(hits, 2, 3), 0.0, NEG).astype(BF16)
    bias = jnp.repeat(bias, block, axis=3)
    pos = jnp.arange(seq)
    hot = jnp.concatenate([pos[None] // block == r[:, None], pos[None] >= length, jnp.zeros((15, seq), bool)], 0)
    hot = hot.astype(BF16)

    def mine(values):
        return lax.dynamic_slice_in_dim(values, core * half, half, 0)

    def theirs(values):
        return lax.dynamic_slice_in_dim(values, (1 - core) * half, half, 0)

    def pair_sum(partial):
        return mine(partial) + lax.ppermute(theirs(partial).astype(BF16), "dp", swap).astype(F32)

    def pair_join(values):
        other = lax.ppermute(values, "dp", swap)
        lo = jnp.where(core == 0, values, other)
        hi = jnp.where(core == 0, other, values)
        return jnp.concatenate([lo, hi], 0)

    def dot(spec, a, b):
        return jnp.einsum(spec, a, b, preferred_element_type=F32)

    a_qkv, a_out = ga[:, :, : 3 * cols], ga[:, :, 3 * cols :]
    qkv = dot("mrc,tr->mct", a_qkv, x).astype(BF16)
    ctx, lse = attend(qkv, bias, hot, head)
    attn = pair_sum(dot("mct,mdc->td", ctx, a_out))
    x_mine = mine(x).astype(F32)

    def norm(z):
        centre = z - jnp.mean(z, -1, keepdims=True)
        inv = lax.rsqrt(jnp.mean(centre * centre, -1, keepdims=True) + EPS)
        return centre * inv, inv

    n1, inv1 = norm(x_mine + attn)
    hidden = n1 * g1 + b1
    hidden_b = pair_join(hidden.astype(BF16))
    inner = dot("td,mdk->tmk", hidden_b, gb)
    cumul = 0.5 * (1.0 + lax.erf(inner * (1.0 / math.sqrt(2.0))))
    active = (inner * cumul).astype(BF16)
    slope = cumul + inner * jnp.exp(-0.5 * inner * inner) * (1.0 / math.sqrt(2.0 * math.pi))
    n2, inv2 = norm(hidden + pair_sum(dot("tmk,mdk->td", active, gc)))
    valid = (core * half + jnp.arange(half) < length).astype(F32)[:, None]
    out = ((n2 * g2 + b2) * valid).astype(BF16)

    def norm_back(e, n, inv):
        return (e - jnp.mean(e, -1, keepdims=True) - n * jnp.mean(e * n, -1, keepdims=True)) * inv

    gy = ct.astype(F32) * valid
    g_mid = norm_back(gy * g2, n2, inv2)
    d_gain2, d_shift2 = jnp.sum(gy * n2, 0), jnp.sum(gy, 0)
    g_ffn = pair_join(g_mid.astype(BF16))
    d_c = dot("td,tmk->mdk", g_ffn, active).astype(BF16)
    g_inner = (dot("td,mdk->tmk", g_ffn, gc) * slope).astype(BF16)
    d_b = dot("td,tmk->mdk", hidden_b, g_inner).astype(BF16)
    g_hidden = g_mid + pair_sum(dot("tmk,mdk->td", g_inner, gb))
    d_gain1, d_shift1 = jnp.sum(g_hidden * n1, 0), jnp.sum(g_hidden, 0)
    g_res = norm_back(g_hidden * g1, n1, inv1)
    g_attn = pair_join(g_res.astype(BF16))
    d_out = dot("td,mct->mdc", g_attn, ctx).astype(BF16)
    g_ctx = dot("td,mdc->mct", g_attn, a_out).astype(BF16)
    dq, dk, dv = attend_back(qkv, bias, hot, lse, g_ctx, head)
    dqkv = jnp.concatenate([dq, dk, dv], 1)
    d_qkv = dot("tr,mct->mrc", x, dqkv).astype(BF16)
    d_a = jnp.concatenate([d_qkv, d_out], 2)
    gtok = (g_res + pair_sum(dot("mct,mrc->tr", dqkv, a_qkv))).astype(BF16)
    ra, rb, rc, out, gtok = (deliver if kernels else deliver_plain)(*sizes, d_a, d_b, d_c, out, gtok, rows, quarter)
    ra, rb, rc = (jnp.sum(v.astype(F32), 0) for v in (ra, rb, rc))
    sums = lax.psum(jnp.stack([d_gain1, d_shift1, d_gain2, d_shift2]), ("dp", "mp"))
    sums = lax.dynamic_slice_in_dim(sums, d * rows, rows, 1)
    return (
        out, gtok, ra[:, :cols], ra[:, cols : 2 * cols], ra[:, 2 * cols : 3 * cols], ra[:, 3 * cols :].T, rb, rc.T,
        sums[0], sums[1], sums[2], sums[3],
    )


def solution(mesh):
    dp, mp = mesh.shape["dp"], mesh.shape["mp"]
    act, vec = P("dp", "mp", None), P("dp")
    w_in, w_back = P("dp", "mp"), P("mp", "dp")

    def step(*args):
        return layer(dp, mp, *args)

    return jax.shard_map(
        step,
        mesh=mesh,
        in_specs=(act, act, w_in, w_in, w_in, w_back, w_in, w_back, vec, vec, vec, vec, vec, P("mp", None, None)),
        out_specs=(act, act, w_in, w_in, w_in, w_back, w_in, w_back, vec, vec, vec, vec),
        check_vma=False,
    )
```

time: 1070 us -> 390 us (0.36)
  waiting for transfers between devices: 751 us -> 7.93 us
  Pallas kernels: 0 us -> 214 us
  matrix products: 127 us -> 43.7 us
  other arithmetic: 60.4 us -> 27 us
  blocking collectives: 63.5 us -> 48.2 us
  between operations: 17.1 us -> 3.1 us
    reduce_scatter x6 -> x0, waiting for transfers between devices: 423 us -> none  [the longest x1 108 us: per_device(): lax.psum_scatter(jnp.einsum('whj,cj->whc', inner_gradient, inner_backward...]
    pallas_call x0 -> x4, Pallas kernels: none -> 214 us  [the longest x1 89.7 us: deliver(): pl.pallas_call(lambda *refs: deliver_kernel(mp, *refs), name='deliver', o...]
    all_gather x6 -> x0, waiting for transfers between devices: 210 us -> none  [the longest x1 64.1 us: per_device(): lax.all_gather(d_resid_two.astype(bf16), 'mp', axis=1, tiled=True)]
    unnamed x22 -> x0, waiting for transfers between devices: 118 us -> none
    dot_general x40 -> x12, matrix products: 127 us -> 43.7 us  [dot(): return jnp.einsum(spec, a, b, preferred_element_type=F32)]
    all_gather x4 -> x0, blocking collectives: 38.9 us -> none  [the longest x1 11.3 us: per_device(): lax.all_gather(w_query, 'dp', axis=0, tiled=True)]
    psum x1, blocking collectives: 10 us -> 48.2 us  [layer(): lax.psum(jnp.stack([d_gain1, d_shift1, d_gain2, d_shift2]), ('dp', 'mp'))]
    convert_element_type x14 -> x10, other arithmetic: 39 us -> 6.52 us  [the longest x1 1.89 us: layer(): g_attn = pair_join(g_res.astype(BF16))]
  transfers between devices with their start and end apart: 17 -> 7, of which waited for: 13 -> 4; matrix products, arithmetic and copies ran while one was open for 14% -> 6% of each run, Pallas kernels for 0% -> 0%
where the time goes in v1:
time: 390 us; the launch traced here: 383 us
  Pallas kernels  214 us (55%)
  blocking collectives  48.2 us (12%)
  matrix products  43.7 us (11%)
  local copies, waits for them, and re-layouts  28.5 us (7%)
  other arithmetic  27 us (7%)
  starting transfers between devices  10.9 us (3%)
  waiting for transfers between devices  7.93 us (2%)
    pallas_call x1, Pallas kernels, deliver(): pl.pallas_call(lambda *refs: deliver_kernel(mp, *refs), name='deliver', o...  89.7 us
    pallas_call x1, Pallas kernels, fetch(): pl.pallas_call(lambda *refs: fetch_kernel(mp, *refs), name='fetch', out_s...  81.9 us
    psum x1, blocking collectives, layer(): lax.psum(jnp.stack([d_gain1, d_shift1, d_gain2, d_shift2]), ('dp', 'mp'))  48.2 us
    dot_general x12, matrix products, dot(): return jnp.einsum(spec, a, b, preferred_element_type=F32)  43.7 us
    pallas_call x1, Pallas kernels, attend_back(): pl.pallas_call(attend_back_kernel, name='attend_back', grid=(groups, per)...  24.5 us
    pallas_call x1, Pallas kernels, attend(): pl.pallas_call(attend_kernel, name='attend', grid=(groups, per), out_shap...  17.8 us
    unnamed x76, local copies, waits for them, and re-layouts  14.5 us
    ppermute x4, starting transfers between devices, pair_sum(): lax.ppermute(theirs(partial).astype(BF16), 'dp', swap).astype(F32)  9.99 us
  transfers between devices with their start and end apart: 7, of which 4 were waited for; matrix products, arithmetic and copies ran while one was open for 6% of the time, Pallas kernels for 0%

profile of v1, /device:TPU:0, one launch (start us, length us, event | category | flops | bytes accessed | tf_op | source)
XLA Modules:
  0.0 383.3 jit_solution(11784334559076806780)
XLA Ops:
  6.9 81.9 %fetch.1 = (bf16[1024,768]{1,0:T(8,128)(2,1)}, bf16[512,768]{1,0:T(8,128)(2,1)}, bf16[2,768,768]{2,1,0:T(8,128)(2,1)}, bf16[2,768,768]{2,1,0:T(8,128)(2,1)}, bf1...) custom-call(bf16[2,256,768]{2,1,0:T(8,128)(2,1)} %refs_0_.1, bf16[2,256,768]{2,1,0:T(8,128)(2,1)} %refs_1_.1, ...), custom_call_target="tpu_custom_call" | custom-call | tf_op jit(solution)/shard_map/fetch/pallas_call | solution.py:382
  93.4 4.4 %convolution_convert_fusion.q_ref.k_ref.v_ref = bf16[2,576,1024]{2,1,0:T(8,128)(2,1)S(1)} fusion(bf16[2,768,768]{2,1,0:T(8,128)(2,1)} %get-tuple-element.29, bf16[1024,768]{1,0:T(8,128)(2,1)} %get-tuple-element.30), kind=kOutput, calls=%fused_computation.12 | convolution fusion | flops 1813118976 | bytes 5898240 | tf_op jit(solution)/shard_map/mrc,tr->mct/dot_general | solution.py:660
  97.8 17.8 %attend.1 = (bf16[2,192,1024]{2,1,0:T(8,128)(2,1)S(1)}, f32[2,3,1,1024]{3,2,1,0:T(1,128)S(1)}) custom-call(bf16[2,576,1024]{2,1,0:T(8,128)(2,1)S(1)} %convolution_convert_fusion.q_ref.k_ref.v_ref, bf16[2,576,1024]{2,1,0:T(8,128)(2,1)S(1)} %convolution_convert_fusion.q_ref.k_ref.v_ref, bf16[2,576,1024]{2,1,0:T(8,128)(2,1)S(1)} %convolution_convert_fusion.q_ref.k_ref.v_ref, ...), custom_call_target="tpu_custom_call" | custom-call | tf_op jit(solution)/shard_map/attend/pallas_call | solution.py:486
  116.5 4.1 %convolution_bitcast_fusion.3 = f32[1024,768]{1,0:T(8,128)} fusion(bf16[2,192,1024]{2,1,0:T(8,128)(2,1)S(1)} %get-tuple-element.35, bf16[2,768,768]{2,1,0:T(8,128)(2,1)} %get-tuple-element.29), kind=kOutput, calls=%fused_computation.16 | convolution fusion | flops 603979776 | bytes 4718592 | tf_op jit(solution)/shard_map/mct,mdc->td/dot_general | solution.py:660
  120.6 2.4 dynamic-slice_convert_fusion.3
  123.0 9.2 %collective-permute-start = (bf16[512,768]{1,0:T(8,128)(2,1)}, bf16[512,768]{1,0:T(8,128)(2,1)S(1)}, u32[]{:S(2)}, u32[]{:S(2)}) collective-permute-start(bf16[512,768]{1,0:T(8,128)(2,1)} %dynamic-slice_convert_fusion.3), channel_id=1, source_target_pairs={{0,4},{4,0},{8,12},{12,8},{16,20},{20,16},{24,28},{28,24},{1,5},{5... | collective-permute-start | bytes 2359304 | tf_op jit(solution)/shard_map/ppermute | solution.py:651
  134.3 2.0 fusion.34
  138.2 2.1 collective-permute-done.1
  142.3 5.5 %multiply_convert_fusion = (bf16[1024,2,768]{2,0,1:T(8,128)(2,1)S(1)}, f32[1024,2,768]{2,0,1:T(8,128)}) fusion(bf16[2,768,768]{2,1,0:T(8,128)(2,1)S(1)} %copy-done.26, bf16[512,768]{1,0:T(8,128)(2,1)S(1)} %get-tuple-element.131, bf16[512,768]{1,0:T(8,128)(2,1)S(1)} %get-tuple-element.130), kind=kOutput, calls=%fused_computation.7 | convolution fusion | flops 2426929152 | bytes 13369344 | tf_op jit(solution)/shard_map/td,mdk->tmk/dot_general | solution.py:660
  147.8 2.6 convolution_bitcast_fusion.2
  153.5 2.0 collective-permute-done.2
  155.5 2.5 fusion.33
  164.0 4.7 %fusion.5 = bf16[1024,2,768]{2,0,1:T(8,128)(2,1)S(1)} fusion(f32[1024,2,768]{2,0,1:T(8,128)S(1)} %copy-done.30, bf16[2,768,768]{2,1,0:T(8,128)(2,1)S(1)} %copy-done.29, bf16[512,768]{1,0:T(8,128)(2,1)S(1)} %get-tuple-element.129, bf16[512,768]{1,0:T(8,128)(2,1)S(1)} %get-tuple-element.128), kind=kOutput, calls=%fused_computation.6 | convolution fusion | flops 2434793472 | bytes 13369344 | tf_op jit(solution)/shard_map/td,mdk->tmk/dot_general | solution.py:660
  168.7 2.6 convolution_bitcast_fusion.1
  174.4 6.5 %convert_bitcast_fusion.refs_2_ = bf16[2,768,768]{2,1,0:T(8,128)(2,1)} fusion(bf16[1024,2,768]{2,0,1:T(8,128)(2,1)} %copy-done.31, bf16[512,768]{1,0:T(8,128)(2,1)} %copy-done.21, bf16[512,768]{1,0:T(8,128)(2,1)} %copy-done.20), kind=kOutput, calls=%fused_computation.10 | convolution fusion | flops 2420244480 | bytes 7077888 | tf_op jit(solution)/shard_map/td,tmk->mdk/dot_general | solution.py:660
  181.0 2.6 multiply_reduce_fusion.1
  186.8 3.9 %convert_bitcast_fusion.1.refs_1_ = bf16[2,768,768]{2,1,0:T(8,128)(2,1)} fusion(bf16[1024,2,768]{2,0,1:T(8,128)(2,1)S(1)} %copy-done.33, bf16[512,768]{1,0:T(8,128)(2,1)S(1)} %copy-done.19, bf16[512,768]{1,0:T(8,128)(2,1)S(1)} %copy-done.17), kind=kOutput, calls=%fused_computation.11 | convolution fusion | flops 2420244480 | bytes 7077888 | tf_op jit(solution)/shard_map/td,tmk->mdk/dot_general | solution.py:660
  190.8 48.2 %psum.7 = f32[4,768]{1,0:T(4,128)S(1)} all-reduce(f32[4,768]{1,0:T(4,128)S(1)} %pad_maximum_fusion.2), channel_id=1, replica_groups=mesh['dp'=8,'mp'=4] {'dp','mp'}, use_global_device_ids=true, to_apply=%region_16.17 | all-reduce | flops 3072 | bytes 24576 | tf_op jit(solution)/shard_map/psum | solution.py:707
  243.0 24.5 %attend_back.1 = (bf16[2,192,1024]{2,1,0:T(8,128)(2,1)S(1)}, bf16[2,192,1024]{2,1,0:T(8,128)(2,1)S(1)}, bf16[2,192,1024]{2,1,0:T(8,128)(2,1)S(1)}) custom-call(bf16[2,576,1024]{2,1,0:T(8,128)(2,1)S(1)} %convolution_convert_fusion.q_ref.k_ref.v_ref, bf16[2,576,1024]{2,1,0:T(8,128)(2,1)S(1)} %convolution_convert_fusion.q_ref.k_ref.v_ref, ...), custom_call_target="tpu_custom_call" | custom-call | tf_op jit(solution)/shard_map/attend_back/pallas_call | solution.py:539
  267.7 2.3 convolution_bitcast_fusion
  275.0 5.0 %convolution_convert_fusion.1 = bf16[2,576,768]{2,1,0:T(8,128)(2,1)} fusion(bf16[2,576,1024]{2,1,0:T(8,128)(2,1)} %copy-done.24, bf16[1024,768]{1,0:T(8,128)(2,1)S(1)} %copy-done.22), kind=kOutput, calls=%fused_computation.17 | convolution fusion | flops 1812824064 | bytes 5701632 | tf_op jit(solution)/shard_map/tr,mct->mrc/dot_general | solution.py:660
  280.0 2.7 copy.100
  282.8 3.1 pad_maximum_fusion.refs_0_
  287.3 89.7 %deliver.1 = (bf16[4,96,768]{2,1,0:T(8,128)(2,1)S(1)}, bf16[4,96,768]{2,1,0:T(8,128)(2,1)S(1)}, bf16[4,96,768]{2,1,0:T(8,128)(2,1)S(1)}, bf16[2,256,768]{2,1,0:T(8,128)(2,1)S(1)}, bf16[2,256,768]{2,1,0:T(8,128)(2,1)S(1)}) custom-call(bf16[2,768,768]{2,1,0:T(8,128)(2,1)} %pad_maximum_fusion.refs_0_, bf16[2,768,768]{2,1,0:T(8,128)(2,1)} %convert_bitcast_fusion.1.refs_1_, ...), custom_call_target="tpu_custom_call" | custom-call | tf_op jit(solution)/shard_map/deliver/pallas_call | solution.py:432
  (162 shorter events, 47.8 us)
Async XLA Ops:
  120.6 11.6 %copy-start.25 = (f32[8,8,128]{2,1,0:T(8,128)S(1)}, f32[8,8,128]{2,1,0:T(8,128)}, u32[]{:S(2)}) copy-start(f32[8,8,128]{2,1,0:T(8,128)} %get-tuple-element.32) | copy-start | bytes 98308
  123.0 11.4 %collective-permute-start = (bf16[512,768]{1,0:T(8,128)(2,1)}, bf16[512,768]{1,0:T(8,128)(2,1)S(1)}, u32[]{:S(2)}, u32[]{:S(2)}) collective-permute-start(bf16[512,768]{1,0:T(8,128)(2,1)} %dynamic-slice_convert_fusion.3), channel_id=1, source_target_pairs={{0,4},{4,0},{8,12},{12,8},{16,20},{20,16},{24,28},{28,24},{1,5},{5... | collective-permute-start | bytes 2359304 | tf_op jit(solution)/shard_map/ppermute | solution.py:651
  137.8 2.5 collective-permute-start.1
  138.2 4.1 %copy-start.26 = (bf16[2,768,768]{2,1,0:T(8,128)(2,1)S(1)}, bf16[2,768,768]{2,1,0:T(8,128)(2,1)}, u32[]{:S(2)}) copy-start(bf16[2,768,768]{2,1,0:T(8,128)(2,1)} %get-tuple-element.36) | copy-start | bytes 7077892
  142.2 5.5 %copy-start.16 = (bf16[512,768]{1,0:T(8,128)(2,1)}, bf16[512,768]{1,0:T(8,128)(2,1)S(1)}, u32[]{:S(2)}) copy-start(bf16[512,768]{1,0:T(8,128)(2,1)S(1)} %get-tuple-element.130) | copy-start | bytes 2359300
  142.3 5.5 %copy-start.18 = (bf16[512,768]{1,0:T(8,128)(2,1)}, bf16[512,768]{1,0:T(8,128)(2,1)S(1)}, u32[]{:S(2)}) copy-start(bf16[512,768]{1,0:T(8,128)(2,1)S(1)} %get-tuple-element.131) | copy-start | bytes 2359300
  142.3 5.5 %copy-start.28 = (bf16[2,768,768]{2,1,0:T(8,128)(2,1)S(1)}, bf16[2,768,768]{2,1,0:T(8,128)(2,1)}, u32[]{:S(2)}) copy-start(bf16[2,768,768]{2,1,0:T(8,128)(2,1)} %get-tuple-element.37) | copy-start | bytes 7077892
  153.0 2.5 collective-permute-start.2
  158.0 2.9 copy-start.6
  159.7 4.2 %copy-start.30 = (f32[1024,2,768]{2,0,1:T(8,128)S(1)}, f32[1024,2,768]{2,0,1:T(8,128)}, u32[]{:S(2)}) copy-start(f32[1024,2,768]{2,0,1:T(8,128)} %get-tuple-element.143) | copy-start | bytes 18874372
  161.5 2.4 collective-permute-start.3
  163.9 4.7 %copy-start.20 = (bf16[512,768]{1,0:T(8,128)(2,1)}, bf16[512,768]{1,0:T(8,128)(2,1)S(1)}, u32[]{:S(2)}) copy-start(bf16[512,768]{1,0:T(8,128)(2,1)S(1)} %get-tuple-element.128) | copy-start | bytes 2359300
  163.9 4.7 %copy-start.21 = (bf16[512,768]{1,0:T(8,128)(2,1)}, bf16[512,768]{1,0:T(8,128)(2,1)S(1)}, u32[]{:S(2)}) copy-start(bf16[512,768]{1,0:T(8,128)(2,1)S(1)} %get-tuple-element.129) | copy-start | bytes 2359300
  164.0 4.7 %copy-start.27 = (bf16[2,768,768]{2,1,0:T(8,128)(2,1)S(1)}, bf16[2,768,768]{2,1,0:T(8,128)(2,1)}, u32[]{:S(2)}) copy-start(bf16[2,768,768]{2,1,0:T(8,128)(2,1)} %get-tuple-element.36) | copy-start | bytes 7077892
  174.0 6.9 %collective-permute-start.4 = (bf16[512,768]{1,0:T(8,128)(2,1)}, bf16[512,768]{1,0:T(8,128)(2,1)}, u32[]{:S(2)}, u32[]{:S(2)}) collective-permute-start(bf16[512,768]{1,0:T(8,128)(2,1)} %dynamic-slice_convert_fusion.1), channel_id=1, source_target_pairs={{0,4},{4,0},{8,12},{12,8},{16,20},{20,16},{24,28},{28,24},{1,5},{5... | collective-permute-start | bytes 2359304 | tf_op jit(solution)/shard_map/ppermute | solution.py:651
  174.4 6.6 %copy-start.5 = (f32[512,768]{1,0:T(8,128)S(1)}, f32[512,768]{1,0:T(8,128)}, u32[]{:S(2)}) copy-start(f32[512,768]{1,0:T(8,128)} %copy-done.4) | copy-start | bytes 4718596
  174.4 6.6 %copy-start.7 = (f32[512,768]{1,0:T(8,128)S(1)}, f32[512,768]{1,0:T(8,128)}, u32[]{:S(2)}) copy-start(f32[512,768]{1,0:T(8,128)} %copy-done.6) | copy-start | bytes 4718596
  174.4 6.5 %copy-start.9 = (bf16[512,768]{1,0:T(8,128)(2,1)S(1)}, bf16[512,768]{1,0:T(8,128)(2,1)}, u32[]{:S(2)}) copy-start(bf16[512,768]{1,0:T(8,128)(2,1)} %get-tuple-element.34) | copy-start | bytes 2359300
  174.4 6.5 %copy-start.14 = (f32[1024,768]{1,0:T(8,128)S(1)}, f32[1024,768]{1,0:T(8,128)}, u32[]{:S(2)}) copy-start(f32[1024,768]{1,0:T(8,128)} %copy-done.13) | copy-start | bytes 9437188
  183.6 3.2 copy-start.33
  185.5 54.0 %collective-permute-start.5 = (bf16[512,768]{1,0:T(8,128)(2,1)}, bf16[512,768]{1,0:T(8,128)(2,1)}, u32[]{:S(2)}, u32[]{:S(2)}) collective-permute-start(bf16[512,768]{1,0:T(8,128)(2,1)} %get-tuple-element.118), channel_id=1, source_target_pairs={{0,4},{4,0},{8,12},{12,8},{16,20},{20,16},{24,28},{28,24},{1,5},{5... | collective-permute-start | bytes 2359304 | tf_op jit(solution)/shard_map/ppermute | solution.py:654
  272.6 13.3 %collective-permute-start.6 = (bf16[512,768]{1,0:T(8,128)(2,1)}, bf16[512,768]{1,0:T(8,128)(2,1)}, u32[]{:S(2)}, u32[]{:S(2)}) collective-permute-start(bf16[512,768]{1,0:T(8,128)(2,1)} %dynamic-slice_convert_fusion), channel_id=1, source_target_pairs={{0,4},{4,0},{8,12},{12,8},{16,20},{20,16},{24,28},{28,24},{1,5},{5... | collective-permute-start | bytes 2359304 | tf_op jit(solution)/shard_map/ppermute | solution.py:651
  282.8 3.2 copy-start.10
  282.8 3.2 copy-start.12
  (17 other events, 31.7 us)

commit v2 on v1

--- a/solution.py
+++ b/solution.py
@@ -334,38 +334,26 @@
     return [DMA((3,)), DMA((3,)), DMA((3,)), DMA((3,)), DMA((4,)), DMA((mp,))]
 
 
-def fetch_kernel(mp, tok, cot, pa, pb, pc, vec, x, ct, ga, gb, gc, gvd, gvz, *sems):
+def fetch_kernel(mp, tok, pa, vec, x, ga, gvd, gvz, *sems):
     p = Place()
     vs, vr, us, ur = sems[:4]
     tokens = Tokens(p, tok, x, sems[4:8])
-    cots = Quarters(p, cot, ct, sems[8:10])
-    weights = [Gather(p, s, g, sems[10 + 6 * i : 16 + 6 * i], mp) for i, (s, g) in enumerate(((pa, ga), (pb, gb), (pc, gc)))]
+    weight = Gather(p, pa, ga, sems[8:14], mp)
     plane = [lax.rem(p.d + k, 8) for k in range(1, 8)]
     greet(column_peers(p, mp) + [(d, p.m) for d in plane])
-    weights[0].z_send()
+    weight.z_send()
     tokens.send()
     vcopies = [remote(vec, gvd.at[p.d], vs.at[k], vr.at[p.d], (d, p.m)) for k, d in enumerate(plane)]
     ucopies = [remote(vec, gvz.at[p.m], us.at[k - 1], ur.at[p.m], (p.d, lax.rem(p.m + k, mp))) for k in range(1, mp)]
     own = [pltpu.make_async_copy(vec, gvd.at[p.d], vr.at[p.d]), pltpu.make_async_copy(vec, gvz.at[p.m], ur.at[p.m])]
     for copy in vcopies + ucopies + own:
         copy.start()
-    weights[0].z_recv()
-    weights[0].xy_send()
-    weights[1].z_send()
+    weight.z_recv()
+    weight.xy_send()
     tokens.forward(mp)
-    weights[0].forward()
-    weights[1].z_recv()
-    weights[1].xy_send()
-    weights[2].z_send()
-    cots.send()
-    weights[1].forward()
-    weights[2].z_recv()
-    weights[2].xy_send()
-    weights[2].forward()
+    weight.forward()
     tokens.finish(mp)
-    cots.finish()
-    for w in weights:
-        w.finish()
+    weight.finish()
     for d in range(8):
         got(gvd.at[d], vs.at[0], vr.at[d], (p.d, p.m))
     for z in range(mp):
@@ -374,74 +362,100 @@
         copy.wait_send()
 
 
-def fetch(mp, tok, cot, pa, pb, pc, vec):
+def fetch(mp, tok, pa, vec):
     rows, width = pa.shape
-    seq = tok.shape[1] * mp
     shape = jax.ShapeDtypeStruct
-    gathered = shape((2, 8 * rows, width), BF16)
     return pl.pallas_call(
         lambda *refs: fetch_kernel(mp, *refs),
         name="fetch",
         out_shape=[
-            shape((seq, tok.shape[2]), BF16),
-            shape((seq // 2, tok.shape[2]), BF16),
-            gathered,
-            gathered,
-            gathered,
+            shape((tok.shape[1] * mp, tok.shape[2]), BF16),
+            shape((2, 8 * rows, width), BF16),
             shape((8,) + vec.shape, F32),
             shape((mp,) + vec.shape, F32),
         ],
-        in_specs=[ANY] * 6,
-        out_specs=[ANY] * 7,
+        in_specs=[ANY] * 3,
+        out_specs=[ANY] * 4,
         scratch_shapes=[
             DMA((7,)), DMA((8,)), DMA((mp - 1,)), DMA((mp,)),
             DMA((4,)), DMA((mp,)), DMA((mp,)), DMA((mp,)),
-            DMA((2,)), DMA((2,)),
-            *gather_sems(mp), *gather_sems(mp), *gather_sems(mp),
+            *gather_sems(mp),
         ],
         compiler_params=pltpu.CompilerParams(collective_id=0, has_side_effects=True),
-    )(tok, cot, pa, pb, pc, vec)
-
-
-def deliver_kernel(mp, da, db, dc, out, gtok, ra, rb, rc, hout, hgtok, *scr):
+    )(tok, pa, vec)
+
+
+def deliver_kernel(mp, da, gtok, ra, hgtok, *scr):
     p = Place()
-    weights = []
-    for i, (s, o) in enumerate(((da, ra), (db, rb), (dc, rc))):
-        weights.append(Scatter(p, s, o, scr[4 * i : 4 * i + 4], scr[12 + 6 * i : 18 + 6 * i], mp))
-    home = Homewards(p, out, hout, scr[30:32])
-    home_g = Homewards(p, gtok, hgtok, scr[32:34])
+    weight = Scatter(p, da, ra, scr[0:4], scr[4:10], mp)
+    home = Homewards(p, gtok, hgtok, scr[10:12])
     greet(column_peers(p, mp) + [(p.sib, p.m), (p.xp, p.m), (p.yp, p.m)])
     home.send()
-    home_g.send()
-    for w in weights:
-        w.first()
-    for w in weights:
-        w.second()
-        w.third()
-    for w in weights:
-        w.finish()
+    weight.first()
+    weight.second()
+    weight.third()
+    weight.finish()
     home.finish()
-    home_g.finish()
-
-
-def deliver(mp, da, db, dc, out, gtok, rows, quarter):
+
+
+def deliver(mp, da, gtok, rows, quarter):
     width = da.shape[2]
     shape = jax.ShapeDtypeStruct
-    part = shape((mp, rows, width), BF16)
-    piece = shape((2, quarter, out.shape[1]), BF16)
     return pl.pallas_call(
         lambda *refs: deliver_kernel(mp, *refs),
         name="deliver",
-        out_shape=[part, part, part, piece, piece],
-        in_specs=[VMEM] * 3 + [ANY] * 2,
-        out_specs=[ANY] * 5,
-        scratch_shapes=[
-            *scatter_bufs(rows, width), *scatter_bufs(rows, width), *scatter_bufs(rows, width),
-            *scatter_sems(mp), *scatter_sems(mp), *scatter_sems(mp),
-            DMA((2,)), DMA((2,)), DMA((2,)), DMA((2,)),
-        ],
+        out_shape=[shape((mp, rows, width), BF16), shape((2, quarter, gtok.shape[1]), BF16)],
+        in_specs=[VMEM, ANY],
+        out_specs=[ANY] * 2,
+        scratch_shapes=[*scatter_bufs(rows, width), *scatter_sems(mp), DMA((2,)), DMA((2,))],
         compiler_params=pltpu.CompilerParams(collective_id=1, has_side_effects=True, vmem_limit_bytes=48 << 20),
-    )(da, db, dc, out, gtok)
+    )(da, gtok)
+
+
+class Sums:
+    def __init__(self, p, src, out, bufs, sems, mp):
+        self.p, self.src, self.out, self.mp = p, src, out, mp
+        self.mine, self.came, self.parts = bufs
+        self.s, self.r, self.zs, self.zr = sems
+
+    def hop(self, i):
+        p = self.p
+        dev = (p.sib, p.xp, p.yp)[i]
+        return remote(self.mine.at[i], self.came.at[i], self.s.at[i], self.r.at[i], (dev, p.m))
+
+    def start(self):
+        self.mine[0] = self.src[...]
+        self.hop(0).start()
+
+    def step(self, i):
+        self.hop(i).wait_recv()
+        total = self.mine[i] + self.came[i]
+        if i < 2:
+            self.mine[i + 1] = total
+            self.hop(i + 1).start()
+        else:
+            self.parts[self.p.m] = total
+            for k in range(1, self.mp):
+                self.column(k).start()
+
+    def column(self, k):
+        p = self.p
+        part = self.parts.at[p.m]
+        return remote(part, part, self.zs.at[k - 1], self.zr.at[p.m], (p.d, lax.rem(p.m + k, self.mp)))
+
+    def finish(self):
+        p = self.p
+        for k in range(1, self.mp):
+            z = lax.rem(p.m + k, self.mp)
+            got(self.parts.at[z], self.zs.at[0], self.zr.at[z], (p.d, p.m))
+        total = self.parts[0]
+        for z in range(1, self.mp):
+            total = total + self.parts[z]
+        self.out[...] = total
+        for i in range(3):
+            self.hop(i).wait_send()
+        for k in range(1, self.mp):
+            self.column(k).wait_send()
 
 
 def attend_kernel(q_ref, k_ref, v_ref, bias_ref, hot_ref, ctx_ref, lse_ref, qa, ka):
@@ -476,6 +490,66 @@
         pl.BlockSpec((1, 1, 1, seq), lambda m, h: (m, h, 0, 0)),
         row(0),
     )
+
+
+def attend_fetch_kernel(mp, q, k, v, bias, hot, pb, pc, cot, ctx, lse, gb, gc, ct, qa, ka, *sems):
+    p = Place()
+    step = pl.program_id(0) * pl.num_programs(1) + pl.program_id(1)
+    last = pl.num_programs(0) * pl.num_programs(1) - 1
+    first, second = (Gather(p, s, g, sems[6 * i : 6 * i + 6], mp) for i, (s, g) in enumerate(((pb, gb), (pc, gc))))
+    cots = Quarters(p, cot, ct, sems[12:14])
+
+    @pl.when(step == 0)
+    def _():
+        greet(column_peers(p, mp) + [(p.sib, p.m), (p.xp, p.m), (p.yp, p.m)])
+        first.z_send()
+
+    @pl.when(step == last - 1)
+    def _():
+        first.z_recv()
+        first.xy_send()
+        second.z_send()
+
+    attend_kernel(q, k, v, bias, hot, ctx, lse, qa, ka)
+
+    @pl.when(step == last)
+    def _():
+        first.forward()
+        second.z_recv()
+        second.xy_send()
+        cots.send()
+        second.forward()
+        first.finish()
+        second.finish()
+        cots.finish()
+
+
+def attend_fetch(mp, qkv, bias, hot, head, pb, pc, cot):
+    groups, width, seq = qkv.shape
+    per = width // (3 * head)
+    rows, bias_spec, hot_spec, line, out = head_specs(head, seq, per, bias.shape[2], hot.shape[0])
+    deep = head + hot.shape[0]
+    shape = jax.ShapeDtypeStruct
+    gathered = shape((2, 8 * pb.shape[0], pb.shape[1]), BF16)
+    return pl.pallas_call(
+        lambda *refs: attend_fetch_kernel(mp, *refs),
+        name="attend_fetch",
+        grid=(groups, per),
+        out_shape=[
+            shape((groups, per * head, seq), BF16),
+            shape((groups, per, 1, seq), F32),
+            gathered,
+            gathered,
+            shape((seq // 2, cot.shape[2]), BF16),
+        ],
+        in_specs=rows + [bias_spec, hot_spec] + [ANY] * 3,
+        out_specs=[out, line] + [ANY] * 3,
+        scratch_shapes=[
+            pltpu.VMEM((deep, seq), BF16), pltpu.VMEM((deep, seq), BF16),
+            *gather_sems(mp), *gather_sems(mp), DMA((2,)), DMA((2,)),
+        ],
+        compiler_params=pltpu.CompilerParams(collective_id=2, has_side_effects=True, vmem_limit_bytes=48 << 20),
+    )(qkv, qkv, qkv, bias, hot, pb, pc, cot)
 
 
 def attend(qkv, bias, hot, head):
@@ -531,6 +605,83 @@
     dv_ref[0] = av[...].astype(BF16)
 
 
+def attend_deliver_kernel(
+    mp, q, k, v, bias, hot, lse, g, db, dc, out, norm, dq, dk, dv, rb, rc, hout, sums, qa, ka, ak, av, *scr
+):
+    p = Place()
+    step = pl.program_id(0) * pl.num_programs(1) + pl.program_id(1)
+    last = pl.num_programs(0) * pl.num_programs(1) - 1
+    early = Scatter(p, dc, rc, scr[0:4], scr[8:14], mp)
+    late = Scatter(p, db, rb, scr[4:8], scr[14:20], mp)
+    home = Homewards(p, out, hout, scr[20:22])
+    small = Sums(p, norm, sums, scr[22:25], scr[25:29], mp)
+
+    @pl.when(step == 0)
+    def _():
+        greet(column_peers(p, mp) + [(p.sib, p.m), (p.xp, p.m), (p.yp, p.m)])
+        small.start()
+        early.first()
+        home.send()
+
+    for i in range(3):
+
+        @pl.when(step == i + 1)
+        def _():
+            small.step(i)
+
+    @pl.when(step == last - 2)
+    def _():
+        early.second()
+        late.first()
+
+    @pl.when(step == last)
+    def _():
+        early.third()
+
+    attend_back_kernel(q, k, v, bias, hot, lse, g, dq, dk, dv, qa, ka, ak, av)
+
+    @pl.when(step == last)
+    def _():
+        late.second()
+        late.third()
+        small.finish()
+        early.finish()
+        late.finish()
+        home.finish()
+
+
+def attend_deliver(mp, qkv, bias, hot, lse, grad, head, db, dc, out_rows, norm, n, quarter):
+    groups, width, seq = qkv.shape
+    per = width // (3 * head)
+    rows, bias_spec, hot_spec, line, out = head_specs(head, seq, per, bias.shape[2], hot.shape[0])
+    deep = head + hot.shape[0]
+    shape = jax.ShapeDtypeStruct
+    part = shape((mp, n, db.shape[2]), BF16)
+    return pl.pallas_call(
+        lambda *refs: attend_deliver_kernel(mp, *refs),
+        name="attend_deliver",
+        grid=(groups, per),
+        out_shape=[
+            *[shape((groups, per * head, seq), BF16)] * 3,
+            part,
+            part,
+            shape((2, quarter, out_rows.shape[1]), BF16),
+            shape(norm.shape, F32),
+        ],
+        in_specs=rows + [bias_spec, hot_spec, line, out, VMEM, VMEM, ANY, VMEM],
+        out_specs=[out] * 3 + [ANY] * 3 + [VMEM],
+        scratch_shapes=[
+            pltpu.VMEM((deep, seq), BF16), pltpu.VMEM((deep, seq), BF16),
+            pltpu.VMEM((head, seq), F32), pltpu.VMEM((head, seq), F32),
+            *scatter_bufs(n, db.shape[2]), *scatter_bufs(n, db.shape[2]),
+            *scatter_sems(mp), *scatter_sems(mp), DMA((2,)), DMA((2,)),
+            pltpu.VMEM((3,) + norm.shape, F32), pltpu.VMEM((3,) + norm.shape, F32), pltpu.VMEM((mp,) + norm.shape, F32),
+            DMA((3,)), DMA((3,)), DMA((mp - 1,)), DMA((mp,)),
+        ],
+        compiler_params=pltpu.CompilerParams(collective_id=3, has_side_effects=True, vmem_limit_bytes=56 << 20),
+    )(qkv, qkv, qkv, bias, hot, lse, grad, db, dc, out_rows, norm)
+
+
 def attend_back(qkv, bias, hot, lse, grad, head):
     groups, width, seq = qkv.shape
     per = width // (3 * head)
@@ -618,10 +769,11 @@
     vec = jnp.stack([jnp.pad(v, (0, 128 - v.shape[0])) for v in vec_rows] + [jnp.zeros(128, F32)])
     pa = jnp.concatenate([w_query, w_key, w_value, w_out.T], 1)
     kernels = dp == 8 and mp == 4 and rows % 16 == 0 and pa.shape[1] % 128 == 0
-    sizes = (mp,) if kernels else (dp, mp)
-    x, ct, ga, gb, gc, gvd, gvz = (fetch if kernels else fetch_plain)(
-        *sizes, tokens, cotangent, pa, w_inner, w_outer.T, vec
-    )
+    pb, pc = w_inner, w_outer.T
+    if kernels:
+        x, ga, gvd, gvz = fetch(mp, tokens, pa, vec)
+    else:
+        x, ct, ga, gb, gc, gvd, gvz = fetch_plain(dp, mp, tokens, cotangent, pa, pb, pc, vec)
     norms = jnp.swapaxes(gvd[:, :4, :rows], 0, 1).reshape(4, width)
     g1, b1, g2, b2 = (norms[i][None] for i in range(4))
     owner = d - core + m // 2
@@ -661,7 +813,10 @@
 
     a_qkv, a_out = ga[:, :, : 3 * cols], ga[:, :, 3 * cols :]
     qkv = dot("mrc,tr->mct", a_qkv, x).astype(BF16)
-    ctx, lse = attend(qkv, bias, hot, head)
+    if kernels:
+        ctx, lse, gb, gc, ct = attend_fetch(mp, qkv, bias, hot, head, pb, pc, cotangent)
+    else:
+        ctx, lse = attend(qkv, bias, hot, head)
     attn = pair_sum(dot("mct,mdc->td", ctx, a_out))
     x_mine = mine(x).astype(F32)
 
@@ -697,14 +852,23 @@
     g_attn = pair_join(g_res.astype(BF16))
     d_out = dot("td,mct->mdc", g_attn, ctx).astype(BF16)
     g_ctx = dot("td,mdc->mct", g_attn, a_out).astype(BF16)
-    dq, dk, dv = attend_back(qkv, bias, hot, lse, g_ctx, head)
+    sums = jnp.stack([d_gain1, d_shift1, d_gain2, d_shift2] + [jnp.zeros_like(d_gain1)] * 4)
+    if kernels:
+        dq, dk, dv, rb, rc, out, sums = attend_deliver(
+            mp, qkv, bias, hot, lse, g_ctx, head, d_b, d_c, out, sums, rows, quarter
+        )
+    else:
+        dq, dk, dv = attend_back(qkv, bias, hot, lse, g_ctx, head)
     dqkv = jnp.concatenate([dq, dk, dv], 1)
     d_qkv = dot("tr,mct->mrc", x, dqkv).astype(BF16)
     d_a = jnp.concatenate([d_qkv, d_out], 2)
     gtok = (g_res + pair_sum(dot("mct,mrc->tr", dqkv, a_qkv))).astype(BF16)
-    ra, rb, rc, out, gtok = (deliver if kernels else deliver_plain)(*sizes, d_a, d_b, d_c, out, gtok, rows, quarter)
+    if kernels:
+        ra, gtok = deliver(mp, d_a, gtok, rows, quarter)
+    else:
+        ra, rb, rc, out, gtok = deliver_plain(dp, mp, d_a, d_b, d_c, out, gtok, rows, quarter)
+        sums = lax.psum(sums, ("dp", "mp"))
     ra, rb, rc = (jnp.sum(v.astype(F32), 0) for v in (ra, rb, rc))
-    sums = lax.psum(jnp.stack([d_gain1, d_shift1, d_gain2, d_shift2]), ("dp", "mp"))
     sums = lax.dynamic_slice_in_dim(sums, d * rows, rows, 1)
     return (
         out, gtok, ra[:, :cols], ra[:, cols : 2 * cols], ra[:, 2 * cols : 3 * cols], ra[:, 3 * cols :].T, rb, rc.T,

time: 390 us -> 316 us (0.81)
  blocking collectives: 48.2 us -> 0 us
  Pallas kernels: 214 us -> 198 us
  starting transfers between devices: 10.9 us -> 3.7 us
  other arithmetic: 27 us -> 22.4 us
    pallas_call x2, Pallas kernels: 42.3 us -> 124 us  [the longest x1 62.1 us: attend_deliver(): pl.pallas_call(lambda *refs: attend_deliver_kernel(mp, *refs), name='atte...]
    pallas_call x1, Pallas kernels: 89.7 us -> 35.3 us  [deliver(): pl.pallas_call(lambda *refs: deliver_kernel(mp, *refs), name='deliver', o...]
    psum x1 -> x0, blocking collectives: 48.2 us -> none  [layer(): lax.psum(jnp.stack([d_gain1, d_shift1, d_gain2, d_shift2]), ('dp', 'mp'))]
    pallas_call x1, Pallas kernels: 81.9 us -> 39.4 us  [fetch(): pl.pallas_call(lambda *refs: fetch_kernel(mp, *refs), name='fetch', out_s...]
    ppermute x4, starting transfers between devices: 9.99 us -> 3.22 us  [pair_sum(): lax.ppermute(theirs(partial).astype(BF16), 'dp', swap).astype(F32)]
    unnamed x76 -> x82, local copies, waits for them, and re-layouts: 14.5 us -> 16.3 us
  transfers between devices with their start and end apart: 7 -> 7, of which waited for: 4 -> 5; matrix products, arithmetic and copies ran while one was open for 6% -> 4% of each run, Pallas kernels for 0% -> 0%
where the time goes in v2:
time: 316 us; the launch traced here: 313 us
  Pallas kernels  198 us (63%)
  matrix products  43.4 us (14%)
  local copies, waits for them, and re-layouts  30.6 us (10%)
  other arithmetic  22.4 us (7%)
  waiting for transfers between devices  11.6 us (4%)
  starting transfers between devices  3.7 us (1%)
    pallas_call x1, Pallas kernels, attend_deliver(): pl.pallas_call(lambda *refs: attend_deliver_kernel(mp, *refs), name='atte...  62.1 us
    pallas_call x1, Pallas kernels, attend_fetch(): pl.pallas_call(lambda *refs: attend_fetch_kernel(mp, *refs), name='attend...  61.5 us
    dot_general x12, matrix products, dot(): return jnp.einsum(spec, a, b, preferred_element_type=F32)  43.4 us
    pallas_call x1, Pallas kernels, fetch(): pl.pallas_call(lambda *refs: fetch_kernel(mp, *refs), name='fetch', out_s...  39.4 us
    pallas_call x1, Pallas kernels, deliver(): pl.pallas_call(lambda *refs: deliver_kernel(mp, *refs), name='deliver', o...  35.3 us
    unnamed x82, local copies, waits for them, and re-layouts  16.3 us
    ppermute x4, waiting for transfers between devices, pair_sum(): lax.ppermute(theirs(partial).astype(BF16), 'dp', swap).astype(F32)  6.99 us
  transfers between devices with their start and end apart: 7, of which 5 were waited for; matrix products, arithmetic and copies ran while one was open for 4% of the time, Pallas kernels for 0%

profile of v2, /device:TPU:0, one launch (start us, length us, event | category | flops | bytes accessed | tf_op | source)
XLA Modules:
  0.0 312.7 jit_solution(3245055959035608772)
XLA Ops:
  6.8 39.4 %fetch.1 = (bf16[1024,768]{1,0:T(8,128)(2,1)}, bf16[2,768,768]{2,1,0:T(8,128)(2,1)}, f32[8,8,128]{2,1,0:T(8,128)}, f32[4,8,128]{2,1,0:T(8,128)}) custom-call(bf16[2,256,768]{2,1,0:T(8,128)(2,1)} %refs_0_.1, bf16[96,768]{1,0:T(8,128)(2,1)} %pad_maximum_fusion.1.refs_1_, f32[8,128]{1,0:T(8,128)} %stack.65.refs_2_), custom_call_target="tpu_custom_call" | custom-call | tf_op jit(solution)/shard_map/fetch/pallas_call | solution.py:368
  50.9 5.9 %convolution_convert_fusion.refs_0_.refs_1_.refs_2_ = bf16[2,576,1024]{2,1,0:T(8,128)(2,1)} fusion(bf16[2,768,768]{2,1,0:T(8,128)(2,1)} %get-tuple-element.30, bf16[1024,768]{1,0:T(8,128)(2,1)} %get-tuple-element.31), kind=kOutput, calls=%fused_computation.12 | convolution fusion | flops 1813118976 | bytes 5898240 | tf_op jit(solution)/shard_map/mrc,tr->mct/dot_general | solution.py:812
  56.9 61.5 %attend_fetch.1 = (bf16[2,192,1024]{2,1,0:T(8,128)(2,1)S(1)}, f32[2,3,1,1024]{3,2,1,0:T(1,128)S(1)}, bf16[2,768,768]{2,1,0:T(8,128)(2,1)S(1)}, bf16[2,768,768]{2,1,0:T(8,128)(2,1)}, bf16[512,768]{1,0:T(8,128)(2,1)S(1)}) custom-call(bf16[2,576,1024]{2,1,0:T(8,128)(2,1)} %convolution_convert_fusion.refs_0_.refs_1_.refs_2_, ...), custom_call_target="tpu_custom_call" | custom-call | tf_op jit(solution)/shard_map/attend_fetch/pallas_call | solution.py:534
  120.5 4.1 %convolution_bitcast_fusion.3 = f32[1024,768]{1,0:T(8,128)} fusion(bf16[2,192,1024]{2,1,0:T(8,128)(2,1)S(1)} %get-tuple-element.36, bf16[2,768,768]{2,1,0:T(8,128)(2,1)} %get-tuple-element.30), kind=kOutput, calls=%fused_computation.16 | convolution fusion | flops 603979776 | bytes 4718592 | tf_op jit(solution)/shard_map/mct,mdc->td/dot_general | solution.py:812
  126.4 2.2 collective-permute-done
  128.6 2.2 fusion.34
  132.4 2.5 collective-permute-done.1
  136.6 5.4 %multiply_convert_fusion = (bf16[1024,2,768]{2,0,1:T(8,128)(2,1)S(1)}, f32[1024,2,768]{2,0,1:T(8,128)}) fusion(bf16[2,768,768]{2,1,0:T(8,128)(2,1)S(1)} %copy-done.7, bf16[512,768]{1,0:T(8,128)(2,1)S(1)} %get-tuple-element.133, bf16[512,768]{1,0:T(8,128)(2,1)S(1)} %get-tuple-element.132), kind=kOutput, calls=%fused_computation.7 | convolution fusion | flops 2426929152 | bytes 13369344 | tf_op jit(solution)/shard_map/td,mdk->tmk/dot_general | solution.py:812
  142.0 2.6 convolution_bitcast_fusion.2
  147.6 2.3 collective-permute-done.2
  149.9 2.2 fusion.33
  157.5 4.7 %fusion.5 = bf16[1024,2,768]{2,0,1:T(8,128)(2,1)S(1)} fusion(f32[1024,2,768]{2,0,1:T(8,128)S(1)} %copy-done.32, bf16[2,768,768]{2,1,0:T(8,128)(2,1)S(1)} %copy-done.31, bf16[512,768]{1,0:T(8,128)(2,1)S(1)} %get-tuple-element.131, bf16[512,768]{1,0:T(8,128)(2,1)S(1)} %get-tuple-element.130), kind=kOutput, calls=%fused_computation.6 | convolution fusion | flops 2434793472 | bytes 13369344 | tf_op jit(solution)/shard_map/td,mdk->tmk/dot_general | solution.py:812
  162.2 2.6 convolution_bitcast_fusion.1
  167.7 2.5 collective-permute-done.4
  170.1 3.1 multiply_reduce_fusion.1
  176.2 3.9 %convert_bitcast_fusion.1.refs_7_ = bf16[2,768,768]{2,1,0:T(8,128)(2,1)} fusion(bf16[1024,2,768]{2,0,1:T(8,128)(2,1)S(1)} %copy-done.36, bf16[512,768]{1,0:T(8,128)(2,1)S(1)} %copy-done.17, bf16[512,768]{1,0:T(8,128)(2,1)S(1)} %copy-done.15), kind=kOutput, calls=%fused_computation.11 | convolution fusion | flops 2420244480 | bytes 7077888 | tf_op jit(solution)/shard_map/td,tmk->mdk/dot_general | solution.py:812
  180.1 3.9 %convert_bitcast_fusion.refs_8_ = bf16[2,768,768]{2,1,0:T(8,128)(2,1)} fusion(bf16[1024,2,768]{2,0,1:T(8,128)(2,1)S(1)} %copy-done.34, bf16[512,768]{1,0:T(8,128)(2,1)S(1)} %copy-done.24, bf16[512,768]{1,0:T(8,128)(2,1)S(1)} %copy-done.22), kind=kOutput, calls=%fused_computation.10 | convolution fusion | flops 2420244480 | bytes 7077888 | tf_op jit(solution)/shard_map/td,tmk->mdk/dot_general | solution.py:812
  186.4 2.2 convolution_convert_fusion.2.refs_6_
  189.4 62.1 %attend_deliver.1 = (bf16[2,192,1024]{2,1,0:T(8,128)(2,1)}, bf16[2,192,1024]{2,1,0:T(8,128)(2,1)}, bf16[2,192,1024]{2,1,0:T(8,128)(2,1)}, bf16[4,96,768]{2,1,0:T...) custom-call(bf16[2,576,1024]{2,1,0:T(8,128)(2,1)} %convolution_convert_fusion.refs_0_.refs, ...), custom_call_target="tpu_custom_call" | custom-call | tf_op jit(solution)/shard_map/attend_deliver/pallas_call | solution.py:660
  254.3 3.2 %convolution_convert_fusion.1 = bf16[2,576,768]{2,1,0:T(8,128)(2,1)} fusion(bf16[2,576,1024]{2,1,0:T(8,128)(2,1)S(1)} %constant_dynamic-update-slice_fusion, bf16[1024,768]{1,0:T(8,128)(2,1)S(1)} %copy-done.27), kind=kOutput, calls=%fused_computation.17 | convolution fusion | flops 1812824064 | bytes 5701632 | tf_op jit(solution)/shard_map/tr,mct->mrc/dot_general | solution.py:812
  257.6 4.0 %convolution_bitcast_fusion = f32[1024,768]{1,0:T(8,128)} fusion(bf16[2,576,1024]{2,1,0:T(8,128)(2,1)S(1)} %constant_dynamic-update-slice_fusion, bf16[2,768,768]{2,1,0:T(8,128)(2,1)S(1)} %copy-done.28), kind=kOutput, calls=%fused_computation.13 | convolution fusion | flops 1811939328 | bytes 7471104 | tf_op jit(solution)/shard_map/mct,mrc->tr/dot_general | solution.py:812
  261.8 2.7 copy.104
  266.2 2.9 collective-permute-start.6
  274.0 35.3 %deliver.1 = (bf16[4,96,768]{2,1,0:T(8,128)(2,1)S(1)}, bf16[2,256,768]{2,1,0:T(8,128)(2,1)S(1)}) custom-call(bf16[2,768,768]{2,1,0:T(8,128)(2,1)S(1)} %pad_maximum_fusion.refs_0_, bf16[512,768]{1,0:T(8,128)(2,1)S(1)} %add_convert_fusion.refs_1_), custom_call_target="tpu_custom_call" | custom-call | tf_op jit(solution)/shard_map/deliver/pallas_call | solution.py:404
  (168 shorter events, 46.5 us)
Async XLA Ops:
  48.0 8.8 %copy-start = (bf16[2,3,16,1024]{3,2,1,0:T(8,128)(2,1)}, bf16[2,3,16,1024]{3,2,1,0:T(8,128)(2,1)S(1)}, u32[]{:S(2)}) copy-start(bf16[2,3,16,1024]{3,2,1,0:T(8,128)(2,1)S(1)} %reshape.220.refs_3_) | copy-start | bytes 589828
  50.9 6.0 %copy-start.1 = (bf16[2,256,768]{2,1,0:T(8,128)(2,1)S(1)}, bf16[2,256,768]{2,1,0:T(8,128)(2,1)}, u32[]{:S(2)}) copy-start(bf16[2,256,768]{2,1,0:T(8,128)(2,1)} %refs_7_.1) | copy-start | bytes 2359300
  50.9 6.0 %copy-start.3 = (bf16[96,768]{1,0:T(8,128)(2,1)S(1)}, bf16[96,768]{1,0:T(8,128)(2,1)}, u32[]{:S(2)}) copy-start(bf16[96,768]{1,0:T(8,128)(2,1)} %refs_5_.1) | copy-start | bytes 442372
  50.9 6.0 %copy-start.4 = (bf16[768,96]{0,1:T(8,128)(2,1)S(1)}, bf16[768,96]{0,1:T(8,128)(2,1)}, u32[]{:S(2)}) copy-start(bf16[768,96]{0,1:T(8,128)(2,1)} %param.21) | copy-start | bytes 442372
  56.9 61.6 %copy-start.2 = (bf16[32,1024]{1,0:T(8,128)(2,1)}, bf16[32,1024]{1,0:T(8,128)(2,1)S(1)}, u32[]{:S(2)}) copy-start(bf16[32,1024]{1,0:T(8,128)(2,1)S(1)} %add_convert_fusion.1.refs_4_) | copy-start | bytes 196612
  126.1 2.5 collective-permute-start
  132.3 2.6 collective-permute-start.1
  136.5 5.5 %copy-start.14 = (bf16[512,768]{1,0:T(8,128)(2,1)}, bf16[512,768]{1,0:T(8,128)(2,1)S(1)}, u32[]{:S(2)}) copy-start(bf16[512,768]{1,0:T(8,128)(2,1)S(1)} %get-tuple-element.132) | copy-start | bytes 2359300
  136.5 5.5 %copy-start.16 = (bf16[512,768]{1,0:T(8,128)(2,1)}, bf16[512,768]{1,0:T(8,128)(2,1)S(1)}, u32[]{:S(2)}) copy-start(bf16[512,768]{1,0:T(8,128)(2,1)S(1)} %get-tuple-element.133) | copy-start | bytes 2359300
  136.6 5.5 %copy-start.30 = (bf16[2,768,768]{2,1,0:T(8,128)(2,1)S(1)}, bf16[2,768,768]{2,1,0:T(8,128)(2,1)}, u32[]{:S(2)}) copy-start(bf16[2,768,768]{2,1,0:T(8,128)(2,1)} %get-tuple-element.38) | copy-start | bytes 7077892
  147.3 2.6 collective-permute-start.2
  152.5 5.0 %copy-start.32 = (f32[1024,2,768]{2,0,1:T(8,128)S(1)}, f32[1024,2,768]{2,0,1:T(8,128)}, u32[]{:S(2)}) copy-start(f32[1024,2,768]{2,0,1:T(8,128)} %get-tuple-element.145) | copy-start | bytes 18874372
  155.0 2.4 collective-permute-start.3
  157.5 4.7 %copy-start.21 = (bf16[512,768]{1,0:T(8,128)(2,1)}, bf16[512,768]{1,0:T(8,128)(2,1)S(1)}, u32[]{:S(2)}) copy-start(bf16[512,768]{1,0:T(8,128)(2,1)S(1)} %get-tuple-element.130) | copy-start | bytes 2359300
  157.5 4.7 %copy-start.23 = (bf16[512,768]{1,0:T(8,128)(2,1)}, bf16[512,768]{1,0:T(8,128)(2,1)S(1)}, u32[]{:S(2)}) copy-start(bf16[512,768]{1,0:T(8,128)(2,1)S(1)} %get-tuple-element.131) | copy-start | bytes 2359300
  157.5 4.7 %copy-start.8 = (bf16[2,768,768]{2,1,0:T(8,128)(2,1)S(1)}, bf16[2,768,768]{2,1,0:T(8,128)(2,1)}, u32[]{:S(2)}) copy-start(bf16[2,768,768]{2,1,0:T(8,128)(2,1)} %copy-done.6) | copy-start | bytes 7077892
  167.5 2.6 collective-permute-start.4
  175.0 5.2 %copy-start.22 = (bf16[512,768]{1,0:T(8,128)(2,1)S(1)}, bf16[512,768]{1,0:T(8,128)(2,1)}, u32[]{:S(2)}) copy-start(bf16[512,768]{1,0:T(8,128)(2,1)} %copy-done.21) | copy-start | bytes 2359300
  175.0 5.2 %copy-start.24 = (bf16[512,768]{1,0:T(8,128)(2,1)S(1)}, bf16[512,768]{1,0:T(8,128)(2,1)}, u32[]{:S(2)}) copy-start(bf16[512,768]{1,0:T(8,128)(2,1)} %copy-done.23) | copy-start | bytes 2359300
  175.0 5.2 %copy-start.34 = (bf16[1024,2,768]{2,0,1:T(8,128)(2,1)S(1)}, bf16[1024,2,768]{2,0,1:T(8,128)(2,1)}, u32[]{:S(2)}) copy-start(bf16[1024,2,768]{2,0,1:T(8,128)(2,1)} %copy-done.33) | copy-start | bytes 9437188
  175.0 9.8 %collective-permute-start.5 = (bf16[512,768]{1,0:T(8,128)(2,1)S(1)}, bf16[512,768]{1,0:T(8,128)(2,1)S(1)}, u32[]{:S(2)}, u32[]{:S(2)}) collective-permute-start(bf16[512,768]{1,0:T(8,128)(2,1)S(1)} %get-tuple-element.120), channel_id=1, source_target_pairs={{0,4},{4,0},{8,12},{12,8},{16,20},{20,16},{24,28},{28,24},{1,5},{5... | collective-permute-start | bytes 2359304 | tf_op jit(solution)/shard_map/ppermute | solution.py:806
  264.6 5.2 %copy-start.26 = (bf16[4,96,768]{2,1,0:T(8,128)(2,1)S(1)}, bf16[4,96,768]{2,1,0:T(8,128)(2,1)}, u32[]{:S(2)}) copy-start(bf16[4,96,768]{2,1,0:T(8,128)(2,1)} %get-tuple-element.45) | copy-start | bytes 1769476
  264.6 6.0 %copy-start.25 = (bf16[4,96,768]{2,1,0:T(8,128)(2,1)S(1)}, bf16[4,96,768]{2,1,0:T(8,128)(2,1)}, u32[]{:S(2)}) copy-start(bf16[4,96,768]{2,1,0:T(8,128)(2,1)} %get-tuple-element.46) | copy-start | bytes 1769476
  266.2 6.2 %collective-permute-start.6 = (bf16[512,768]{1,0:T(8,128)(2,1)S(1)}, bf16[512,768]{1,0:T(8,128)(2,1)S(1)}, u32[]{:S(2)}, u32[]{:S(2)}) collective-permute-start(bf16[512,768]{1,0:T(8,128)(2,1)S(1)} %dynamic-slice_convert_fusion), channel_id=1, source_target_pairs={{0,4},{4,0},{8,12},{12,8},{16,20},{20,16},{24,28},{28,24},{1,5},{5... | collective-permute-start | bytes 2359304 | tf_op jit(solution)/shard_map/ppermute | solution.py:803
  (20 other events, 39.3 us)

commit v3 on v1

--- a/solution.py
+++ b/solution.py
@@ -68,6 +68,10 @@
     pl.semaphore_wait(barrier, len(peers))
 
 
+def dots(a, b, ca, cb):
+    return lax.dot_general(a, b, (((ca,), (cb,)), ((), ())), preferred_element_type=F32)
+
+
 def column_peers(p, mp):
     peers = []
     for k in range(1, mp):
@@ -77,19 +81,21 @@
 
 
 class Gather:
-    def __init__(self, p, src, dst, sems, mp):
+    def __init__(self, p, src, dst, first, count, sems, mp):
         self.p, self.src, self.dst, self.mp = p, src, dst, mp
         self.zs, self.zr, self.xs, self.xr, self.ys, self.yr = sems
         self.n = src.shape[0]
+        self.cols = pl.ds(first, count)
 
     def rows(self, a, first, count):
-        return self.dst.at[a, pl.ds(first * self.n, count * self.n), :]
+        return self.dst.at[a, pl.ds(first * self.n, count * self.n), self.cols]
 
     def z_args(self, k):
         p = self.p
         z = lax.rem(p.m + k, self.mp)
         same = (p.h == p.c) if k == 0 else None
-        return (self.src, self.rows(p.a, p.d, 1), self.zs.at[k], self.zr.at[2 * p.c + p.a], (p.base + p.h, z)), same
+        src = self.src.at[:, self.cols]
+        return (src, self.rows(p.a, p.d, 1), self.zs.at[k], self.zr.at[2 * p.c + p.a], (p.base + p.h, z)), same
 
     def z_send(self):
         for k in (2, 1, 3, 0):
@@ -132,11 +138,13 @@
         self.arrived(1, 0, 1)
         self.hop(0, 1, 1).start()
 
-    def finish(self):
+    def land(self):
         self.arrived(0, 0, 1)
         self.arrived(1, 0, 0)
         self.arrived(1, 1, 0)
         self.arrived(0, 1, 1)
+
+    def finish(self):
         for k in range(self.mp):
             args, same = self.z_args(k)
             if same is None:
@@ -183,10 +191,14 @@
             got(self.part(q, p.c), self.s.at[0], self.r.at[q], (p.d, p.m))
             remote(self.part(q, p.c), self.part(q, p.c), self.fs.at[q], self.fr.at[q], (p.sib, p.m)).start()
 
-    def finish(self, mp):
+    def land(self, mp):
         p = self.p
         for q in range(mp):
             got(self.part(q, 1 - p.c), self.fs.at[q], self.fr.at[q], (p.d, p.m))
+
+    def finish(self, mp):
+        p = self.p
+        for q in range(mp):
             remote(self.part(q, p.c), self.part(q, p.c), self.fs.at[q], self.fr.at[q], (p.sib, p.m)).wait_send()
         for i in range(2):
             for half in range(2):
@@ -249,199 +261,630 @@
 
 
 class Scatter:
-    def __init__(self, p, src, out, bufs, sems, mp):
-        self.p, self.src, self.out, self.mp = p, src, out, mp
+    def __init__(self, p, src, out, a, first, count, axis, bufs, sems, mp):
+        self.p, self.src, self.out, self.a, self.axis, self.mp = p, src, out, a, axis, mp
         self.r1, self.r2, self.r3, self.total = bufs
-        self.xs, self.xr, self.ys, self.yr, self.zs, self.zr = sems
+        self.s, self.r, self.zs, self.zr = sems
         self.n = out.shape[1]
-
-    def rows(self, a, first):
-        return self.src.at[a, pl.ds(first * self.n, 2 * self.n), :]
-
-    def hop(self, kind, axis):
-        p = self.p
-        peer = p.xp if axis == 0 else p.yp
-        s, r = (self.xs, self.xr) if axis == 0 else (self.ys, self.yr)
+        self.cols = pl.ds(first, count)
+        self.near, self.far = ((p.xp, p.bx), (p.yp, p.by)) if axis == 0 else ((p.yp, p.by), (p.xp, p.bx))
+
+    def rows(self, first):
+        return self.src.at[self.a, pl.ds(first * self.n, 2 * self.n), self.cols]
+
+    def hop(self, kind):
+        p = self.p
         if kind == 0:
-            a = 1 if axis == 0 else 0
-            src, dst = self.rows(a, p.bd), self.r1.at[axis]
+            src, dst, peer = self.rows(p.bd), self.r1, self.near[0]
         elif kind == 1:
-            a = 1 if axis == 0 else 0
-            src, dst = self.rows(a, p.bx if axis == 0 else p.by), self.r2.at[axis]
+            src, dst, peer = self.rows(self.near[1]), self.r2, self.near[0]
         else:
-            src, dst = self.r1.at[1 - axis], self.r3.at[axis]
-        return remote(src, dst, s.at[kind], r.at[kind], (peer, p.m))
-
-    def first(self):
-        for axis in range(2):
-            self.hop(0, axis).start()
-        for axis in range(2):
-            self.hop(1, axis).start()
+            src, dst, peer = self.r1, self.r3, self.far[0]
+        return remote(src, dst, self.s.at[kind], self.r.at[kind], (peer, p.m))
+
+    def start(self):
+        self.hop(0).start()
+        self.hop(1).start()
 
     def second(self):
-        p = self.p
-        for axis in range(2):
-            other = 1 - axis
-            self.hop(0, axis).wait_recv()
-            a = 1 if axis == 0 else 0
-            rows = pl.ds((p.by if axis == 0 else p.bx) * self.n, 2 * self.n)
-            self.r1[axis] = (self.src[a, rows, :].astype(F32) + self.r1[axis].astype(F32)).astype(BF16)
-            self.hop(2, other).start()
+        self.hop(0).wait_recv()
+        self.r1[...] = (self.rows(self.far[1])[...].astype(F32) + self.r1[...].astype(F32)).astype(BF16)
+        self.hop(2).start()
 
     def third(self):
-        p = self.p
-        rows = pl.ds(p.base * self.n, 2 * self.n)
-        for axis in range(2):
-            self.hop(1, axis).wait_recv()
-            self.hop(2, axis).wait_recv()
+        self.hop(1).wait_recv()
+        self.hop(2).wait_recv()
+        self.total[...] = (
+            self.rows(self.p.base)[...].astype(F32) + self.r2[...].astype(F32) + self.r3[...].astype(F32)
+        ).astype(BF16)
+        for core in range(2):
+            args, same = self.z_args(core)
+            push(*args, same)
+
+    def z_args(self, core):
+        p = self.p
+        owner = (p.base + core, 2 * p.c + self.a)
+        same = jnp.logical_and(p.c == core, p.m == 2 * p.c + self.a)
+        src = self.total.at[pl.ds(core * self.n, self.n), :]
+        return (src, self.out.at[p.m, :, self.cols], self.zs.at[core], self.zr.at[p.m], owner), same
+
+    def finish(self):
+        for kind in range(3):
+            self.hop(kind).wait_send()
+        for core in range(2):
+            args, same = self.z_args(core)
+            pushed(*args, same)
+
+
+def owned(p, out, first, count, zs, zr, mp):
+    for z in range(mp):
+        got(out.at[z, :, pl.ds(first, count)], zs.at[0], zr.at[z], (p.d, p.m))
+
+
+class Sums:
+    def __init__(self, p, out, bufs, sems, mp):
+        self.p, self.out, self.mp = p, out, mp
+        self.mine, self.came, self.parts = bufs
+        self.s, self.r, self.zs, self.zr = sems
+
+    def hop(self, i):
+        p = self.p
+        dev = (p.sib, p.xp, p.yp)[i]
+        return remote(self.mine.at[i], self.came.at[i], self.s.at[i], self.r.at[i], (dev, p.m))
+
+    def start(self, values):
+        self.mine[0] = values
+        self.hop(0).start()
+
+    def step(self, i):
+        self.hop(i).wait_recv()
+        total = self.mine[i] + self.came[i]
+        if i < 2:
+            self.mine[i + 1] = total
+            self.hop(i + 1).start()
+        else:
+            self.parts[self.p.m] = total
+            for k in range(1, self.mp):
+                self.column(k).start()
+
+    def column(self, k):
+        p = self.p
+        part = self.parts.at[p.m]
+        return remote(part, part, self.zs.at[k - 1], self.zr.at[p.m], (p.d, lax.rem(p.m + k, self.mp)))
+
+    def finish(self):
+        p = self.p
+        for k in range(1, self.mp):
+            z = lax.rem(p.m + k, self.mp)
+            got(self.parts.at[z], self.zs.at[0], self.zr.at[z], (p.d, p.m))
+        total = self.parts[0]
+        for z in range(1, self.mp):
+            total = total + self.parts[z]
+        self.out[...] = total
+        for i in range(3):
+            self.hop(i).wait_send()
+        for k in range(1, self.mp):
+            self.column(k).wait_send()
+
+
+class Swap:
+    def __init__(self, p, src, dst, sems, src_first=0, dst_first=0, came_first=0, count=256):
+        self.p, self.src, self.dst = p, src, dst
+        self.s, self.r = sems
+        self.firsts = (src_first, dst_first, came_first)
+        self.n = count
+
+    def copy(self, i, side):
+        p, n = self.p, self.n
+        src_first, dst_first, came_first = self.firsts
+        if side == 0:
+            src = self.src.at[pl.ds(src_first + i * n, n), :]
+            dst = self.dst.at[pl.ds(dst_first + i * n, n), :]
+        else:
+            src = dst = self.dst.at[pl.ds(came_first + i * n, n), :]
+        return remote(src, dst, self.s.at[i], self.r.at[i], (p.sib, p.m))
+
+    def send(self, i):
+        self.copy(i, 0).start()
+
+    def recv(self, i):
+        self.copy(i, 1).wait_recv()
+
+    def finish(self):
+        for i in range(2):
+            self.copy(i, 0).wait_send()
+
+
+def gelu_pair(inner):
+    cumul = 0.5 * (1.0 + lax.erf(inner * (1.0 / math.sqrt(2.0))))
+    slope = cumul + inner * jnp.exp(-0.5 * inner * inner) * (1.0 / math.sqrt(2.0 * math.pi))
+    return inner * cumul, slope
+
+
+def norm_back(e, n, inv):
+    return (e - jnp.mean(e, -1, keepdims=True) - n * jnp.mean(e * n, -1, keepdims=True)) * inv
+
+
+def norm_rows(z):
+    centre = z - jnp.mean(z, -1, keepdims=True)
+    inv = lax.rsqrt(jnp.mean(centre * centre, -1, keepdims=True) + EPS)
+    return centre * inv, inv
+
+
+def scatter_sems(mp):
+    return [DMA((3,)), DMA((3,)), DMA((2,)), DMA((mp,))]
+
+
+def layer_kernel(mp, head, nblocks, picks, names, *refs):
+    r = dict(zip(names, refs, strict=True))
+    p = Place()
+    x, ga, gb, gc, at, qkv, ctx, gctx = (r[k] for k in ("x", "ga", "gb", "gc", "at", "qkv", "ctx", "gctx"))
+    seq, width = x.shape
+    half = seq // 2
+    rc = half // 2
+    group = qkv.shape[0] // 2
+    cols = group // 3
+    per = cols // head
+    heads = 2 * per
+    n = r["pa"].shape[0]
+    scale = 1.0 / math.sqrt(head)
+    mine = pl.multiple_of(p.c * half, half)
+    theirs = pl.multiple_of(half - p.c * half, half)
+    hw = width // 2
+
+    def sems(key):
+        return [v for k, v in r.items() if k.startswith(key + ".")]
+
+    tokens = Tokens(p, r["tok"], x, sems("tok"))
+    cots = Quarters(p, r["cot"], r["ct"], sems("cot"))
+    gathers = [
+        Gather(p, r["p" + w], r["g" + w], i * hw, hw, sems(f"g{w}{i}"), mp) for w in "abc" for i in range(2)
+    ]
+    a0, a1, b0, b1, c0, c1 = gathers
+    plane = [lax.rem(p.d + k, 8) for k in range(1, 8)]
+    vec, pick, gvec, gpick = r["vec"], r["pick"], r["gvec"], r["gpick"]
+    vs, vr, us, ur = sems("vec")
+    sums = Sums(p, r["sums"], sems("sumbuf"), sems("sum"), mp)
+    home = Homewards(p, r["outb"], r["hout"], sems("home"))
+    home_g = Homewards(p, r["gtokb"], r["hgtok"], sems("homeg"))
+    pair_attn = Swap(p, r["send"], r["recv"], sems("sw0"), count=rc)
+    pair_hid = Swap(p, r["hb"], r["hb"], sems("sw1"), mine, mine, theirs, rc)
+    pair_ffn = Swap(p, r["send1"], r["recv1"], sems("sw2"), count=rc)
+    pair_gf = Swap(p, r["gf"], r["gf"], sems("sw3"), mine, mine, theirs, rc)
+    pair_gh = Swap(p, r["send2"], r["recv2"], sems("sw4"), count=rc)
+    pair_ga = Swap(p, r["gat"], r["gat"], sems("sw5"), mine, mine, theirs, rc)
+    pair_gt = Swap(p, r["send3"], r["recv3"], sems("sw6"), count=rc)
+
+    def units(name, src, out):
+        made = []
         for a in range(2):
-            self.total[a] = (
-                self.src[a, rows, :].astype(F32)
-                + self.r2[1 - a].astype(F32)
-                + self.r3[a].astype(F32)
-            ).astype(BF16)
-        for a in range(2):
-            for core in range(2):
-                args, same = self.z_args(a, core)
-                push(*args, same)
-
-    def z_args(self, a, core):
-        p = self.p
-        i = 2 * a + core
-        owner = (p.base + core, 2 * p.c + a)
-        same = jnp.logical_and(p.c == core, p.m == 2 * p.c + a)
-        src = self.total.at[a, pl.ds(core * self.n, self.n), :]
-        return (src, self.out.at[p.m], self.zs.at[i], self.zr.at[p.m], owner), same
-
-    def finish(self):
-        p = self.p
-        for z in range(self.mp):
-            got(self.out.at[z], self.zs.at[0], self.zr.at[z], (p.d, p.m))
-        for axis in range(2):
-            for kind in range(3):
-                self.hop(kind, axis).wait_send()
-        for a in range(2):
-            for core in range(2):
-                args, same = self.z_args(a, core)
-                pushed(*args, same)
-
-
-def scatter_bufs(n, width):
-    return [pltpu.VMEM((2, 2 * n, width), BF16)] * 4
-
-
-def scatter_sems(mp):
-    return [DMA((3,)), DMA((3,)), DMA((3,)), DMA((3,)), DMA((4,)), DMA((mp,))]
-
-
-def fetch_kernel(mp, tok, cot, pa, pb, pc, vec, x, ct, ga, gb, gc, gvd, gvz, *sems):
-    p = Place()
-    vs, vr, us, ur = sems[:4]
-    tokens = Tokens(p, tok, x, sems[4:8])
-    cots = Quarters(p, cot, ct, sems[8:10])
-    weights = [Gather(p, s, g, sems[10 + 6 * i : 16 + 6 * i], mp) for i, (s, g) in enumerate(((pa, ga), (pb, gb), (pc, gc)))]
-    plane = [lax.rem(p.d + k, 8) for k in range(1, 8)]
+            for i in range(2):
+                made.append(Scatter(p, src, out, a, i * hw, hw, i, sems(f"s{name}{a}{i}b"), sems(f"s{name}{a}{i}s"), mp))
+        return made
+
+    ua, ub, uc = units("a", ga, r["la"]), units("b", r["db"], r["lb"]), units("c", r["dc"], r["lc"])
+
     greet(column_peers(p, mp) + [(d, p.m) for d in plane])
-    weights[0].z_send()
+    a0.z_send()
+    a1.z_send()
     tokens.send()
-    vcopies = [remote(vec, gvd.at[p.d], vs.at[k], vr.at[p.d], (d, p.m)) for k, d in enumerate(plane)]
-    ucopies = [remote(vec, gvz.at[p.m], us.at[k - 1], ur.at[p.m], (p.d, lax.rem(p.m + k, mp))) for k in range(1, mp)]
-    own = [pltpu.make_async_copy(vec, gvd.at[p.d], vr.at[p.d]), pltpu.make_async_copy(vec, gvz.at[p.m], ur.at[p.m])]
+    vcopies = [remote(vec, gvec.at[p.d], vs.at[k], vr.at[p.d], (d, p.m)) for k, d in enumerate(plane)]
+    ucopies = [remote(pick, gpick.at[p.m], us.at[k - 1], ur.at[p.m], (p.d, lax.rem(p.m + k, mp))) for k in range(1, mp)]
+    own = [pltpu.make_async_copy(vec, gvec.at[p.d], vr.at[p.d]), pltpu.make_async_copy(pick, gpick.at[p.m], ur.at[p.m])]
     for copy in vcopies + ucopies + own:
         copy.start()
-    weights[0].z_recv()
-    weights[0].xy_send()
-    weights[1].z_send()
+    a0.z_recv()
+    a0.xy_send()
+    a1.z_recv()
+    a1.xy_send()
+
+    for d in range(8):
+        got(gvec.at[d], vs.at[0], vr.at[d], (p.d, p.m))
+    for z in range(mp):
+        got(gpick.at[z], us.at[0], ur.at[z], (p.d, p.m))
+    vecs = gvec[0].astype(F32)
+    for d in range(1, 8):
+        vecs = vecs + gvec[d].astype(F32)
+    r["norms"][...] = vecs
+    lane = lax.broadcasted_iota(jnp.int32, (1, width), 1)
+    spot = (p.base + p.h) * n + 2 * p.a
+    row = vecs[4:5]
+    length = jnp.sum(jnp.where(lane == spot, row * 32.0, 0.0) + jnp.where(lane == spot + 1, row, 0.0), 1, keepdims=True)
+    block = seq // nblocks
+    sub = lax.broadcasted_iota(jnp.int32, (nblocks, seq), 0)
+    place = lax.broadcasted_iota(jnp.int32, (nblocks, seq), 1)
+    rb = lax.div(place, block)
+    near = (rb == 0) | (rb == nblocks - 1) | (sub == 0) | (sub == nblocks - 1) | (jnp.abs(rb - sub) <= 1)
+    spread = lax.broadcasted_iota(jnp.int32, (128, seq), 0) == lax.div(lax.broadcasted_iota(jnp.int32, (128, seq), 1), block)
+    spread = jnp.where(spread, 1.0, 0.0).astype(BF16)
+    subf = sub.astype(F32)
+    for a in range(2):
+        wide = dots(gpick[2 * p.c + a], spread, 1, 0)
+        for h in range(per):
+            hit = near
+            for j in range(picks):
+                at_row = h * picks + j
+                hit = hit | (wide[at_row : at_row + 1] == subf)
+            r["bias"][a * per + h] = jnp.where(hit, 0.0, NEG).astype(BF16)
+    qa, ka = r["qa"], r["ka"]
+    low = lax.broadcasted_iota(jnp.int32, (16, seq), 0)
+    ka[head : head + nblocks, :] = jnp.where(rb == sub, 1.0, 0.0).astype(BF16)
+    beyond = lax.broadcasted_iota(jnp.int32, (16, seq), 1).astype(F32) >= length
+    ka[head + nblocks :, :] = jnp.where((low == 0) & beyond, 1.0, 0.0).astype(BF16)
+    qa[head + nblocks :, :] = jnp.where(low == 0, NEG, 0.0).astype(BF16)
+
+    a0.forward()
+    a1.forward()
     tokens.forward(mp)
-    weights[0].forward()
-    weights[1].z_recv()
-    weights[1].xy_send()
-    weights[2].z_send()
+    b0.z_send()
+    b1.z_send()
+    a0.land()
+    a1.land()
+    for a in range(2):
+        at[a] = ga[a].T
+    tokens.land(mp)
+
+    def project(i, _):
+        rows = pl.ds(pl.multiple_of(i * rc, rc), rc)
+        for a in range(2):
+            qkv[a * group : (a + 1) * group, rows] = dots(at[a, :group, :], x[rows, :], 1, 1).astype(BF16)
+        return 0
+
+    lax.fori_loop(0, seq // rc, project, 0)
+
+    def parts(i):
+        a = lax.div(i, per)
+        first = a * group + (i - a * per) * head
+        return [pl.ds(pl.multiple_of(first + part * cols, head), head) for part in range(3)]
+
+    def set_head(i):
+        q, k, v = parts(i)
+        qa[0:head, :] = (qkv[q, :].astype(F32) * scale).astype(BF16)
+        qa[head : head + nblocks, :] = r["bias"][i]
+        ka[0:head, :] = qkv[k, :]
+        return q, k, v
+
+    def attend_head(i, _):
+        q, k, v = set_head(i)
+        own_rows = pl.ds(pl.multiple_of(i * head, head), head)
+        for j in range(2):
+            span = slice(j * half, (j + 1) * half)
+            scores = dots(ka[...], qa[:, span], 0, 0)
+            peak = jnp.max(scores, 0, keepdims=True)
+            weights = jnp.exp(scores - peak)
+            total = jnp.sum(weights, 0, keepdims=True)
+            mixed = jnp.dot(qkv[v, :], weights.astype(BF16), preferred_element_type=F32)
+            ctx[own_rows, span] = (mixed / total).astype(BF16)
+            r["lse"][i, :, span] = peak + jnp.log(total)
+
+        @pl.when(i == 2)
+        def _():
+            b0.z_recv()
+            b0.xy_send()
+            b1.z_recv()
+            b1.xy_send()
+            c0.z_send()
+            c1.z_send()
+
+        return 0
+
+    lax.fori_loop(0, heads, attend_head, 0)
+    b0.forward()
+
+    wo = r["wo"]
+    for a in range(2):
+        wo[a * cols : (a + 1) * cols, :] = at[a, group:, :]
+    norms = r["norms"]
+    g1, s1, g2, s2 = (norms[i : i + 1] for i in range(4))
+
+    def attn_part(first):
+        return dots(ctx[:, pl.ds(first, rc)], wo[...], 0, 0)
+
+    for i in range(2):
+        r["send"][i * rc : (i + 1) * rc, :] = attn_part(pl.multiple_of(theirs + i * rc, rc)).astype(BF16)
+        pair_attn.send(i)
+    b1.forward()
+    for i in range(2):
+        rows = pl.ds(pl.multiple_of(mine + i * rc, rc), rc)
+        here = slice(i * rc, (i + 1) * rc)
+        part = attn_part(pl.multiple_of(mine + i * rc, rc))
+        pair_attn.recv(i)
+        n1, inv = norm_rows(x[rows, :].astype(F32) + part + r["recv"][here, :].astype(F32))
+        hidden = n1 * g1 + s1
+        r["n1"][here, :] = n1
+        r["inv1"][here, :] = jnp.broadcast_to(inv, (rc, 128))
+        r["res"][here, :] = hidden
+        r["hb"][rows, :] = hidden.astype(BF16)
+        pair_hid.send(i)
+
+    c0.z_recv()
+    c0.xy_send()
+    c1.z_recv()
+    c1.xy_send()
     cots.send()
-    weights[1].forward()
-    weights[2].z_recv()
-    weights[2].xy_send()
-    weights[2].forward()
-    tokens.finish(mp)
+    b0.land()
+    b1.land()
+
+    def up(i, _):
+        for k in range(2):
+
+            @pl.when(i == 2 + k)
+            def _():
+                pair_hid.recv(k)
+
+        rows = pl.ds(pl.multiple_of(lax.rem(2 * p.c + i, 4) * rc, rc), rc)
+        for a in range(2):
+            active, slope = gelu_pair(dots(r["hb"][rows, :], gb[a], 1, 0))
+            r["act"][rows, a * width : (a + 1) * width] = active.astype(BF16)
+            r["slope"][rows, a * width : (a + 1) * width] = slope.astype(BF16)
+        return 0
+
+    lax.fori_loop(0, 4, up, 0)
+    c0.forward()
+    c1.forward()
+    c0.land()
+    c1.land()
+
+    def ffn_part(rows):
+        return dots(r["act"][rows, :width], gc[0], 1, 1) + dots(r["act"][rows, width:], gc[1], 1, 1)
+
+    for i in range(2):
+        r["send1"][i * rc : (i + 1) * rc, :] = ffn_part(pl.ds(pl.multiple_of(theirs + i * rc, rc), rc)).astype(BF16)
+        pair_ffn.send(i)
     cots.finish()
-    for w in weights:
-        w.finish()
-    for d in range(8):
-        got(gvd.at[d], vs.at[0], vr.at[d], (p.d, p.m))
-    for z in range(mp):
-        got(gvz.at[z], us.at[0], ur.at[z], (p.d, p.m))
+    small = r["small"]
+    small[...] = jnp.zeros_like(small)
+    for i in range(2):
+        rows = pl.ds(pl.multiple_of(mine + i * rc, rc), rc)
+        here = slice(i * rc, (i + 1) * rc)
+        part = ffn_part(rows)
+        pair_ffn.recv(i)
+        n2, inv = norm_rows(r["res"][here, :] + part + r["recv1"][here, :].astype(F32))
+        pos = (lax.broadcasted_iota(jnp.int32, (rc, 1), 0) + (mine + i * rc)).astype(F32)
+        valid = jnp.where(pos < length, 1.0, 0.0)
+        r["outb"][here, :] = ((n2 * g2 + s2) * valid).astype(BF16)
+        gy = r["ct"][here, :].astype(F32) * valid
+        small[2:3, :] += jnp.sum(gy * n2, 0, keepdims=True)
+        small[3:4, :] += jnp.sum(gy, 0, keepdims=True)
+        g_mid = norm_back(gy * g2, n2, inv)
+        r["res"][here, :] = g_mid
+        r["gf"][rows, :] = g_mid.astype(BF16)
+        pair_gf.send(i)
+    home.send()
+
+    for g in gathers:
+        g.finish()
+    for i in range(2):
+        pair_gf.recv(i)
+
+    def grad_c(j, _):
+        span = pl.ds(pl.multiple_of(j * rc, rc), rc)
+        for a in range(2):
+            r["dc"][a, span, :] = dots(r["gf"][:, span], r["act"][:, a * width : (a + 1) * width], 0, 0).astype(BF16)
+        return 0
+
+    lax.fori_loop(0, width // rc, grad_c, 0)
+    for u in uc:
+        u.start()
+
+    def back(i, _):
+        rows = pl.ds(pl.multiple_of(i * rc, rc), rc)
+        for a in range(2):
+            part = (rows, slice(a * width, (a + 1) * width))
+            r["slope"][part] = (dots(r["gf"][rows, :], gc[a], 1, 0) * r["slope"][part].astype(F32)).astype(BF16)
+        return 0
+
+    lax.fori_loop(0, 4, back, 0)
+
+    def hid_part(rows):
+        return dots(r["slope"][rows, :width], gb[0], 1, 1) + dots(r["slope"][rows, width:], gb[1], 1, 1)
+
+    for i in range(2):
+        r["send2"][i * rc : (i + 1) * rc, :] = hid_part(pl.ds(pl.multiple_of(theirs + i * rc, rc), rc)).astype(BF16)
+        pair_gh.send(i)
+    for u in uc:
+        u.second()
+
+    def grad_b(j, _):
+        span = pl.ds(pl.multiple_of(j * rc, rc), rc)
+        for a in range(2):
+            r["db"][a, span, :] = dots(r["hb"][:, span], r["slope"][:, a * width : (a + 1) * width], 0, 0).astype(BF16)
+        return 0
+
+    lax.fori_loop(0, width // rc, grad_b, 0)
+    for u in ub:
+        u.start()
+    for i in range(2):
+        rows = pl.ds(pl.multiple_of(mine + i * rc, rc), rc)
+        here = slice(i * rc, (i + 1) * rc)
+        part = hid_part(rows)
+        pair_gh.recv(i)
+        gh = r["res"][here, :] + part + r["recv2"][here, :].astype(F32)
+        n1 = r["n1"][here, :]
+        small[0:1, :] += jnp.sum(gh * n1, 0, keepdims=True)
+        small[1:2, :] += jnp.sum(gh, 0, keepdims=True)
+        g_res = norm_back(gh * g1, n1, r["inv1"][here, 0:1])
+        r["res"][here, :] = g_res
+        r["gat"][rows, :] = g_res.astype(BF16)
+        pair_ga.send(i)
+    sums.start(small[...])
+    for k in range(4):
+        rows = pl.ds(pl.multiple_of(lax.rem(2 * p.c + k, 4) * rc, rc), rc)
+        if k >= 2:
+            pair_ga.recv(k - 2)
+        gctx[:, rows] = dots(wo[...], r["gat"][rows, :], 1, 1).astype(BF16)
+
+    def grad_a(a):
+        turn = r["turn"]
+        turn[:group, :] = jnp.dot(qkv[a * group : (a + 1) * group, :], x[...], preferred_element_type=F32).astype(BF16)
+        turn[group:, :] = jnp.dot(ctx[a * cols : (a + 1) * cols, :], r["gat"][...], preferred_element_type=F32).astype(BF16)
+        ga[a] = turn[...].T
+
+    def attend_head_back(i, _):
+        q, k, v = set_head(i)
+        own_rows = pl.ds(pl.multiple_of(i * head, head), head)
+        gk = gv = None
+        for j in range(2):
+            span = slice(j * half, (j + 1) * half)
+            scores = dots(ka[...], qa[:, span], 0, 0)
+            probs = jnp.exp(scores - r["lse"][i, :, span])
+            grad = gctx[own_rows, span]
+            grad_probs = dots(qkv[v, :], grad, 0, 0)
+            inner = jnp.sum(probs * grad_probs, 0, keepdims=True)
+            grad_scores = (probs * (grad_probs - inner)).astype(BF16)
+            qkv[q, span] = (jnp.dot(ka[0:head, :], grad_scores, preferred_element_type=F32) * scale).astype(BF16)
+            dk = dots(qa[0:head, span], grad_scores, 1, 1)
+            dv = dots(grad, probs.astype(BF16), 1, 1)
+            gk, gv = (dk, dv) if gk is None else (gk + dk, gv + dv)
+        qkv[k, :] = gk.astype(BF16)
+        qkv[v, :] = gv.astype(BF16)
+
+        for k in range(3):
+
+            @pl.when(i == k)
+            def _():
+                sums.step(k)
+
+        @pl.when(i == 1)
+        def _():
+            for u in uc:
+                u.third()
+
+        @pl.when(i == 2)
+        def _():
+            grad_a(0)
+            for u in ua[:2]:
+                u.start()
+
+        @pl.when(i == 3)
+        def _():
+            for u in ub:
+                u.second()
+
+        return 0
+
+    lax.fori_loop(0, heads, attend_head_back, 0)
+
+    def tok_part(rows):
+        return dots(qkv[:group, rows], at[0, :group, :], 0, 0) + dots(qkv[group:, rows], at[1, :group, :], 0, 0)
+
+    for i in range(2):
+        r["send3"][i * rc : (i + 1) * rc, :] = tok_part(pl.ds(pl.multiple_of(theirs + i * rc, rc), rc)).astype(BF16)
+        pair_gt.send(i)
+    grad_a(1)
+    for u in ua[2:]:
+        u.start()
+    for i in range(2):
+        rows = pl.ds(pl.multiple_of(mine + i * rc, rc), rc)
+        here = slice(i * rc, (i + 1) * rc)
+        part = tok_part(rows)
+        pair_gt.recv(i)
+        r["gtokb"][here, :] = (r["res"][here, :] + part + r["recv3"][here, :].astype(F32)).astype(BF16)
+    home_g.send()
+    for u in ub:
+        u.third()
+    for u in ua[:2]:
+        u.second()
+    for u in ua[2:]:
+        u.second()
+    for u in ua[:2]:
+        u.third()
+    for u in ua[2:]:
+        u.third()
+    sums.finish()
+
+    def settle(made, land, out):
+        for i in range(2):
+            for a in range(2):
+                u = made[2 * a + i]
+
+                @pl.when(p.a == a)
+                def _():
+                    owned(p, land, i * hw, hw, u.zs, u.zr, mp)
+
+        total = land[0].astype(F32)
+        for z in range(1, mp):
+            total = total + land[z].astype(F32)
+        out[...] = total
+
+    settle(uc, r["lc"], r["rc"])
+    settle(ub, r["lb"], r["rb"])
+    settle(ua, r["la"], r["ra"])
+    home.finish()
+    home_g.finish()
+    cots_done = [tokens.finish(mp)]
+    for swap in (pair_attn, pair_hid, pair_ffn, pair_gf, pair_gh, pair_ga, pair_gt):
+        swap.finish()
+    for u in ua + ub + uc:
+        u.finish()
     for copy in vcopies + ucopies:
         copy.wait_send()
 
 
-def fetch(mp, tok, cot, pa, pb, pc, vec):
-    rows, width = pa.shape
-    seq = tok.shape[1] * mp
+def fused_layer(mp, tok, cot, pa, pb, pc, vec, pick, head, nblocks, picks):
+    n, width = pa.shape
+    quarter = tok.shape[1]
+    seq = quarter * mp
+    half = seq // 2
+    per = width // 4 // head
+    group = 3 * per * head
     shape = jax.ShapeDtypeStruct
-    gathered = shape((2, 8 * rows, width), BF16)
+    names = ["tok", "cot", "pa", "pb", "pc", "vec", "pick"]
+    outs = {
+        "hout": (shape((2, quarter, width), BF16), ANY),
+        "hgtok": (shape((2, quarter, width), BF16), ANY),
+        "ra": (shape((n, width), F32), VMEM),
+        "rb": (shape((n, width), F32), VMEM),
+        "rc": (shape((n, width), F32), VMEM),
+        "sums": (shape((8, width), F32), VMEM),
+    }
+    weight = ((2, 8 * n, width), BF16)
+    rows_b, half_b, half_f = ((seq, width), BF16), ((half, width), BF16), ((half, width), F32)
+    bufs = {
+        "x": rows_b, "ga": weight, "gb": weight, "gc": weight, "at": weight, "db": weight, "dc": weight,
+        "qkv": ((2 * group, seq), BF16), "ctx": ((2 * per * head, seq), BF16), "gctx": ((2 * per * head, seq), BF16),
+        "wo": ((2 * per * head, width), BF16), "lse": ((2 * per, 1, seq), F32), "n1": half_f, "inv1": ((half, 128), F32), "res": half_f,
+        "hb": rows_b, "act": ((seq, 2 * width), BF16), "slope": ((seq, 2 * width), BF16), "gf": rows_b, "gat": rows_b,
+        "send": half_b, "recv": half_b, "send1": half_b, "recv1": half_b, "send2": half_b, "recv2": half_b,
+        "send3": half_b, "recv3": half_b, "outb": half_b, "gtokb": half_b, "ct": half_b,
+        "gvec": ((8,) + vec.shape, BF16), "gpick": ((mp,) + pick.shape, BF16), "norms": (vec.shape, F32),
+        "bias": ((2 * per, nblocks, seq), BF16), "qa": ((head + nblocks + 16, seq), BF16), "ka": ((head + nblocks + 16, seq), BF16),
+        "small": ((8, width), F32), "turn": ((width, width), BF16),
+        "la": ((mp, n, width), BF16), "lb": ((mp, n, width), BF16), "lc": ((mp, n, width), BF16),
+        "sumbuf.0": ((3, 8, width), F32), "sumbuf.1": ((3, 8, width), F32), "sumbuf.2": ((mp, 8, width), F32),
+    }
+    for w in "abc":
+        for a in range(2):
+            for i in range(2):
+                for k in range(4):
+                    bufs[f"s{w}{a}{i}b.{k}"] = ((2 * n, width // 2), BF16)
+    scratch = {k: pltpu.VMEM(*v) for k, v in bufs.items()}
+
+    def add(key, specs):
+        for i, spec in enumerate(specs):
+            scratch[f"{key}.{i}"] = spec
+
+    add("tok", [DMA((4,)), DMA((mp,)), DMA((mp,)), DMA((mp,))])
+    for key in ("cot", "home", "homeg", *(f"sw{i}" for i in range(7))):
+        add(key, [DMA((2,)), DMA((2,))])
+    for w in "abc":
+        for i in range(2):
+            add(f"g{w}{i}", gather_sems(mp))
+        for a in range(2):
+            for i in range(2):
+                add(f"s{w}{a}{i}s", scatter_sems(mp))
+    add("vec", [DMA((7,)), DMA((8,)), DMA((mp - 1,)), DMA((mp,))])
+    add("sum", [DMA((3,)), DMA((3,)), DMA((mp - 1,)), DMA((mp,))])
+    names = names + list(outs) + list(scratch)
     return pl.pallas_call(
-        lambda *refs: fetch_kernel(mp, *refs),
-        name="fetch",
-        out_shape=[
-            shape((seq, tok.shape[2]), BF16),
-            shape((seq // 2, tok.shape[2]), BF16),
-            gathered,
-            gathered,
-            gathered,
-            shape((8,) + vec.shape, F32),
-            shape((mp,) + vec.shape, F32),
-        ],
-        in_specs=[ANY] * 6,
-        out_specs=[ANY] * 7,
-        scratch_shapes=[
-            DMA((7,)), DMA((8,)), DMA((mp - 1,)), DMA((mp,)),
-            DMA((4,)), DMA((mp,)), DMA((mp,)), DMA((mp,)),
-            DMA((2,)), DMA((2,)),
-            *gather_sems(mp), *gather_sems(mp), *gather_sems(mp),
-        ],
-        compiler_params=pltpu.CompilerParams(collective_id=0, has_side_effects=True),
-    )(tok, cot, pa, pb, pc, vec)
-
-
-def deliver_kernel(mp, da, db, dc, out, gtok, ra, rb, rc, hout, hgtok, *scr):
-    p = Place()
-    weights = []
-    for i, (s, o) in enumerate(((da, ra), (db, rb), (dc, rc))):
-        weights.append(Scatter(p, s, o, scr[4 * i : 4 * i + 4], scr[12 + 6 * i : 18 + 6 * i], mp))
-    home = Homewards(p, out, hout, scr[30:32])
-    home_g = Homewards(p, gtok, hgtok, scr[32:34])
-    greet(column_peers(p, mp) + [(p.sib, p.m), (p.xp, p.m), (p.yp, p.m)])
-    home.send()
-    home_g.send()
-    for w in weights:
-        w.first()
-    for w in weights:
-        w.second()
-        w.third()
-    for w in weights:
-        w.finish()
-    home.finish()
-    home_g.finish()
-
-
-def deliver(mp, da, db, dc, out, gtok, rows, quarter):
-    width = da.shape[2]
-    shape = jax.ShapeDtypeStruct
-    part = shape((mp, rows, width), BF16)
-    piece = shape((2, quarter, out.shape[1]), BF16)
-    return pl.pallas_call(
-        lambda *refs: deliver_kernel(mp, *refs),
-        name="deliver",
-        out_shape=[part, part, part, piece, piece],
-        in_specs=[VMEM] * 3 + [ANY] * 2,
-        out_specs=[ANY] * 5,
-        scratch_shapes=[
-            *scatter_bufs(rows, width), *scatter_bufs(rows, width), *scatter_bufs(rows, width),
-            *scatter_sems(mp), *scatter_sems(mp), *scatter_sems(mp),
-            DMA((2,)), DMA((2,)), DMA((2,)), DMA((2,)),
-        ],
-        compiler_params=pltpu.CompilerParams(collective_id=1, has_side_effects=True, vmem_limit_bytes=48 << 20),
-    )(da, db, dc, out, gtok)
+        lambda *refs: layer_kernel(mp, head, nblocks, picks, names, *refs),
+        name="layer",
+        out_shape=[o[0] for o in outs.values()],
+        in_specs=[ANY] * 5 + [VMEM] * 2,
+        out_specs=[o[1] for o in outs.values()],
+        scratch_shapes=list(scratch.values()),
+        compiler_params=pltpu.CompilerParams(collective_id=0, has_side_effects=True, vmem_limit_bytes=64 << 20),
+    )(tok, cot, pa, pb, pc, vec, pick)
 
 
 def attend_kernel(q_ref, k_ref, v_ref, bias_ref, hot_ref, ctx_ref, lse_ref, qa, ka):
@@ -596,7 +1039,7 @@
     return grad(da), grad(db), grad(dc), home(out), home(gtok)
 
 
-def layer(
+def layer_plain(
     dp, mp, tokens, cotangent, w_query, w_key, w_value, w_out, w_inner, w_outer,
     gain_attn, shift_attn, gain_ffn, shift_ffn, seq_lengths, rand_blocks,
 ):
@@ -617,11 +1060,8 @@
     vec_rows += [flat[:128], flat[128:]]
     vec = jnp.stack([jnp.pad(v, (0, 128 - v.shape[0])) for v in vec_rows] + [jnp.zeros(128, F32)])
     pa = jnp.concatenate([w_query, w_key, w_value, w_out.T], 1)
-    kernels = dp == 8 and mp == 4 and rows % 16 == 0 and pa.shape[1] % 128 == 0
-    sizes = (mp,) if kernels else (dp, mp)
-    x, ct, ga, gb, gc, gvd, gvz = (fetch if kernels else fetch_plain)(
-        *sizes, tokens, cotangent, pa, w_inner, w_outer.T, vec
-    )
+    pb, pc = w_inner, w_outer.T
+    x, ct, ga, gb, gc, gvd, gvz = fetch_plain(dp, mp, tokens, cotangent, pa, pb, pc, vec)
     norms = jnp.swapaxes(gvd[:, :4, :rows], 0, 1).reshape(4, width)
     g1, b1, g2, b2 = (norms[i][None] for i in range(4))
     owner = d - core + m // 2
@@ -697,14 +1137,43 @@
     g_attn = pair_join(g_res.astype(BF16))
     d_out = dot("td,mct->mdc", g_attn, ctx).astype(BF16)
     g_ctx = dot("td,mdc->mct", g_attn, a_out).astype(BF16)
+    sums = jnp.stack([d_gain1, d_shift1, d_gain2, d_shift2] + [jnp.zeros_like(d_gain1)] * 4)
     dq, dk, dv = attend_back(qkv, bias, hot, lse, g_ctx, head)
     dqkv = jnp.concatenate([dq, dk, dv], 1)
     d_qkv = dot("tr,mct->mrc", x, dqkv).astype(BF16)
     d_a = jnp.concatenate([d_qkv, d_out], 2)
     gtok = (g_res + pair_sum(dot("mct,mrc->tr", dqkv, a_qkv))).astype(BF16)
-    ra, rb, rc, out, gtok = (deliver if kernels else deliver_plain)(*sizes, d_a, d_b, d_c, out, gtok, rows, quarter)
+    ra, rb, rc, out, gtok = deliver_plain(dp, mp, d_a, d_b, d_c, out, gtok, rows, quarter)
+    sums = lax.psum(sums, ("dp", "mp"))
     ra, rb, rc = (jnp.sum(v.astype(F32), 0) for v in (ra, rb, rc))
-    sums = lax.psum(jnp.stack([d_gain1, d_shift1, d_gain2, d_shift2]), ("dp", "mp"))
+    sums = lax.dynamic_slice_in_dim(sums, d * rows, rows, 1)
+    return (
+        out, gtok, ra[:, :cols], ra[:, cols : 2 * cols], ra[:, 2 * cols : 3 * cols], ra[:, 3 * cols :].T, rb, rc.T,
+        sums[0], sums[1], sums[2], sums[3],
+    )
+
+
+def layer(
+    dp, mp, tokens, cotangent, w_query, w_key, w_value, w_out, w_inner, w_outer,
+    gain_attn, shift_attn, gain_ffn, shift_ffn, seq_lengths, rand_blocks,
+):
+    rows, cols = w_query.shape
+    per, nblocks, picks = rand_blocks.shape
+    if not (dp == 8 and mp == 4 and rows % 16 == 0 and 4 * cols == 8 * rows and tokens.shape[0] == 2):
+        return layer_plain(
+            dp, mp, tokens, cotangent, w_query, w_key, w_value, w_out, w_inner, w_outer,
+            gain_attn, shift_attn, gain_ffn, shift_ffn, seq_lengths, rand_blocks,
+        )
+    d = lax.axis_index("dp")
+    pa = jnp.concatenate([w_query, w_key, w_value, w_out.T], 1)
+    lens = jnp.stack([seq_lengths // 32, seq_lengths % 32], 1).reshape(-1).astype(BF16)
+    vec = jnp.stack([gain_attn, shift_attn, gain_ffn, shift_ffn, jnp.pad(lens, (0, rows - 4))])
+    vec = lax.dynamic_update_slice(jnp.zeros((16, 4 * cols), BF16), vec, (0, d * rows))
+    pick = jnp.swapaxes(rand_blocks, 1, 2).reshape(per * picks, nblocks).astype(BF16)
+    pick = jnp.pad(pick, ((0, 16 - per * picks), (0, 128 - nblocks)))
+    out, gtok, ra, rb, rc, sums = fused_layer(
+        mp, tokens, cotangent, pa, w_inner, w_outer.T, vec, pick, cols // per, nblocks, picks
+    )
     sums = lax.dynamic_slice_in_dim(sums, d * rows, rows, 1)
     return (
         out, gtok, ra[:, :cols], ra[:, cols : 2 * cols], ra[:, 2 * cols : 3 * cols], ra[:, 3 * cols :].T, rb, rc.T,

time: 390 us -> 223 us (0.57); the launches traced: 383 us -> 221 us
  blocking collectives: 48.2 us -> 0 us
  matrix products: 43.7 us -> 0 us
  other arithmetic: 27 us -> 1.59 us
  local copies, waits for them, and re-layouts: 28.5 us -> 14.5 us
  starting transfers between devices: 10.9 us -> 0 us
  Pallas kernels: 214 us -> 204 us
  waiting for transfers between devices: 7.93 us -> 0 us
    psum x1 -> x0, blocking collectives: 48.2 us -> none  [layer(): lax.psum(jnp.stack([d_gain1, d_shift1, d_gain2, d_shift2]), ('dp', 'mp'))]
    dot_general x12 -> x0, matrix products: 43.7 us -> none  [dot(): return jnp.einsum(spec, a, b, preferred_element_type=F32)]
    ppermute x7 -> x0, starting transfers between devices: 10.9 us -> none  [the longest x4 9.99 us: pair_sum(): lax.ppermute(theirs(partial).astype(BF16), 'dp', swap).astype(F32)]
    reduce_sum x9 -> x0, other arithmetic: 10.4 us -> none  [the longest x2 4.46 us: norm(): centre = z - jnp.mean(z, -1, keepdims=True)]
    pallas_call x4 -> x1, Pallas kernels: 214 us -> 204 us  [fused_layer(): pl.pallas_call(lambda *refs: layer_kernel(mp, head, nblocks, picks, names...]
    convert_element_type x8 -> x2, local copies, waits for them, and re-layouts: 9.32 us -> 0.1 us  [the longest x1 0.09 us: layer(): jnp.stack([seq_lengths // 32, seq_lengths % 32], 1).reshape(-1).astype(BF16)]
    ppermute x7 -> x0, waiting for transfers between devices: 7.93 us -> none  [the longest x3 4.04 us: pair_join(): other = lax.ppermute(values, 'dp', swap)]
    unnamed x76 -> x30, local copies, waits for them, and re-layouts: 14.5 us -> 7.33 us
  transfers between devices with their start and end apart: 7 -> 0, of which waited for: 4 -> 0; matrix products, arithmetic and copies ran while one was open for 6% -> 0% of each run, Pallas kernels for 0% -> 0%
where the time goes in v3:
time: 223 us; the launch traced here: 221 us
  Pallas kernels  204 us (91%)
  local copies, waits for them, and re-layouts  14.5 us (7%)
    pallas_call x1, Pallas kernels, fused_layer(): pl.pallas_call(lambda *refs: layer_kernel(mp, head, nblocks, picks, names...  204 us
    unnamed x30, local copies, waits for them, and re-layouts  7.33 us

profile of v3, /device:TPU:0, one launch (start us, length us, event | category | flops | bytes accessed | tf_op | source)
XLA Modules:
  0.0 221.3 jit_solution(8464305256850159356)
XLA Ops:
  0.7 0.9 copy.26
  1.6 1.6 pad_maximum_fusion.refs_2_
  3.2 0.7 copy-done.11
  3.9 0.1 copy.27
  4.0 0.1 convert_element_type.17
  4.1 0.4 copy-done.10
  4.5 0.2 copy-done.7
  4.7 0.0 copy-done.8
  4.7 0.0 copy-done.9
  4.8 0.6 broadcast_in_dim.3
  5.4 2.5 %dynamic_update_slice.3.refs_5_ = bf16[16,768]{1,0:T(8,128)(2,1)} dynamic-update-slice(bf16[16,768]{1,0:T(8,128)(2,1)} %broadcast_in_dim.3, bf16[5,96]{1,0:T(8,128)(2,1)S(1)} %stack.38, s32[]{:T(128)} %constant.33.clone.1, s32[]{:T(128)S(6)} %select_n.18) | dynamic-update-slice | bytes 1924 | tf_op jit(solution)/shard_map/dynamic_update_slice | solution.py:1171
  8.0 0.6 pad.9.refs_6_
  8.6 204.4 %layer.1 = (bf16[2,256,768]{2,1,0:T(8,128)(2,1)}, bf16[2,256,768]{2,1,0:T(8,128)(2,1)}, f32[96,768]{1,0:T(8,128)}, f32[96,768]{1,0:T(8,128)}, f32[96,768]{1,0:T(8,128)}, /*index=5*/f32[8,768]{1,0:T(8,128)}) custom-call(bf16[2,256,768]{2,1,0:T(8,128)(2,1)} %refs_0_.1, bf16[2,256,768]{2,1,0:T(8,128)(2,1)} %refs_1_.1, bf16[96,768]{1,0:T(8,128)(2,1)} %pad_maximum_fusion.refs_2_, ...), custom_call_target="tpu_custom_call" | custom-call | tf_op jit(solution)/shard_map/layer/pallas_call | solution.py:879
  213.0 1.9 slice_bitcast_fusion
  215.0 0.7 copy.28
  215.7 0.8 constant_dynamic-slice_fusion
  216.5 0.5 slice_bitcast_fusion.1
  217.0 0.9 copy.34
  217.9 0.5 copy-done
  218.4 0.9 copy.35
  219.3 0.2 copy-done.3
  219.5 0.7 copy.36
  220.3 0.4 copy-done.2
  220.6 0.7 copy.37
  (22 shorter events, 0.1 us)
Async XLA Ops:
  0.6 0.9 copy-start.4
  0.7 0.9 copy-start.5
  3.2 0.7 copy-start.11
  3.8 0.7 copy-start.10
  4.1 0.7 copy-start.7
  4.1 0.7 copy-start.8
  4.1 0.7 copy-start.9
  4.8 3.2 %copy-start.6 = (s32[3,16,3]{1,2,0:T(4,128)S(1)}, s32[3,16,3]{1,2,0:T(4,128)}, u32[]{:S(2)}) copy-start(s32[3,16,3]{1,2,0:T(4,128)} %param.27) | copy-start | bytes 1732
  213.0 4.0 %copy-start.1 = (bf16[2,256,768]{2,1,0:T(8,128)(2,1)S(1)}, bf16[2,256,768]{2,1,0:T(8,128)(2,1)}, u32[]{:S(2)}) copy-start(bf16[2,256,768]{2,1,0:T(8,128)(2,1)} %get-tuple-element.58) | copy-start | bytes 2359300
  217.0 1.4 copy-start
  218.4 1.1 copy-start.3
  219.5 1.1 copy-start.2

commit v4 on v3

--- a/solution.py
+++ b/solution.py
@@ -33,6 +33,9 @@
         self.bd = self.bx + 4 - 8 * by
         self.h = lax.div(self.m, 2)
         self.a = lax.rem(self.m, 2)
+        self.close = self.h == self.c
+        self.inner = jnp.logical_and(self.h != self.c, self.a + self.h == 1)
+        self.outer = jnp.logical_and(self.h != self.c, self.a + self.h != 1)
 
 
 def remote(src, dst, ssem, rsem, dev):
@@ -81,85 +84,92 @@
 
 
 class Gather:
-    def __init__(self, p, src, dst, first, count, sems, mp):
-        self.p, self.src, self.dst, self.mp = p, src, dst, mp
-        self.zs, self.zr, self.xs, self.xr, self.ys, self.yr = sems
+    def __init__(self, p, src, dst, first, count, sems):
+        self.p, self.src, self.dst = p, src, dst
+        self.zs, self.zr, self.fs, self.fr, self.xs, self.xr, self.ys, self.yr = sems
         self.n = src.shape[0]
         self.cols = pl.ds(first, count)
 
     def rows(self, a, first, count):
         return self.dst.at[a, pl.ds(first * self.n, count * self.n), self.cols]
 
+    def both(self, first):
+        return self.dst.at[:, pl.ds(first * self.n, 2 * self.n), self.cols]
+
     def z_args(self, k):
         p = self.p
-        z = lax.rem(p.m + k, self.mp)
-        same = (p.h == p.c) if k == 0 else None
+        z = (p.m, p.m + 1 - 2 * p.a, 2 - p.h)[k]
         src = self.src.at[:, self.cols]
-        return (src, self.rows(p.a, p.d, 1), self.zs.at[k], self.zr.at[2 * p.c + p.a], (p.base + p.h, z)), same
+        return src, self.rows(p.a, p.d, 1), self.zs.at[k], self.zr.at[2 * p.c + p.a], (p.base + p.h, z)
 
     def z_send(self):
-        for k in (2, 1, 3, 0):
-            args, same = self.z_args(k)
-            if same is None:
-                remote(*args).start()
-            else:
-                push(*args, same)
-
-    def z_recv(self):
-        p = self.p
-        for core in range(2):
-            for a in range(2):
-                got(self.rows(a, p.base + core, 1), self.zs.at[0], self.zr.at[2 * core + a], (p.d, p.m))
-
-    def hop(self, axis, step, a):
+        for k in (2, 1):
+            remote(*self.z_args(k)).start()
+        push(*self.z_args(0), self.p.close)
+
+    def pass_on(self):
+        p = self.p
+        part = self.both(p.base)
+        return remote(part, part, self.fs.at[0], self.fr.at[0], (p.d, 3 * p.h))
+
+    def z_mid(self):
+        p = self.p
+
+        @pl.when(jnp.logical_not(p.outer))
+        def _():
+            for core in range(2):
+                for a in range(2):
+                    got(self.rows(a, p.base + core, 1), self.zs.at[0], self.zr.at[2 * core + a], (p.d, p.m))
+
+        @pl.when(p.inner)
+        def _():
+            self.pass_on().start()
+
+        @pl.when(p.outer)
+        def _():
+            self.pass_on().wait_recv()
+
+        self.hop(0, 0).start()
+        self.hop(1, 0).start()
+
+    def hop(self, axis, step):
         p = self.p
         peer = p.xp if axis == 0 else p.yp
-        first = p.base if step == 0 else (p.by if axis == 0 else p.bx)
-        part = self.rows(a, first, 2)
         s, r = (self.xs, self.xr) if axis == 0 else (self.ys, self.yr)
-        i = 2 if step else a
-        return remote(part, part, s.at[i], r.at[i], (peer, p.m))
-
-    def xy_send(self):
-        for a in range(2):
-            self.hop(0, 0, a).start()
-            self.hop(1, 0, 1 - a).start()
-
-    def arrived(self, axis, step, a):
-        p = self.p
-        first = (p.bx if axis == 0 else p.by) if step == 0 else p.bd
+        part = self.both(p.base) if step == 0 else self.rows(1 - axis, p.by if axis == 0 else p.bx, 2)
+        return remote(part, part, s.at[step], r.at[step], (peer, p.m))
+
+    def arrived(self, axis, step):
+        p = self.p
         s, r = (self.xs, self.xr) if axis == 0 else (self.ys, self.yr)
-        i = 2 if step else a
-        got(self.rows(a, first, 2), s.at[i], r.at[i], (p.d, p.m))
+        part = self.both(p.bx if axis == 0 else p.by) if step == 0 else self.rows(1 - axis, p.bd, 2)
+        got(part, s.at[step], r.at[step], (p.d, p.m))
 
     def forward(self):
-        self.arrived(0, 0, 0)
-        self.hop(1, 1, 0).start()
-        self.arrived(1, 0, 1)
-        self.hop(0, 1, 1).start()
+        for axis in range(2):
+            self.arrived(axis, 0)
+            self.hop(1 - axis, 1).start()
 
     def land(self):
-        self.arrived(0, 0, 1)
-        self.arrived(1, 0, 0)
-        self.arrived(1, 1, 0)
-        self.arrived(0, 1, 1)
+        self.arrived(1, 1)
+        self.arrived(0, 1)
 
     def finish(self):
-        for k in range(self.mp):
-            args, same = self.z_args(k)
-            if same is None:
-                remote(*args).wait_send()
-            else:
-                pushed(*args, same)
-        for a in range(2):
-            self.hop(0, 0, a).wait_send()
-            self.hop(1, 0, a).wait_send()
-        self.hop(1, 1, 0).wait_send()
-        self.hop(0, 1, 1).wait_send()
-
-
-def gather_sems(mp):
-    return [DMA((mp,)), DMA((4,)), DMA((3,)), DMA((3,)), DMA((3,)), DMA((3,))]
+        for k in (1, 2):
+            remote(*self.z_args(k)).wait_send()
+        pushed(*self.z_args(0), self.p.close)
+
+        @pl.when(self.p.inner)
+        def _():
+            self.pass_on().wait_send()
+
+        for axis in range(2):
+            for step in range(2):
+                self.hop(axis, step).wait_send()
+
+
+def gather_sems():
+    return [DMA((3,)), DMA((4,)), DMA((1,)), DMA((1,)), DMA((2,)), DMA((2,)), DMA((2,)), DMA((2,))]
 
 
 class Tokens:
@@ -246,10 +256,9 @@
         same = jnp.logical_and(owner == p.d, p.m == 2 * p.c + q)
         return (src, self.dst.at[p.a], self.s.at[q], self.r.at[p.a], (owner, 2 * p.c + q)), same
 
-    def send(self):
-        for q in range(2):
-            args, same = self.args(q)
-            push(*args, same)
+    def send(self, q):
+        args, same = self.args(q)
+        push(*args, same)
 
     def finish(self):
         p = self.p
@@ -261,16 +270,17 @@
 
 
 class Scatter:
-    def __init__(self, p, src, out, a, first, count, axis, bufs, sems, mp):
-        self.p, self.src, self.out, self.a, self.axis, self.mp = p, src, out, a, axis, mp
-        self.r1, self.r2, self.r3, self.total = bufs
+    def __init__(self, p, src, out, halves, first, count, axis, bufs, sems):
+        self.p, self.src, self.out, self.halves = p, src, out, halves
+        self.r1, self.r2, self.r3, self.total, self.met = bufs
         self.s, self.r, self.zs, self.zr = sems
         self.n = out.shape[1]
+        self.first, self.count = first, count
         self.cols = pl.ds(first, count)
         self.near, self.far = ((p.xp, p.bx), (p.yp, p.by)) if axis == 0 else ((p.yp, p.by), (p.xp, p.bx))
 
     def rows(self, first):
-        return self.src.at[self.a, pl.ds(first * self.n, 2 * self.n), self.cols]
+        return self.src.at[pl.ds(self.halves[0], len(self.halves)), pl.ds(first * self.n, 2 * self.n), self.cols]
 
     def hop(self, kind):
         p = self.p
@@ -282,43 +292,80 @@
             src, dst, peer = self.r1, self.r3, self.far[0]
         return remote(src, dst, self.s.at[kind], self.r.at[kind], (peer, p.m))
 
-    def start(self):
-        self.hop(0).start()
-        self.hop(1).start()
-
     def second(self):
         self.hop(0).wait_recv()
         self.r1[...] = (self.rows(self.far[1])[...].astype(F32) + self.r1[...].astype(F32)).astype(BF16)
         self.hop(2).start()
 
     def third(self):
+        p = self.p
         self.hop(1).wait_recv()
         self.hop(2).wait_recv()
         self.total[...] = (
-            self.rows(self.p.base)[...].astype(F32) + self.r2[...].astype(F32) + self.r3[...].astype(F32)
+            self.rows(p.base)[...].astype(F32) + self.r2[...].astype(F32) + self.r3[...].astype(F32)
         ).astype(BF16)
-        for core in range(2):
-            args, same = self.z_args(core)
-            push(*args, same)
-
-    def z_args(self, core):
-        p = self.p
-        owner = (p.base + core, 2 * p.c + self.a)
-        same = jnp.logical_and(p.c == core, p.m == 2 * p.c + self.a)
-        src = self.total.at[pl.ds(core * self.n, self.n), :]
-        return (src, self.out.at[p.m, :, self.cols], self.zs.at[core], self.zr.at[p.m], owner), same
+
+        @pl.when(p.close)
+        def _():
+            for args in self.z_args():
+                push(*args)
+
+        @pl.when(p.outer)
+        def _():
+            self.meet().start()
+
+    def meet(self):
+        p = self.p
+        return remote(self.total, self.met, self.zs.at[0], self.zr.at[3], (p.d, 1 + p.h))
+
+    def z_args(self):
+        p = self.p
+        slot = jnp.where(p.close, p.a, 2)
+        made = []
+        for i, a in enumerate(self.halves):
+            for core in range(2):
+                same = jnp.logical_and(p.c == core, p.m == 2 * p.c + a)
+                src = self.total.at[i, pl.ds(core * self.n, self.n), :]
+                dst = self.out.at[slot, :, self.cols]
+                made.append((src, dst, self.zs.at[2 * i + core], self.zr.at[slot], (p.base + core, 2 * p.c + a), same))
+        return made
+
+    def line(self):
+        @pl.when(self.p.inner)
+        def _():
+            self.meet().wait_recv()
+            self.total[...] = (self.total[...].astype(F32) + self.met[...].astype(F32)).astype(BF16)
+            for args in self.z_args():
+                remote(*args[:-1]).start()
+
+    def owned(self):
+        for slot in range(3):
+            got(self.out.at[slot, :, self.cols], self.zs.at[0], self.zr.at[slot], (self.p.d, self.p.m))
 
     def finish(self):
+        p = self.p
         for kind in range(3):
             self.hop(kind).wait_send()
-        for core in range(2):
-            args, same = self.z_args(core)
-            pushed(*args, same)
-
-
-def owned(p, out, first, count, zs, zr, mp):
-    for z in range(mp):
-        got(out.at[z, :, pl.ds(first, count)], zs.at[0], zr.at[z], (p.d, p.m))
+
+        @pl.when(p.outer)
+        def _():
+            self.meet().wait_send()
+
+        @pl.when(p.close)
+        def _():
+            for args in self.z_args():
+                pushed(*args)
+
+        @pl.when(p.inner)
+        def _():
+            for args in self.z_args():
+                remote(*args[:-1]).wait_send()
+
+
+def start_all(units):
+    for kind in range(2):
+        for u in units:
+            u.hop(kind).start()
 
 
 class Sums:
@@ -409,10 +456,6 @@
     centre = z - jnp.mean(z, -1, keepdims=True)
     inv = lax.rsqrt(jnp.mean(centre * centre, -1, keepdims=True) + EPS)
     return centre * inv, inv
-
-
-def scatter_sems(mp):
-    return [DMA((3,)), DMA((3,)), DMA((2,)), DMA((mp,))]
 
 
 def layer_kernel(mp, head, nblocks, picks, names, *refs):
@@ -437,10 +480,12 @@
 
     tokens = Tokens(p, r["tok"], x, sems("tok"))
     cots = Quarters(p, r["cot"], r["ct"], sems("cot"))
-    gathers = [
-        Gather(p, r["p" + w], r["g" + w], i * hw, hw, sems(f"g{w}{i}"), mp) for w in "abc" for i in range(2)
-    ]
-    a0, a1, b0, b1, c0, c1 = gathers
+    each = 4 * head
+    ga_parts = [Gather(p, r["pa"], ga, i * each, each, sems(f"ga{i}")) for i in range(per)]
+    b0, b1, c0, c1 = (
+        Gather(p, r["p" + w], r["g" + w], i * hw, hw, sems(f"g{w}{i}")) for w in "bc" for i in range(2)
+    )
+    gathers = ga_parts + [b0, b1, c0, c1]
     plane = [lax.rem(p.d + k, 8) for k in range(1, 8)]
     vec, pick, gvec, gpick = r["vec"], r["pick"], r["gvec"], r["gpick"]
     vs, vr, us, ur = sems("vec")
@@ -451,45 +496,41 @@
     pair_hid = Swap(p, r["hb"], r["hb"], sems("sw1"), mine, mine, theirs, rc)
     pair_ffn = Swap(p, r["send1"], r["recv1"], sems("sw2"), count=rc)
     pair_gf = Swap(p, r["gf"], r["gf"], sems("sw3"), mine, mine, theirs, rc)
-    pair_gh = Swap(p, r["send2"], r["recv2"], sems("sw4"), count=rc)
+    pair_gh = Swap(p, r["send"], r["recv"], sems("sw4"), count=rc)
     pair_ga = Swap(p, r["gat"], r["gat"], sems("sw5"), mine, mine, theirs, rc)
-    pair_gt = Swap(p, r["send3"], r["recv3"], sems("sw6"), count=rc)
-
-    def units(name, src, out):
-        made = []
-        for a in range(2):
-            for i in range(2):
-                made.append(Scatter(p, src, out, a, i * hw, hw, i, sems(f"s{name}{a}{i}b"), sems(f"s{name}{a}{i}s"), mp))
-        return made
-
-    ua, ub, uc = units("a", ga, r["la"]), units("b", r["db"], r["lb"]), units("c", r["dc"], r["lc"])
+    pair_gt = Swap(p, r["send1"], r["recv1"], sems("sw6"), count=rc)
+
+    def unit(name, src, halves, first, count, axis):
+        return Scatter(p, src, r["l" + name[0]], halves, first, count, axis, sems(f"s{name}b"), sems(f"s{name}s"))
+
+    ua = [unit(f"a{i}", ga, (i % 2,), (i // 2) * each, each, i % 2) for i in range(heads)]
+    ub, uc = ([unit(f"{w}{i}", r["d" + w], (0, 1), i * hw, hw, i) for i in range(2)] for w in "bc")
 
     greet(column_peers(p, mp) + [(d, p.m) for d in plane])
-    a0.z_send()
-    a1.z_send()
-    tokens.send()
+    pcopies = [remote(pick, gpick.at[p.m], us.at[k - 1], ur.at[p.m], (p.d, lax.rem(p.m + k, mp))) for k in range(1, mp)]
+    pcopies.append(remote(pick, gpick.at[mp], us.at[mp - 1], ur.at[mp], (p.sib, p.m)))
+    mine_too = pltpu.make_async_copy(pick, gpick.at[p.m], ur.at[p.m])
+    for copy in pcopies + [mine_too]:
+        copy.start()
+    for g in ga_parts:
+        g.z_send()
+    b0.z_send()
+    pl.when(jnp.logical_not(p.inner))(tokens.send)
     vcopies = [remote(vec, gvec.at[p.d], vs.at[k], vr.at[p.d], (d, p.m)) for k, d in enumerate(plane)]
-    ucopies = [remote(pick, gpick.at[p.m], us.at[k - 1], ur.at[p.m], (p.d, lax.rem(p.m + k, mp))) for k in range(1, mp)]
-    own = [pltpu.make_async_copy(vec, gvec.at[p.d], vr.at[p.d]), pltpu.make_async_copy(pick, gpick.at[p.m], ur.at[p.m])]
-    for copy in vcopies + ucopies + own:
+    vcopies.append(pltpu.make_async_copy(vec, gvec.at[p.d], vr.at[p.d]))
+    for g in ga_parts:
+        g.z_mid()
+    b0.z_mid()
+    pl.when(p.inner)(tokens.send)
+    for copy in vcopies:
         copy.start()
-    a0.z_recv()
-    a0.xy_send()
-    a1.z_recv()
-    a1.xy_send()
-
-    for d in range(8):
-        got(gvec.at[d], vs.at[0], vr.at[d], (p.d, p.m))
-    for z in range(mp):
+
+    for z in range(mp + 1):
         got(gpick.at[z], us.at[0], ur.at[z], (p.d, p.m))
-    vecs = gvec[0].astype(F32)
-    for d in range(1, 8):
-        vecs = vecs + gvec[d].astype(F32)
-    r["norms"][...] = vecs
-    lane = lax.broadcasted_iota(jnp.int32, (1, width), 1)
-    spot = (p.base + p.h) * n + 2 * p.a
-    row = vecs[4:5]
-    length = jnp.sum(jnp.where(lane == spot, row * 32.0, 0.0) + jnp.where(lane == spot + 1, row, 0.0), 1, keepdims=True)
+    row = jnp.where(p.close, gpick[p.m, 15:16, :].astype(F32), gpick[mp, 15:16, :].astype(F32))
+    lane = lax.broadcasted_iota(jnp.int32, (1, 128), 1)
+    high, low = (jnp.sum(jnp.where(lane == 2 * p.a + i, row, 0.0), 1, keepdims=True) for i in range(2))
+    length = high * 32.0 + low
     block = seq // nblocks
     sub = lax.broadcasted_iota(jnp.int32, (nblocks, seq), 0)
     place = lax.broadcasted_iota(jnp.int32, (nblocks, seq), 1)
@@ -505,7 +546,7 @@
             for j in range(picks):
                 at_row = h * picks + j
                 hit = hit | (wide[at_row : at_row + 1] == subf)
-            r["bias"][a * per + h] = jnp.where(hit, 0.0, NEG).astype(BF16)
+            r["bias"][2 * h + a] = jnp.where(hit, 0.0, NEG).astype(BF16)
     qa, ka = r["qa"], r["ka"]
     low = lax.broadcasted_iota(jnp.int32, (16, seq), 0)
     ka[head : head + nblocks, :] = jnp.where(rb == sub, 1.0, 0.0).astype(BF16)
@@ -513,29 +554,30 @@
     ka[head + nblocks :, :] = jnp.where((low == 0) & beyond, 1.0, 0.0).astype(BF16)
     qa[head + nblocks :, :] = jnp.where(low == 0, NEG, 0.0).astype(BF16)
 
-    a0.forward()
-    a1.forward()
+    for g in ga_parts:
+        g.forward()
     tokens.forward(mp)
-    b0.z_send()
     b1.z_send()
-    a0.land()
-    a1.land()
-    for a in range(2):
-        at[a] = ga[a].T
+    c0.z_send()
     tokens.land(mp)
 
-    def project(i, _):
-        rows = pl.ds(pl.multiple_of(i * rc, rc), rc)
+    def project(h):
+        span = pl.ds(pl.multiple_of(h * each, each), each)
         for a in range(2):
-            qkv[a * group : (a + 1) * group, rows] = dots(at[a, :group, :], x[rows, :], 1, 1).astype(BF16)
-        return 0
-
-    lax.fori_loop(0, seq // rc, project, 0)
+            at[a, span, :] = ga[a, :, span].T
+        own_rows = pl.ds(pl.multiple_of(h * each, each), 3 * head)
+
+        def some(j, _):
+            rows = pl.ds(pl.multiple_of(j * rc, rc), rc)
+            for a in range(2):
+                to = pl.ds(pl.multiple_of((2 * h + a) * 3 * head, head), 3 * head)
+                qkv[to, rows] = dots(at[a, own_rows, :], x[rows, :], 1, 1).astype(BF16)
+            return 0
+
+        lax.fori_loop(0, seq // rc, some, 0)
 
     def parts(i):
-        a = lax.div(i, per)
-        first = a * group + (i - a * per) * head
-        return [pl.ds(pl.multiple_of(first + part * cols, head), head) for part in range(3)]
+        return [pl.ds(pl.multiple_of((3 * i + part) * head, head), head) for part in range(3)]
 
     def set_head(i):
         q, k, v = parts(i)
@@ -545,6 +587,16 @@
         return q, k, v
 
     def attend_head(i, _):
+        for h in range(per):
+
+            @pl.when(i == 2 * h)
+            def _():
+                ga_parts[h].land()
+
+        @pl.when(lax.rem(i, 2) == 0)
+        def _():
+            project(lax.div(i, 2))
+
         q, k, v = set_head(i)
         own_rows = pl.ds(pl.multiple_of(i * head, head), head)
         for j in range(2):
@@ -557,24 +609,36 @@
             ctx[own_rows, span] = (mixed / total).astype(BF16)
             r["lse"][i, :, span] = peak + jnp.log(total)
 
-        @pl.when(i == 2)
-        def _():
-            b0.z_recv()
-            b0.xy_send()
-            b1.z_recv()
-            b1.xy_send()
-            c0.z_send()
+        @pl.when(i == 0)
+        def _():
+            b1.z_mid()
             c1.z_send()
+            b0.forward()
+
+        @pl.when(i == 3)
+        def _():
+            c0.z_mid()
+
+        @pl.when(i == 5)
+        def _():
+            b1.forward()
+            c1.z_mid()
+            cots.send()
 
         return 0
 
     lax.fori_loop(0, heads, attend_head, 0)
-    b0.forward()
 
     wo = r["wo"]
-    for a in range(2):
-        wo[a * cols : (a + 1) * cols, :] = at[a, group:, :]
+    for i in range(heads):
+        wo[i * head : (i + 1) * head, :] = at[i % 2, (i // 2) * each + 3 * head : (i // 2 + 1) * each, :]
     norms = r["norms"]
+    for d in range(8):
+        got(gvec.at[d], vs.at[0], vr.at[d], (p.d, p.m))
+    vecs = gvec[0].astype(F32)
+    for d in range(1, 8):
+        vecs = vecs + gvec[d].astype(F32)
+    norms[...] = vecs
     g1, s1, g2, s2 = (norms[i : i + 1] for i in range(4))
 
     def attn_part(first):
@@ -583,7 +647,7 @@
     for i in range(2):
         r["send"][i * rc : (i + 1) * rc, :] = attn_part(pl.multiple_of(theirs + i * rc, rc)).astype(BF16)
         pair_attn.send(i)
-    b1.forward()
+    c0.forward()
     for i in range(2):
         rows = pl.ds(pl.multiple_of(mine + i * rc, rc), rc)
         here = slice(i * rc, (i + 1) * rc)
@@ -597,11 +661,6 @@
         r["hb"][rows, :] = hidden.astype(BF16)
         pair_hid.send(i)
 
-    c0.z_recv()
-    c0.xy_send()
-    c1.z_recv()
-    c1.xy_send()
-    cots.send()
     b0.land()
     b1.land()
 
@@ -620,7 +679,6 @@
         return 0
 
     lax.fori_loop(0, 4, up, 0)
-    c0.forward()
     c1.forward()
     c0.land()
     c1.land()
@@ -650,22 +708,28 @@
         r["res"][here, :] = g_mid
         r["gf"][rows, :] = g_mid.astype(BF16)
         pair_gf.send(i)
-    home.send()
+        home.send(i)
 
     for g in gathers:
         g.finish()
+    for swap in (pair_attn, pair_hid, pair_ffn, pair_gf):
+        swap.finish()
     for i in range(2):
         pair_gf.recv(i)
 
-    def grad_c(j, _):
-        span = pl.ds(pl.multiple_of(j * rc, rc), rc)
-        for a in range(2):
-            r["dc"][a, span, :] = dots(r["gf"][:, span], r["act"][:, a * width : (a + 1) * width], 0, 0).astype(BF16)
-        return 0
-
-    lax.fori_loop(0, width // rc, grad_c, 0)
-    for u in uc:
-        u.start()
+    for k in range(2):
+
+        def grad_c(j, _):
+            span = pl.ds(pl.multiple_of(j * rc, rc), rc)
+            for a in range(2):
+                first = a * width + k * hw
+                r["dc"][a, span, k * hw : (k + 1) * hw] = dots(
+                    r["gf"][:, span], r["act"][:, first : first + hw], 0, 0
+                ).astype(BF16)
+            return 0
+
+        lax.fori_loop(0, width // rc, grad_c, 0)
+        start_all([uc[k]])
 
     def back(i, _):
         rows = pl.ds(pl.multiple_of(i * rc, rc), rc)
@@ -680,7 +744,7 @@
         return dots(r["slope"][rows, :width], gb[0], 1, 1) + dots(r["slope"][rows, width:], gb[1], 1, 1)
 
     for i in range(2):
-        r["send2"][i * rc : (i + 1) * rc, :] = hid_part(pl.ds(pl.multiple_of(theirs + i * rc, rc), rc)).astype(BF16)
+        r["send"][i * rc : (i + 1) * rc, :] = hid_part(pl.ds(pl.multiple_of(theirs + i * rc, rc), rc)).astype(BF16)
         pair_gh.send(i)
     for u in uc:
         u.second()
@@ -692,14 +756,13 @@
         return 0
 
     lax.fori_loop(0, width // rc, grad_b, 0)
-    for u in ub:
-        u.start()
+    start_all(ub)
     for i in range(2):
         rows = pl.ds(pl.multiple_of(mine + i * rc, rc), rc)
         here = slice(i * rc, (i + 1) * rc)
         part = hid_part(rows)
         pair_gh.recv(i)
-        gh = r["res"][here, :] + part + r["recv2"][here, :].astype(F32)
+        gh = r["res"][here, :] + part + r["recv"][here, :].astype(F32)
         n1 = r["n1"][here, :]
         small[0:1, :] += jnp.sum(gh * n1, 0, keepdims=True)
         small[1:2, :] += jnp.sum(gh, 0, keepdims=True)
@@ -714,11 +777,13 @@
             pair_ga.recv(k - 2)
         gctx[:, rows] = dots(wo[...], r["gat"][rows, :], 1, 1).astype(BF16)
 
-    def grad_a(a):
+    def grad_a(i):
         turn = r["turn"]
-        turn[:group, :] = jnp.dot(qkv[a * group : (a + 1) * group, :], x[...], preferred_element_type=F32).astype(BF16)
-        turn[group:, :] = jnp.dot(ctx[a * cols : (a + 1) * cols, :], r["gat"][...], preferred_element_type=F32).astype(BF16)
-        ga[a] = turn[...].T
+        rows = pl.ds(pl.multiple_of(i * 3 * head, head), 3 * head)
+        turn[: 3 * head, :] = jnp.dot(qkv[rows, :], x[...], preferred_element_type=F32).astype(BF16)
+        rows = pl.ds(pl.multiple_of(i * head, head), head)
+        turn[3 * head :, :] = jnp.dot(ctx[rows, :], r["gat"][...], preferred_element_type=F32).astype(BF16)
+        ga[lax.rem(i, 2), :, pl.ds(pl.multiple_of(lax.div(i, 2) * each, each), each)] = turn[...].T
 
     def attend_head_back(i, _):
         q, k, v = set_head(i)
@@ -739,71 +804,79 @@
         qkv[k, :] = gk.astype(BF16)
         qkv[v, :] = gv.astype(BF16)
 
-        for k in range(3):
+        grad_a(i)
+        for k in range(heads):
 
             @pl.when(i == k)
             def _():
-                sums.step(k)
-
-        @pl.when(i == 1)
-        def _():
-            for u in uc:
-                u.third()
-
-        @pl.when(i == 2)
-        def _():
-            grad_a(0)
-            for u in ua[:2]:
-                u.start()
-
-        @pl.when(i == 3)
-        def _():
-            for u in ub:
-                u.second()
+                if k == 1:
+                    for u in uc:
+                        u.third()
+                if k == 3:
+                    for u in ub:
+                        u.second()
+                    for u in uc:
+                        u.line()
+                start_all([ua[k]])
+                if k == 4:
+                    ua[0].second()
+                    ua[1].second()
+                if k == 5:
+                    for u in ub:
+                        u.third()
+                if k in (2, 4):
+                    sums.step(k // 2 - 1)
 
         return 0
 
     lax.fori_loop(0, heads, attend_head_back, 0)
 
     def tok_part(rows):
-        return dots(qkv[:group, rows], at[0, :group, :], 0, 0) + dots(qkv[group:, rows], at[1, :group, :], 0, 0)
+        total = None
+        for i in range(heads):
+            mine_rows = slice(i * 3 * head, (i + 1) * 3 * head)
+            first = (i // 2) * each
+            part = dots(qkv[mine_rows, rows], at[i % 2, first : first + 3 * head, :], 0, 0)
+            total = part if total is None else total + part
+        return total
 
     for i in range(2):
-        r["send3"][i * rc : (i + 1) * rc, :] = tok_part(pl.ds(pl.multiple_of(theirs + i * rc, rc), rc)).astype(BF16)
+        r["send1"][i * rc : (i + 1) * rc, :] = tok_part(pl.ds(pl.multiple_of(theirs + i * rc, rc), rc)).astype(BF16)
         pair_gt.send(i)
-    grad_a(1)
-    for u in ua[2:]:
-        u.start()
+    for u in ua[2:4]:
+        u.second()
     for i in range(2):
         rows = pl.ds(pl.multiple_of(mine + i * rc, rc), rc)
         here = slice(i * rc, (i + 1) * rc)
         part = tok_part(rows)
         pair_gt.recv(i)
-        r["gtokb"][here, :] = (r["res"][here, :] + part + r["recv3"][here, :].astype(F32)).astype(BF16)
-    home_g.send()
+        r["gtokb"][here, :] = (r["res"][here, :] + part + r["recv1"][here, :].astype(F32)).astype(BF16)
+        home_g.send(i)
     for u in ub:
+        u.line()
+    for u in ua[:2]:
+        u.third()
+    for u in ua[4:]:
+        u.second()
+    sums.step(2)
+    for u in ua[2:4]:
         u.third()
     for u in ua[:2]:
-        u.second()
-    for u in ua[2:]:
-        u.second()
-    for u in ua[:2]:
+        u.line()
+    for u in ua[4:]:
         u.third()
     for u in ua[2:]:
-        u.third()
+        u.line()
     sums.finish()
 
     def settle(made, land, out):
-        for i in range(2):
-            for a in range(2):
-                u = made[2 * a + i]
-
-                @pl.when(p.a == a)
-                def _():
-                    owned(p, land, i * hw, hw, u.zs, u.zr, mp)
-
+        for u in made:
+            if len(u.halves) == 2:
+                u.owned()
+            else:
+                pl.when(p.a == u.halves[0])(u.owned)
         total = land[0].astype(F32)
-        for z in range(1, mp):
+        for z in range(1, 3):
             total = total + land[z].astype(F32)
         out[...] = total
 
@@ -812,12 +885,12 @@
     settle(ua, r["la"], r["ra"])
     home.finish()
     home_g.finish()
-    cots_done = [tokens.finish(mp)]
-    for swap in (pair_attn, pair_hid, pair_ffn, pair_gf, pair_gh, pair_ga, pair_gt):
+    tokens.finish(mp)
+    for swap in (pair_gh, pair_ga, pair_gt):
         swap.finish()
     for u in ua + ub + uc:
         u.finish()
-    for copy in vcopies + ucopies:
+    for copy in vcopies[:-1] + pcopies:
         copy.wait_send()
 
 
@@ -845,19 +918,18 @@
         "qkv": ((2 * group, seq), BF16), "ctx": ((2 * per * head, seq), BF16), "gctx": ((2 * per * head, seq), BF16),
         "wo": ((2 * per * head, width), BF16), "lse": ((2 * per, 1, seq), F32), "n1": half_f, "inv1": ((half, 128), F32), "res": half_f,
         "hb": rows_b, "act": ((seq, 2 * width), BF16), "slope": ((seq, 2 * width), BF16), "gf": rows_b, "gat": rows_b,
-        "send": half_b, "recv": half_b, "send1": half_b, "recv1": half_b, "send2": half_b, "recv2": half_b,
-        "send3": half_b, "recv3": half_b, "outb": half_b, "gtokb": half_b, "ct": half_b,
-        "gvec": ((8,) + vec.shape, BF16), "gpick": ((mp,) + pick.shape, BF16), "norms": (vec.shape, F32),
+        "send": half_b, "recv": half_b, "send1": half_b, "recv1": half_b, "outb": half_b, "gtokb": half_b, "ct": half_b,
+        "gvec": ((8,) + vec.shape, BF16), "gpick": ((mp + 1,) + pick.shape, BF16), "norms": (vec.shape, F32),
         "bias": ((2 * per, nblocks, seq), BF16), "qa": ((head + nblocks + 16, seq), BF16), "ka": ((head + nblocks + 16, seq), BF16),
-        "small": ((8, width), F32), "turn": ((width, width), BF16),
-        "la": ((mp, n, width), BF16), "lb": ((mp, n, width), BF16), "lc": ((mp, n, width), BF16),
+        "small": ((8, width), F32), "turn": ((4 * head, width), BF16),
+        "la": ((3, n, width), BF16), "lb": ((3, n, width), BF16), "lc": ((3, n, width), BF16),
         "sumbuf.0": ((3, 8, width), F32), "sumbuf.1": ((3, 8, width), F32), "sumbuf.2": ((mp, 8, width), F32),
     }
-    for w in "abc":
-        for a in range(2):
-            for i in range(2):
-                for k in range(4):
-                    bufs[f"s{w}{a}{i}b.{k}"] = ((2 * n, width // 2), BF16)
+    pieces = {"a": (4 * head, 2 * per, 1), "b": (width // 2, 2, 2), "c": (width // 2, 2, 2)}
+    for w, (count, many, halves) in pieces.items():
+        for i in range(many):
+            for k in range(5):
+                bufs[f"s{w}{i}b.{k}"] = ((halves, 2 * n, count), BF16)
     scratch = {k: pltpu.VMEM(*v) for k, v in bufs.items()}
 
     def add(key, specs):
@@ -867,13 +939,12 @@
     add("tok", [DMA((4,)), DMA((mp,)), DMA((mp,)), DMA((mp,))])
     for key in ("cot", "home", "homeg", *(f"sw{i}" for i in range(7))):
         add(key, [DMA((2,)), DMA((2,))])
-    for w in "abc":
-        for i in range(2):
-            add(f"g{w}{i}", gather_sems(mp))
-        for a in range(2):
-            for i in range(2):
-                add(f"s{w}{a}{i}s", scatter_sems(mp))
-    add("vec", [DMA((7,)), DMA((8,)), DMA((mp - 1,)), DMA((mp,))])
+    for w, (count, many, _) in pieces.items():
+        for i in range(width // count):
+            add(f"g{w}{i}", gather_sems())
+        for i in range(many):
+            add(f"s{w}{i}s", [DMA((3,)), DMA((3,)), DMA((4,)), DMA((4,))])
+    add("vec", [DMA((7,)), DMA((8,)), DMA((mp,)), DMA((mp + 1,))])
     add("sum", [DMA((3,)), DMA((3,)), DMA((mp - 1,)), DMA((mp,))])
     names = names + list(outs) + list(scratch)
     return pl.pallas_call(
@@ -1165,20 +1236,20 @@
             gain_attn, shift_attn, gain_ffn, shift_ffn, seq_lengths, rand_blocks,
         )
     d = lax.axis_index("dp")
-    pa = jnp.concatenate([w_query, w_key, w_value, w_out.T], 1)
-    lens = jnp.stack([seq_lengths // 32, seq_lengths % 32], 1).reshape(-1).astype(BF16)
-    vec = jnp.stack([gain_attn, shift_attn, gain_ffn, shift_ffn, jnp.pad(lens, (0, rows - 4))])
+    pa = jnp.stack([w.reshape(rows, per, -1) for w in (w_query, w_key, w_value, w_out.T)], 2).reshape(rows, 4 * cols)
+    lens = jnp.stack([seq_lengths // 32, seq_lengths % 32], 1).reshape(1, -1).astype(BF16)
+    vec = jnp.stack([gain_attn, shift_attn, gain_ffn, shift_ffn])
     vec = lax.dynamic_update_slice(jnp.zeros((16, 4 * cols), BF16), vec, (0, d * rows))
     pick = jnp.swapaxes(rand_blocks, 1, 2).reshape(per * picks, nblocks).astype(BF16)
-    pick = jnp.pad(pick, ((0, 16 - per * picks), (0, 128 - nblocks)))
+    pick = jnp.pad(pick, ((0, 15 - per * picks), (0, 128 - nblocks)))
+    pick = jnp.concatenate([pick, jnp.pad(lens, ((0, 0), (0, 124)))])
     out, gtok, ra, rb, rc, sums = fused_layer(
         mp, tokens, cotangent, pa, w_inner, w_outer.T, vec, pick, cols // per, nblocks, picks
     )
     sums = lax.dynamic_slice_in_dim(sums, d * rows, rows, 1)
-    return (
-        out, gtok, ra[:, :cols], ra[:, cols : 2 * cols], ra[:, 2 * cols : 3 * cols], ra[:, 3 * cols :].T, rb, rc.T,
-        sums[0], sums[1], sums[2], sums[3],
-    )
+    ra = ra.reshape(rows, per, 4, -1)
+    gq, gk, gv, go = (ra[:, :, i].reshape(rows, cols) for i in range(4))
+    return out, gtok, gq, gk, gv, go.T, rb, rc.T, sums[0], sums[1], sums[2], sums[3]
 
 
 def solution(mesh):

time: 223 us -> 201 us (0.901)
  Pallas kernels: 204 us -> 182 us
  local copies, waits for them, and re-layouts: 14.5 us -> 17.5 us
    pallas_call x1, Pallas kernels: 204 us -> 182 us  [fused_layer(): pl.pallas_call(lambda *refs: layer_kernel(mp, head, nblocks, picks, names...]
    unnamed x30 -> x36, local copies, waits for them, and re-layouts: 7.33 us -> 10.2 us
where the time goes in v4:
time: 201 us
  Pallas kernels  182 us (91%)
  local copies, waits for them, and re-layouts  17.5 us (9%)
    pallas_call x1, Pallas kernels, fused_layer(): pl.pallas_call(lambda *refs: layer_kernel(mp, head, nblocks, picks, names...  182 us
    unnamed x36, local copies, waits for them, and re-layouts  10.2 us

profile of v4, /device:TPU:0, one launch (start us, length us, event | category | flops | bytes accessed | tf_op | source)
XLA Modules:
  0.0 200.6 jit_solution(1645195721125055987)
XLA Ops:
  0.7 0.9 copy.34
  1.7 0.7 copy-done.6
  2.5 0.7 copy-done.4
  3.3 0.8 copy.37.refs_2_
  4.1 0.6 copy-done.8
  4.8 0.6 broadcast_in_dim.3
  5.4 2.6 %dynamic_update_slice.3.refs_5_ = bf16[16,768]{1,0:T(8,128)(2,1)} dynamic-update-slice(bf16[16,768]{1,0:T(8,128)(2,1)} %broadcast_in_dim.3, bf16[4,96]{1,0:T(4,128)(2,1)S(1)} %pad_maximum_fusion.1, s32[]{:T(128)} %constant.32.clone.1, s32[]{:T(128)S(6)} %select_n.16) | dynamic-update-slice | bytes 1540 | tf_op jit(solution)/shard_map/dynamic_update_slice | solution.py:1242
  8.2 0.5 copy-done.7
  8.7 0.6 fusion.2.refs_6_
  9.3 181.7 %layer.1 = (bf16[2,256,768]{2,1,0:T(8,128)(2,1)}, bf16[2,256,768]{2,1,0:T(8,128)(2,1)}, f32[96,768]{1,0:T(8,128)}, f32[96,768]{1,0:T(8,128)}, f32[96,768]{1,0:T(8,128)}, /*index=5*/f32[8,768]{1,0:T(8,128)}) custom-call(bf16[2,256,768]{2,1,0:T(8,128)(2,1)} %refs_0_.1, bf16[2,256,768]{2,1,0:T(8,128)(2,1)} %refs_1_.1, bf16[96,768]{1,0:T(8,128)(2,1)} %copy.37.refs_2_, ...), custom_call_target="tpu_custom_call" | custom-call | tf_op jit(solution)/shard_map/layer/pallas_call | solution.py:950
  191.0 1.1 copy.38
  192.1 0.7 fusion.5
  192.8 0.7 copy.39
  193.5 0.7 copy.40
  194.2 0.7 copy.41
  195.0 0.8 constant_dynamic-slice_fusion
  195.7 0.5 slice_bitcast_fusion
  196.3 0.9 copy.47
  197.2 0.5 copy-done
  197.7 0.9 copy.48
  198.6 0.2 copy-done.3
  198.8 0.7 copy.49
  199.5 0.4 copy-done.2
  199.9 0.7 copy.50
  (30 shorter events, 0.6 us)
Async XLA Ops:
  0.6 0.9 copy-start.5
  1.6 0.8 copy-start.6
  2.4 0.8 copy-start.4
  3.3 0.8 copy-start.11
  4.1 0.7 copy-start.8
  4.1 0.7 copy-start.9
  4.1 0.7 copy-start.10
  5.4 2.6 %copy-start.12 = (s32[2]{0:T(128)S(1)}, s32[2]{0:T(128)}, u32[]{:S(2)}) copy-start(s32[2]{0:T(128)} %param.26) | copy-start | bytes 28
  8.0 0.7 copy-start.7
  192.1 4.2 %copy-start.1 = (bf16[2,256,768]{2,1,0:T(8,128)(2,1)S(1)}, bf16[2,256,768]{2,1,0:T(8,128)(2,1)}, u32[]{:S(2)}) copy-start(bf16[2,256,768]{2,1,0:T(8,128)(2,1)} %get-tuple-element.58) | copy-start | bytes 2359300
  196.3 1.4 copy-start
  197.7 1.1 copy-start.3
  198.8 1.1 copy-start.2

commit v5 on v4

--- a/solution.py
+++ b/solution.py
@@ -369,8 +369,8 @@
 
 
 class Sums:
-    def __init__(self, p, out, bufs, sems, mp):
-        self.p, self.out, self.mp = p, out, mp
+    def __init__(self, p, bufs, sems, mp):
+        self.p, self.mp = p, mp
         self.mine, self.came, self.parts = bufs
         self.s, self.r, self.zs, self.zr = sems
 
@@ -407,11 +407,11 @@
         total = self.parts[0]
         for z in range(1, self.mp):
             total = total + self.parts[z]
-        self.out[...] = total
         for i in range(3):
             self.hop(i).wait_send()
         for k in range(1, self.mp):
             self.column(k).wait_send()
+        return total
 
 
 class Swap:
@@ -469,7 +469,8 @@
     cols = group // 3
     per = cols // head
     heads = 2 * per
-    n = r["pa"].shape[0]
+    n, narrow = r["wq"].shape
+    pa, pick, vec = r["pa"], r["pick"], r["vec"]
     scale = 1.0 / math.sqrt(head)
     mine = pl.multiple_of(p.c * half, half)
     theirs = pl.multiple_of(half - p.c * half, half)
@@ -487,9 +488,9 @@
     )
     gathers = ga_parts + [b0, b1, c0, c1]
     plane = [lax.rem(p.d + k, 8) for k in range(1, 8)]
-    vec, pick, gvec, gpick = r["vec"], r["pick"], r["gvec"], r["gpick"]
+    gvec, gpick = r["gvec"], r["gpick"]
     vs, vr, us, ur = sems("vec")
-    sums = Sums(p, r["sums"], sems("sumbuf"), sems("sum"), mp)
+    sums = Sums(p, sems("sumbuf"), sems("sum"), mp)
     home = Homewards(p, r["outb"], r["hout"], sems("home"))
     home_g = Homewards(p, r["gtokb"], r["hgtok"], sems("homeg"))
     pair_attn = Swap(p, r["send"], r["recv"], sems("sw0"), count=rc)
@@ -506,6 +507,29 @@
     ua = [unit(f"a{i}", ga, (i % 2,), (i // 2) * each, each, i % 2) for i in range(heads)]
     ub, uc = ([unit(f"{w}{i}", r["d" + w], (0, 1), i * hw, hw, i) for i in range(2)] for w in "bc")
 
+    for h in range(per):
+        for i, w in enumerate(("wq", "wk", "wv")):
+            pa[:, h * each + i * head : h * each + (i + 1) * head] = r[w][:, h * head : (h + 1) * head]
+    flip = r["flip"]
+    flip[:, :n] = r["wo_in"][...]
+    turned = flip[...].T
+    for h in range(per):
+        pa[:, h * each + 3 * head : (h + 1) * each] = turned[:n, h * head : (h + 1) * head]
+    sub16 = lax.broadcasted_iota(jnp.int32, (16, 128), 0)
+    lane16 = lax.broadcasted_iota(jnp.int32, (16, 128), 1)
+    table = jnp.zeros((16, 128), F32)
+    for h in range(per):
+        for j in range(picks):
+            for b in range(nblocks):
+                here = (sub16 == h * picks + j) & (lane16 == b)
+                table = jnp.where(here, r["rand"][h, j, b].astype(F32), table)
+    for i in range(2):
+        count = r["lens"][i]
+        high = lax.div(count, 32)
+        table = jnp.where((sub16 == 15) & (lane16 == 2 * i), high.astype(F32), table)
+        table = jnp.where((sub16 == 15) & (lane16 == 2 * i + 1), (count - 32 * high).astype(F32), table)
+    pick[...] = table.astype(BF16)
+
     greet(column_peers(p, mp) + [(d, p.m) for d in plane])
     pcopies = [remote(pick, gpick.at[p.m], us.at[k - 1], ur.at[p.m], (p.d, lax.rem(p.m + k, mp))) for k in range(1, mp)]
     pcopies.append(remote(pick, gpick.at[mp], us.at[mp - 1], ur.at[mp], (p.sib, p.m)))
@@ -514,12 +538,22 @@
         copy.start()
     for g in ga_parts:
         g.z_send()
-    b0.z_send()
-    pl.when(jnp.logical_not(p.inner))(tokens.send)
+
+    @pl.when(jnp.logical_not(p.inner))
+    def _():
+        b0.z_send()
+        tokens.send()
+
+    wide = lax.broadcasted_iota(jnp.int32, (128, width), 1) - p.d * n
+    deep = lax.broadcasted_iota(jnp.int32, (128, width), 0)
+    spots = jnp.where((wide == deep) & (deep < n), 1.0, 0.0).astype(BF16)
+    vec[...] = dots(r["gains"][...], spots, 1, 0).astype(BF16)
     vcopies = [remote(vec, gvec.at[p.d], vs.at[k], vr.at[p.d], (d, p.m)) for k, d in enumerate(plane)]
     vcopies.append(pltpu.make_async_copy(vec, gvec.at[p.d], vr.at[p.d]))
     for g in ga_parts:
         g.z_mid()
+    pl.when(p.inner)(b0.z_send)
+    ga_parts[0].forward()
     b0.z_mid()
     pl.when(p.inner)(tokens.send)
     for copy in vcopies:
@@ -554,11 +588,13 @@
     ka[head + nblocks :, :] = jnp.where((low == 0) & beyond, 1.0, 0.0).astype(BF16)
     qa[head + nblocks :, :] = jnp.where(low == 0, NEG, 0.0).astype(BF16)
 
-    for g in ga_parts:
+    for g in ga_parts[1:]:
         g.forward()
     tokens.forward(mp)
     b1.z_send()
     c0.z_send()
+    c1.z_send()
+    b0.forward()
     tokens.land(mp)
 
     def project(h):
@@ -609,19 +645,22 @@
             ctx[own_rows, span] = (mixed / total).astype(BF16)
             r["lse"][i, :, span] = peak + jnp.log(total)
 
-        @pl.when(i == 0)
+        late = jnp.where(p.outer, 1, 0)
+
+        @pl.when(i == 0 + late)
         def _():
             b1.z_mid()
-            c1.z_send()
-            b0.forward()
+
+        @pl.when(i == 2 + late)
+        def _():
+            c0.z_mid()
 
         @pl.when(i == 3)
         def _():
-            c0.z_mid()
-
-        @pl.when(i == 5)
-        def _():
             b1.forward()
+
+        @pl.when(i == 4 + late)
+        def _():
             c1.z_mid()
             cots.send()
 
@@ -805,27 +844,34 @@
         qkv[v, :] = gv.astype(BF16)
 
         grad_a(i)
-        for k in range(heads):
+        for k in range(1, heads):
 
             @pl.when(i == k)
             def _():
                 if k == 1:
                     for u in uc:
                         u.third()
-                if k == 3:
+                if k == 2:
                     for u in ub:
                         u.second()
+                    start_all(ua[:2])
+                if k == 3:
                     for u in uc:
                         u.line()
-                start_all([ua[k]])
                 if k == 4:
-                    ua[0].second()
-                    ua[1].second()
+                    for u in ub:
+                        u.third()
+                    for u in ua[:2]:
+                        u.second()
                 if k == 5:
                     for u in ub:
-                        u.third()
-                if k in (2, 4):
-                    sums.step(k // 2 - 1)
+                        u.line()
+                    for u in ua[2:4]:
+                        u.second()
+                if k % 2 == 1:
+                    sums.step(k // 2)
+                if k >= 2:
+                    start_all([ua[k]])
 
         return 0
 
@@ -843,8 +889,6 @@
     for i in range(2):
         r["send1"][i * rc : (i + 1) * rc, :] = tok_part(pl.ds(pl.multiple_of(theirs + i * rc, rc), rc)).astype(BF16)
         pair_gt.send(i)
-    for u in ua[2:4]:
-        u.second()
     for i in range(2):
         rows = pl.ds(pl.multiple_of(mine + i * rc, rc), rc)
         here = slice(i * rc, (i + 1) * rc)
@@ -852,13 +896,10 @@
         pair_gt.recv(i)
         r["gtokb"][here, :] = (r["res"][here, :] + part + r["recv1"][here, :].astype(F32)).astype(BF16)
         home_g.send(i)
-    for u in ub:
-        u.line()
     for u in ua[:2]:
         u.third()
     for u in ua[4:]:
         u.second()
-    sums.step(2)
     for u in ua[2:4]:
         u.third()
     for u in ua[:2]:
@@ -867,22 +908,13 @@
         u.third()
     for u in ua[2:]:
         u.line()
-    sums.finish()
-
-    def settle(made, land, out):
-        for u in made:
-            if len(u.halves) == 2:
-                u.owned()
-            else:
-                pl.when(p.a == u.halves[0])(u.owned)
-        total = land[0].astype(F32)
-        for z in range(1, 3):
-            total = total + land[z].astype(F32)
-        out[...] = total
-
-    settle(uc, r["lc"], r["rc"])
-    settle(ub, r["lb"], r["rb"])
-    settle(ua, r["la"], r["ra"])
+    summed = sums.finish()
+    r["sums"][...] = pltpu.roll(summed, width - p.d * n, 1)[:, :128]
+
+    for u in uc + ub:
+        u.owned()
+    for u in ua:
+        pl.when(p.a == u.halves[0])(u.owned)
     home.finish()
     home_g.finish()
     tokens.finish(mp)
@@ -894,22 +926,22 @@
         copy.wait_send()
 
 
-def fused_layer(mp, tok, cot, pa, pb, pc, vec, pick, head, nblocks, picks):
-    n, width = pa.shape
-    quarter = tok.shape[1]
+def fused_layer(mp, tok, cot, wq, wk, wv, wo, w_inner, w_outer, gains, lens, rand):
+    n, narrow = wq.shape
+    quarter, width = tok.shape[1:]
+    per, picks, nblocks = rand.shape
+    head = narrow // per
     seq = quarter * mp
     half = seq // 2
-    per = width // 4 // head
     group = 3 * per * head
     shape = jax.ShapeDtypeStruct
-    names = ["tok", "cot", "pa", "pb", "pc", "vec", "pick"]
+    SMEM = pl.BlockSpec(memory_space=pltpu.SMEM)
+    names = ["tok", "cot", "wq", "wk", "wv", "wo_in", "pb", "pc", "gains", "lens", "rand"]
     outs = {
         "hout": (shape((2, quarter, width), BF16), ANY),
         "hgtok": (shape((2, quarter, width), BF16), ANY),
-        "ra": (shape((n, width), F32), VMEM),
-        "rb": (shape((n, width), F32), VMEM),
-        "rc": (shape((n, width), F32), VMEM),
-        "sums": (shape((8, width), F32), VMEM),
+        **{k: (shape((3, n, width), BF16), ANY) for k in ("la", "lb", "lc")},
+        "sums": (shape((8, 128), F32), VMEM),
     }
     weight = ((2, 8 * n, width), BF16)
     rows_b, half_b, half_f = ((seq, width), BF16), ((half, width), BF16), ((half, width), F32)
@@ -919,10 +951,11 @@
         "wo": ((2 * per * head, width), BF16), "lse": ((2 * per, 1, seq), F32), "n1": half_f, "inv1": ((half, 128), F32), "res": half_f,
         "hb": rows_b, "act": ((seq, 2 * width), BF16), "slope": ((seq, 2 * width), BF16), "gf": rows_b, "gat": rows_b,
         "send": half_b, "recv": half_b, "send1": half_b, "recv1": half_b, "outb": half_b, "gtokb": half_b, "ct": half_b,
-        "gvec": ((8,) + vec.shape, BF16), "gpick": ((mp + 1,) + pick.shape, BF16), "norms": (vec.shape, F32),
+        "gvec": ((8, 16, width), BF16), "gpick": ((mp + 1, 16, 128), BF16), "norms": ((16, width), F32),
+        "pa": ((n, width), BF16), "pick": ((16, 128), BF16), "vec": ((16, width), BF16),
+        "flip": ((narrow, 128), BF16),
         "bias": ((2 * per, nblocks, seq), BF16), "qa": ((head + nblocks + 16, seq), BF16), "ka": ((head + nblocks + 16, seq), BF16),
         "small": ((8, width), F32), "turn": ((4 * head, width), BF16),
-        "la": ((3, n, width), BF16), "lb": ((3, n, width), BF16), "lc": ((3, n, width), BF16),
         "sumbuf.0": ((3, 8, width), F32), "sumbuf.1": ((3, 8, width), F32), "sumbuf.2": ((mp, 8, width), F32),
     }
     pieces = {"a": (4 * head, 2 * per, 1), "b": (width // 2, 2, 2), "c": (width // 2, 2, 2)}
@@ -951,11 +984,11 @@
         lambda *refs: layer_kernel(mp, head, nblocks, picks, names, *refs),
         name="layer",
         out_shape=[o[0] for o in outs.values()],
-        in_specs=[ANY] * 5 + [VMEM] * 2,
+        in_specs=[ANY] * 2 + [VMEM] * 4 + [ANY] * 2 + [VMEM] + [SMEM] * 2,
         out_specs=[o[1] for o in outs.values()],
         scratch_shapes=list(scratch.values()),
         compiler_params=pltpu.CompilerParams(collective_id=0, has_side_effects=True, vmem_limit_bytes=64 << 20),
-    )(tok, cot, pa, pb, pc, vec, pick)
+    )(tok, cot, wq, wk, wv, wo, w_inner, w_outer, gains, lens, rand)
 
 
 def attend_kernel(q_ref, k_ref, v_ref, bias_ref, hot_ref, ctx_ref, lse_ref, qa, ka):
@@ -1067,6 +1100,46 @@
     )(qkv, qkv, qkv, bias, hot, lse, grad)
 
 
+def settle_kernel(head, out, gtok, la, lb, lc, out_to, gtok_to, gq, gk, gv, go, gb, gc, turn, sem):
+    copies = [pltpu.make_async_copy(out, out_to, sem.at[0]), pltpu.make_async_copy(gtok, gtok_to, sem.at[1])]
+    for copy in copies:
+        copy.start()
+
+    def total(land):
+        return land[0].astype(F32) + land[1].astype(F32) + land[2].astype(F32)
+
+    gb[...] = total(lb)
+    gc[...] = total(lc)
+    n = gb.shape[0]
+    summed = total(la)
+    turn[:n, :] = summed
+    turned = turn[...].T
+    for h in range(gq.shape[1] // head):
+        each = 4 * head
+        span = slice(h * head, (h + 1) * head)
+        for i, to in enumerate((gq, gk, gv)):
+            first = h * each + i * head
+            to[:, span] = summed[:, first : first + head]
+        go[span, :] = turned[h * each + 3 * head : (h + 1) * each, :n]
+    for copy in copies:
+        copy.wait()
+
+
+def settle(head, narrow, out, gtok, la, lb, lc):
+    _, n, width = la.shape
+    shape = jax.ShapeDtypeStruct
+    small, wide = shape((n, narrow), F32), shape((n, width), F32)
+    return pl.pallas_call(
+        lambda *refs: settle_kernel(head, *refs),
+        name="settle",
+        out_shape=[shape(out.shape, BF16)] * 2 + [small] * 3 + [shape((narrow, n), F32), wide, wide],
+        in_specs=[ANY] * 2 + [VMEM] * 3,
+        out_specs=[VMEM] * 8,
+        scratch_shapes=[pltpu.VMEM((128, width), F32), DMA((2,))],
+        compiler_params=pltpu.CompilerParams(vmem_limit_bytes=64 << 20),
+    )(out, gtok, la, lb, lc)
+
+
 def fetch_plain(dp, mp, tok, cot, pa, pb, pc, vec):
     d, m = lax.axis_index("dp"), lax.axis_index("mp")
     core = d % 2
@@ -1235,21 +1308,13 @@
             dp, mp, tokens, cotangent, w_query, w_key, w_value, w_out, w_inner, w_outer,
             gain_attn, shift_attn, gain_ffn, shift_ffn, seq_lengths, rand_blocks,
         )
-    d = lax.axis_index("dp")
-    pa = jnp.stack([w.reshape(rows, per, -1) for w in (w_query, w_key, w_value, w_out.T)], 2).reshape(rows, 4 * cols)
-    lens = jnp.stack([seq_lengths // 32, seq_lengths % 32], 1).reshape(1, -1).astype(BF16)
-    vec = jnp.stack([gain_attn, shift_attn, gain_ffn, shift_ffn])
-    vec = lax.dynamic_update_slice(jnp.zeros((16, 4 * cols), BF16), vec, (0, d * rows))
-    pick = jnp.swapaxes(rand_blocks, 1, 2).reshape(per * picks, nblocks).astype(BF16)
-    pick = jnp.pad(pick, ((0, 15 - per * picks), (0, 128 - nblocks)))
-    pick = jnp.concatenate([pick, jnp.pad(lens, ((0, 0), (0, 124)))])
-    out, gtok, ra, rb, rc, sums = fused_layer(
-        mp, tokens, cotangent, pa, w_inner, w_outer.T, vec, pick, cols // per, nblocks, picks
+    gains = jnp.pad(jnp.stack([gain_attn, shift_attn, gain_ffn, shift_ffn]), ((0, 12), (0, 128 - rows)))
+    picked = jnp.swapaxes(rand_blocks, 1, 2)
+    *landed, sums = fused_layer(
+        mp, tokens, cotangent, w_query, w_key, w_value, w_out, w_inner, w_outer.T, gains, seq_lengths, picked
     )
-    sums = lax.dynamic_slice_in_dim(sums, d * rows, rows, 1)
-    ra = ra.reshape(rows, per, 4, -1)
-    gq, gk, gv, go = (ra[:, :, i].reshape(rows, cols) for i in range(4))
-    return out, gtok, gq, gk, gv, go.T, rb, rc.T, sums[0], sums[1], sums[2], sums[3]
+    *grads, grad_outer = settle(cols // per, cols, *landed)
+    return *grads, grad_outer.T, *(sums[i, :rows] for i in range(4))
 
 
 def solution(mesh):

time: 201 us -> 187 us (0.930)
  local copies, waits for them, and re-layouts: 17.5 us -> 1.87 us
    unnamed x36 -> x10, local copies, waits for them, and re-layouts: 10.2 us -> 1.35 us
    pallas_call x0 -> x1, Pallas kernels: none -> 4.13 us  [settle(): pl.pallas_call(lambda *refs: settle_kernel(head, *refs), name='settle', o...]
    dynamic_update_slice x1 -> x0, local copies, waits for them, and re-layouts: 2.56 us -> none  [layer(): lax.dynamic_update_slice(jnp.zeros((16, 4 * cols), BF16), vec, (0, d * ro...]
    pallas_call x1, Pallas kernels: 182 us -> 179 us  [fused_layer(): pl.pallas_call(lambda *refs: layer_kernel(mp, head, nblocks, picks, names...]
where the time goes in v5:
time: 187 us
  Pallas kernels  183 us (98%)
  local copies, waits for them, and re-layouts  1.87 us (1%)
    pallas_call x1, Pallas kernels, fused_layer(): pl.pallas_call(lambda *refs: layer_kernel(mp, head, nblocks, picks, names...  179 us
    pallas_call x1, Pallas kernels, settle(): pl.pallas_call(lambda *refs: settle_kernel(head, *refs), name='settle', o...  4.13 us

profile of v5, /device:TPU:0, one launch (start us, length us, event | category | flops | bytes accessed | tf_op | source)
XLA Modules:
  0.0 186.6 jit_solution(14074197493247780958)
XLA Ops:
  0.6 0.0 copy-start.4
  0.7 0.0 copy-start.1
  0.7 0.0 copy-start.2
  0.7 0.0 copy-start.3
  0.7 0.6 copy-done.4
  1.3 0.0 copy-done.1
  1.3 0.0 copy-done.2
  1.3 0.0 copy-done.3
  1.3 0.6 fusion.8.refs_8_
  2.0 179.3 %layer.1 = (bf16[2,256,768]{2,1,0:T(8,128)(2,1)}, bf16[2,256,768]{2,1,0:T(8,128)(2,1)}, bf16[3,96,768]{2,1,0:T(8,128)(2,1)}, bf16[3,96,768]{2,1,0:T(8,128)(2,1)}...) custom-call(bf16[2,256,768]{2,1,0:T(8,128)(2,1)} %refs_0_.1, bf16[2,256,768]{2,1,0:T(8,128)(2,1)} %refs_1_.1, ...), custom_call_target="tpu_custom_call" | custom-call | tf_op jit(solution)/shard_map/layer/pallas_call | solution.py:983
  181.3 4.1 %settle.1 = (bf16[2,256,768]{2,1,0:T(8,128)(2,1)}, bf16[2,256,768]{2,1,0:T(8,128)(2,1)}, f32[96,192]{1,0:T(8,128)}, f32[96,192]{1,0:T(8,128)}, f32[96,192]{1,0:T...) custom-call(bf16[2,256,768]{2,1,0:T(8,128)(2,1)} %get-tuple-element.26.refs_0_, ...), custom_call_target="tpu_custom_call" | custom-call | tf_op jit(solution)/shard_map/settle/pallas_call | solution.py:1132
  185.4 0.0 copy-start
  185.4 0.7 copy-done
  186.1 0.5 slice_bitcast_fusion
Async XLA Ops:
  0.6 0.7 copy-start.4
  0.7 0.7 copy-start.1
  0.7 0.7 copy-start.2
  0.7 0.7 copy-start.3
  185.4 0.7 copy-start

commit v6 on v5

--- a/solution.py
+++ b/solution.py
@@ -1100,18 +1100,26 @@
     )(qkv, qkv, qkv, bias, hot, lse, grad)
 
 
-def settle_kernel(head, out, gtok, la, lb, lc, out_to, gtok_to, gq, gk, gv, go, gb, gc, turn, sem):
-    copies = [pltpu.make_async_copy(out, out_to, sem.at[0]), pltpu.make_async_copy(gtok, gtok_to, sem.at[1])]
+def settle_kernel(
+    head, out, gtok, la, lb, lc, sums, out_to, gtok_to, gq, gk, gv, go, gb, gc, s0, s1, s2, s3, va, vb, vc, turn, sem
+):
+    pairs = ((lc, vc), (lb, vb), (la, va), (out, out_to), (gtok, gtok_to))
+    copies = [pltpu.make_async_copy(src, dst, sem.at[i]) for i, (src, dst) in enumerate(pairs)]
     for copy in copies:
         copy.start()
 
     def total(land):
         return land[0].astype(F32) + land[1].astype(F32) + land[2].astype(F32)
 
-    gb[...] = total(lb)
-    gc[...] = total(lc)
     n = gb.shape[0]
-    summed = total(la)
+    for i, to in enumerate((s0, s1, s2, s3)):
+        to[...] = sums[i, :n]
+    copies[0].wait()
+    gc[...] = total(vc)
+    copies[1].wait()
+    gb[...] = total(vb)
+    copies[2].wait()
+    summed = total(va)
     turn[:n, :] = summed
     turned = turn[...].T
     for h in range(gq.shape[1] // head):
@@ -1121,23 +1129,24 @@
             first = h * each + i * head
             to[:, span] = summed[:, first : first + head]
         go[span, :] = turned[h * each + 3 * head : (h + 1) * each, :n]
-    for copy in copies:
+    for copy in copies[3:]:
         copy.wait()
 
 
-def settle(head, narrow, out, gtok, la, lb, lc):
+def settle(head, narrow, out, gtok, la, lb, lc, sums):
     _, n, width = la.shape
     shape = jax.ShapeDtypeStruct
     small, wide = shape((n, narrow), F32), shape((n, width), F32)
+    land = pltpu.VMEM(la.shape, BF16)
     return pl.pallas_call(
         lambda *refs: settle_kernel(head, *refs),
         name="settle",
-        out_shape=[shape(out.shape, BF16)] * 2 + [small] * 3 + [shape((narrow, n), F32), wide, wide],
-        in_specs=[ANY] * 2 + [VMEM] * 3,
-        out_specs=[VMEM] * 8,
-        scratch_shapes=[pltpu.VMEM((128, width), F32), DMA((2,))],
+        out_shape=[shape(out.shape, BF16)] * 2 + [small] * 3 + [shape((narrow, n), F32), wide, wide] + [shape((n,), F32)] * 4,
+        in_specs=[ANY] * 5 + [VMEM],
+        out_specs=[VMEM] * 12,
+        scratch_shapes=[land, land, land, pltpu.VMEM((128, width), F32), DMA((5,))],
         compiler_params=pltpu.CompilerParams(vmem_limit_bytes=64 << 20),
-    )(out, gtok, la, lb, lc)
+    )(out, gtok, la, lb, lc, sums)
 
 
 def fetch_plain(dp, mp, tok, cot, pa, pb, pc, vec):
@@ -1310,11 +1319,11 @@
         )
     gains = jnp.pad(jnp.stack([gain_attn, shift_attn, gain_ffn, shift_ffn]), ((0, 12), (0, 128 - rows)))
     picked = jnp.swapaxes(rand_blocks, 1, 2)
-    *landed, sums = fused_layer(
+    landed = fused_layer(
         mp, tokens, cotangent, w_query, w_key, w_value, w_out, w_inner, w_outer.T, gains, seq_lengths, picked
     )
-    *grads, grad_outer = settle(cols // per, cols, *landed)
-    return *grads, grad_outer.T, *(sums[i, :rows] for i in range(4))
+    done = settle(cols // per, cols, *landed)
+    return *done[:7], done[7].T, *done[8:]
 
 
 def solution(mesh):

time: 187 us -> 186 us (level)
  no operation moved by 1% of the time
where the time goes in v6:
time: 186 us; the launch traced here: 185 us
  Pallas kernels  183 us (98%)
    pallas_call x1, Pallas kernels, fused_layer(): pl.pallas_call(lambda *refs: layer_kernel(mp, head, nblocks, picks, names...  179 us
    pallas_call x1, Pallas kernels, settle(): pl.pallas_call(lambda *refs: settle_kernel(head, *refs), name='settle', o...  3.96 us

profile of v6, /device:TPU:0, one launch (start us, length us, event | category | flops | bytes accessed | tf_op | source)
XLA Modules:
  0.0 185.4 jit_solution(9908806837077800994)
XLA Ops:
  0.6 0.0 copy-start.3
  0.7 0.0 copy-start
  0.7 0.0 copy-start.1
  0.7 0.0 copy-start.2
  0.7 0.6 copy-done.3
  1.3 0.0 copy-done
  1.3 0.0 copy-done.1
  1.3 0.0 copy-done.2
  1.3 0.6 fusion.8.refs_8_
  2.0 179.3 %layer.1 = (bf16[2,256,768]{2,1,0:T(8,128)(2,1)}, bf16[2,256,768]{2,1,0:T(8,128)(2,1)}, bf16[3,96,768]{2,1,0:T(8,128)(2,1)}, bf16[3,96,768]{2,1,0:T(8,128)(2,1)}...) custom-call(bf16[2,256,768]{2,1,0:T(8,128)(2,1)} %refs_0_.1, bf16[2,256,768]{2,1,0:T(8,128)(2,1)} %refs_1_.1, ...), custom_call_target="tpu_custom_call" | custom-call | tf_op jit(solution)/shard_map/layer/pallas_call | solution.py:983
  181.3 4.0 %settle.1 = (bf16[2,256,768]{2,1,0:T(8,128)(2,1)}, bf16[2,256,768]{2,1,0:T(8,128)(2,1)}, f32[96,192]{1,0:T(8,128)}, f32[96,192]{1,0:T(8,128)}, f32[96,192]{1,0:T...) custom-call(bf16[2,256,768]{2,1,0:T(8,128)(2,1)} %get-tuple-element., ...), custom_call_target="tpu_custom_call" | custom-call | tf_op jit(solution)/shard_map/settle/pallas_call | solution.py:1141
Async XLA Ops:
  0.6 0.7 copy-start.3
  0.7 0.7 copy-start
  0.7 0.7 copy-start.1
  0.7 0.7 copy-start.2

commit v7 on v6

--- a/solution.py
+++ b/solution.py
@@ -635,8 +635,7 @@
 
         q, k, v = set_head(i)
         own_rows = pl.ds(pl.multiple_of(i * head, head), head)
-        for j in range(2):
-            span = slice(j * half, (j + 1) * half)
+        for span in (slice(0, seq),):
             scores = dots(ka[...], qa[:, span], 0, 0)
             peak = jnp.max(scores, 0, keepdims=True)
             weights = jnp.exp(scores - peak)

time: 186 us -> 185 us (level)
  no operation moved by 1% of the time
where the time goes in v7:
time: 185 us
  Pallas kernels  183 us (99%)
    pallas_call x1, Pallas kernels, fused_layer(): pl.pallas_call(lambda *refs: layer_kernel(mp, head, nblocks, picks, names...  179 us
    pallas_call x1, Pallas kernels, settle(): pl.pallas_call(lambda *refs: settle_kernel(head, *refs), name='settle', o...  3.96 us

profile of v7, /device:TPU:0, one launch (start us, length us, event | category | flops | bytes accessed | tf_op | source)
XLA Modules:
  0.0 185.1 jit_solution(4307582411633670627)
XLA Ops:
  0.6 0.0 copy-start.3
  0.7 0.0 copy-start
  0.7 0.0 copy-start.1
  0.7 0.0 copy-start.2
  0.7 0.6 copy-done.3
  1.3 0.0 copy-done
  1.3 0.0 copy-done.1
  1.3 0.0 copy-done.2
  1.3 0.6 fusion.8.refs_8_
  2.0 179.0 %layer.1 = (bf16[2,256,768]{2,1,0:T(8,128)(2,1)}, bf16[2,256,768]{2,1,0:T(8,128)(2,1)}, bf16[3,96,768]{2,1,0:T(8,128)(2,1)}, bf16[3,96,768]{2,1,0:T(8,128)(2,1)}...) custom-call(bf16[2,256,768]{2,1,0:T(8,128)(2,1)} %refs_0_.1, bf16[2,256,768]{2,1,0:T(8,128)(2,1)} %refs_1_.1, ...), custom_call_target="tpu_custom_call" | custom-call | tf_op jit(solution)/shard_map/layer/pallas_call | solution.py:982
  180.9 4.0 %settle.1 = (bf16[2,256,768]{2,1,0:T(8,128)(2,1)}, bf16[2,256,768]{2,1,0:T(8,128)(2,1)}, f32[96,192]{1,0:T(8,128)}, f32[96,192]{1,0:T(8,128)}, f32[96,192]{1,0:T...) custom-call(bf16[2,256,768]{2,1,0:T(8,128)(2,1)} %get-tuple-element., ...), custom_call_target="tpu_custom_call" | custom-call | tf_op jit(solution)/shard_map/settle/pallas_call | solution.py:1140
Async XLA Ops:
  0.6 0.7 copy-start.3
  0.7 0.7 copy-start
  0.7 0.7 copy-start.1
  0.7 0.7 copy-start.2
